TPU v7x, 512 devices: a whole 4x4x16 slice. The times are simulated.
512 devices in a mesh: ctx: 8 (over y_hi, x), head: 64 (over z, y_lo, core).
Axes of the slice: x: 4, y: 4 (y_hi: 2, y_lo: 2; y = y_hi * 2 + y_lo), z: 16, core: 2. Of those that a mesh axis runs over, the one named last changes fastest.
Arguments:
- queries: bfloat16 [4096, 8192], P('ctx', 'head'), may hold values from -6 to 6
- outputs: bfloat16 [4096, 8192], P('ctx', 'head'), may hold values from -6 to 6
- out_grad: bfloat16 [4096, 8192], P('ctx', 'head'), may hold values from -6 to 6
- keys_values: bfloat16 [2, 4096, 1024], P(None, 'ctx', 'head'), may hold values from -6 to 6
- row_lse: float32 [64, 4096], P('head', 'ctx'), may hold values from 4.5 to 6.5
- collide: int32 [64, 32, 8], P('head', 'ctx'), may hold values from 0 to 31, as said below
Outputs:
- query_grad: bfloat16 [4096, 8192], P('ctx', 'head')
- kv_grad: float32 [2, 4096, 1024], P(None, 'ctx', 'head')
Inputs may be any that keep to these rules, and one draw needn't show every extreme that they name: Each row of collide names 8 different key blocks.
All inputs are finite; a program needn't handle non-finite values.
Results may differ from a plain program's by a relative error of at most 0.0042.
Values may be sent and summed in bfloat16 or wider, within the bound.
No kernel may reach another device: no remote copies, remote signals or barrier semaphores. Data moves between devices by JAX's collectives and lax.ppermute only.
A program may use at most 64 MiB of HBM per device.

v0:
```python
import jax
import jax.numpy as jnp
from jax import lax
from jax.sharding import PartitionSpec as P

KVH = 8
DH = 128
BLOCK = 128


def from_partner(value, axis, stride):
    return lax.ppermute(value, axis, [(i, i ^ 1 << stride) for i in range(lax.axis_size(axis))])


def tile_terms(query_blk, grad_blk, lse_blk, delta_blk, block_ids, key_blocks, value_blocks):
    score_scale = query_blk.shape[-1] ** (-0.5)
    key_tiles = key_blocks[block_ids]
    value_tiles = value_blocks[block_ids]
    scores = (
        jnp.einsum("gid,grjd->grij", query_blk, key_tiles, preferred_element_type=jnp.float32)
        * score_scale
    )
    weights = jnp.exp(scores - lse_blk[:, None, :, None])
    weights_bf = weights.astype(jnp.bfloat16)
    value_grad = jnp.einsum(
        "grij,gid->grjd", weights_bf, grad_blk, preferred_element_type=jnp.float32
    )
    weight_grad = jnp.einsum(
        "gid,grjd->grij", grad_blk, value_tiles, preferred_element_type=jnp.float32
    )
    score_grad = (weights * (weight_grad - delta_blk[:, None, :, None]) * score_scale).astype(
        jnp.bfloat16
    )
    query_grad = jnp.einsum(
        "grij,grjd->gid", score_grad, key_tiles, preferred_element_type=jnp.float32
    ).astype(jnp.bfloat16)
    key_grad = jnp.einsum(
        "grij,gid->grjd", score_grad, query_blk, preferred_element_type=jnp.float32
    )
    return (query_grad, key_grad, value_grad)


def upper_side(position, which_bit):
    return position // 2**which_bit % 2 == 1


def split_halves(current, position, which_bit):
    half_width = current.shape[2] // 2
    low_half = current[:, :, :half_width]
    high_half = current[:, :, half_width:]
    is_upper = upper_side(position, which_bit)
    outgoing = jnp.where(is_upper, low_half, high_half)
    kept_half = jnp.where(is_upper, high_half, low_half)
    return (kept_half, outgoing)


def shards(queries, outputs, out_grad, keys_values, row_lse, collide):
    local_rows = queries.shape[0]
    heads_here = queries.shape[1] // DH
    local_blocks = local_rows // BLOCK
    group_bits = (lax.axis_size("head") // KVH).bit_length() - 1
    position = lax.axis_index("head")
    current = lax.all_gather(keys_values, "ctx", axis=1, tiled=True)
    for which_bit in range(group_bits):
        received = from_partner(current, "head", which_bit)
        current = jnp.where(
            upper_side(position, which_bit),
            jnp.concatenate((received, current), 2),
            jnp.concatenate((current, received), 2),
        )
    group_kv = current
    all_blocks = group_kv.shape[1] // BLOCK
    key_blocks = group_kv[0].reshape(all_blocks, BLOCK, DH)
    value_blocks = group_kv[1].reshape(all_blocks, BLOCK, DH)

    def to_items(array):
        return (
            array.reshape(local_blocks, BLOCK, heads_here, DH)
            .transpose(2, 0, 1, 3)
            .reshape(-1, 2, BLOCK, DH)
        )

    query_items = to_items(queries)
    grad_items = to_items(out_grad)
    delta_rows = jnp.sum(
        (out_grad.astype(jnp.float32) * outputs.astype(jnp.float32)).reshape(
            local_rows, heads_here, DH
        ),
        axis=2,
    )
    delta_items = delta_rows.T.reshape(-1, 2, BLOCK)
    lse_items = row_lse.reshape(-1, 2, BLOCK)
    id_items = collide.reshape(-1, 2, collide.shape[2])

    def pair_step(carry, items):
        query_blk, grad_blk, lse_blk, delta_blk, block_ids = items
        query_grad, key_grad, value_grad = tile_terms(
            query_blk, grad_blk, lse_blk, delta_blk, block_ids, key_blocks, value_blocks
        )
        flat_ids = block_ids.reshape(-1)
        carry = carry.at[0, flat_ids].add(key_grad.reshape(-1, BLOCK, DH))
        carry = carry.at[1, flat_ids].add(value_grad.reshape(-1, BLOCK, DH))
        return (carry, query_grad)

    start = jnp.zeros((2, all_blocks, BLOCK, DH), jnp.float32)
    totals, grads = lax.scan(
        pair_step, start, (query_items, grad_items, lse_items, delta_items, id_items)
    )
    query_grad = (
        grads.reshape(heads_here, local_blocks, BLOCK, DH)
        .transpose(1, 2, 0, 3)
        .reshape(local_rows, heads_here * DH)
    )
    current = totals.reshape(2, all_blocks * BLOCK, DH)
    bit_order = list(reversed(range(group_bits)))
    for which_bit in bit_order:
        kept_half, outgoing = split_halves(current, position, which_bit)
        current = kept_half + from_partner(outgoing, "head", which_bit)
    kv_grad = lax.psum_scatter(current, "ctx", scatter_dimension=1, tiled=True)
    return (query_grad, kv_grad)


def solution(mesh):
    placed = (
        P("ctx", "head"),
        P("ctx", "head"),
        P("ctx", "head"),
        P(None, "ctx", "head"),
        P("head", "ctx"),
        P("head", "ctx", None),
    )
    return jax.shard_map(
        shards,
        mesh=mesh,
        in_specs=placed,
        out_specs=(P("ctx", "head"), P(None, "ctx", "head")),
        check_vma=False,
    )
```

profile of v0, /device:TPU:1, one launch (start us, length us, event | category | flops | bytes accessed | tf_op | source)
XLA Modules:
  0.0 303.9 jit_solution(12023473060539154175)
XLA Ops:
  7.2 29.9 %all_gather.3 = bf16[2,4096,16]{1,2,0:T(8,128)(2,1)S(1)} all-gather(bf16[2,512,16]{1,2,0:T(8,128)(2,1)} %param.11), channel_id=1, replica_groups=mesh['ctx'=8,'head'=64] {'ctx'}, dimensions={1}, use_global_device_ids=true | all-gather | bytes 294912 | tf_op jit(solution)/shard_map/all_gather | solution.py:63
  37.1 13.6 %collective-permute-start = (bf16[2,4096,16]{1,2,0:T(8,128)(2,1)S(1)}, bf16[2,4096,16]{1,2,0:T(8,128)(2,1)S(1)}, u32[]{:S(2)}, u32[]{:S(2)}) collective-permute-start(bf16[2,4096,16]{1,2,0:T(8,128)(2,1)S(1)} %all_gather.3), channel_id=1, source_target_pairs={{0,1},{1,0},{2,3},{3,2},{4,5},{5,4},{6,7},{7,6},{8,9},{9,8},{10,11... | collective-permute-start | bytes 786440 | tf_op jit(solution)/shard_map/ppermute | solution.py:12
  50.7 1.1 collective-permute-done
  52.0 1.9 collective-permute-start.1
  53.9 13.0 %collective-permute-done.1 = bf16[2,4096,32]{1,2,0:T(8,128)(2,1)S(1)} collective-permute-done((bf16[2,4096,32]{1,2,0:T(8,128)(2,1)S(1)}, bf16[2,4096,32]{1,2,0:T(8,128)(2,1)S(1)}, u32[]{:S(2)}, u32[]{:S(2)}) %collective-permute-start.1) | collective-permute-done | bytes 524320 | tf_op jit(solution)/shard_map/ppermute | solution.py:12
  67.2 1.9 collective-permute-start.2
  69.3 23.2 %collective-permute-done.2 = bf16[2,4096,64]{1,2,0:T(8,128)(2,1)S(1)} collective-permute-done((bf16[2,4096,64]{1,2,0:T(8,128)(2,1)S(1)}, bf16[2,4096,64]{1,2,0:T(8,128)(2,1)S(1)}, u32[]{:S(2)}, u32[]{:S(2)}) %collective-permute-start.2) | collective-permute-done | bytes 1048608 | tf_op jit(solution)/shard_map/ppermute | solution.py:12
  92.6 0.5 maximum_select_fusion
  93.2 0.7 copy.10
  93.9 0.7 copy.9
  94.6 2.5 broadcast_in_dim.7
  97.1 20.8 %while.12 = (s32[]{:T(128)}, f32[2,32,128,128]{3,2,1,0:T(8,128)}, bf16[2,2,128,128]{3,2,1,0:T(8,128)(2,1)}, s32[2,2,8]{2,1,0:T(2,128)S(1)}, bf16[32,128,128]{2,1...) while((s32[]{:T(128)}, f32[2,32,128,128]{3,2,1,0:T(8,128)}, ...), condition=%wide.region_4.5_spmd, body=%wide.region_1.4_spmd.sunk | while | flops 337937600 | bytes 26553664 | solution.py:106
  97.3 0.6 gather_fusion.1
  98.0 0.6 gather_fusion
  99.5 0.4 fusion.65
  100.6 3.5 %scatter_fusion = f32[2,32,128,128]{3,2,1,0:T(8,128)} fusion(f32[2,32,128,128]{3,2,1,0:T(8,128)} %get-tuple-element.172, s32[16]{0:T(128)S(1)} %get-tuple-element.155, f32[16,128,128]{2,1,0:T(8,128)S(1)} %bitcast.108), kind=kCustom, calls=%fused_computation.2.clone.1 | custom fusion | flops 262144 | bytes 3145856 | tf_op jit(solution)/shard_map/while/body/eval_jaxpr/scatter-add | solution.py:101
  104.0 3.5 %scatter_fusion.1 = f32[2,32,128,128]{3,2,1,0:T(8,128)} fusion(f32[2,32,128,128]{3,2,1,0:T(8,128)} %scatter_fusion, s32[16]{0:T(128)S(1)} %get-tuple-element.159, f32[16,128,128]{2,1,0:T(8,128)S(1)} %bitcast.107), kind=kCustom, calls=%fused_computation.3.clone.1 | custom fusion | flops 262144 | bytes 3145856 | tf_op jit(solution)/shard_map/while/body/eval_jaxpr/scatter-add | solution.py:102
  107.7 0.6 gather_fusion.1
  108.4 0.6 gather_fusion
  111.0 3.4 %scatter_fusion = f32[2,32,128,128]{3,2,1,0:T(8,128)} fusion(f32[2,32,128,128]{3,2,1,0:T(8,128)} %get-tuple-element.172, s32[16]{0:T(128)S(1)} %get-tuple-element.155, f32[16,128,128]{2,1,0:T(8,128)S(1)} %bitcast.108), kind=kCustom, calls=%fused_computation.2.clone.1 | custom fusion | flops 262144 | bytes 3145856 | tf_op jit(solution)/shard_map/while/body/eval_jaxpr/scatter-add | solution.py:101
  114.4 3.4 %scatter_fusion.1 = f32[2,32,128,128]{3,2,1,0:T(8,128)} fusion(f32[2,32,128,128]{3,2,1,0:T(8,128)} %scatter_fusion, s32[16]{0:T(128)S(1)} %get-tuple-element.159, f32[16,128,128]{2,1,0:T(8,128)S(1)} %bitcast.107), kind=kCustom, calls=%fused_computation.3.clone.1 | custom fusion | flops 262144 | bytes 3145856 | tf_op jit(solution)/shard_map/while/body/eval_jaxpr/scatter-add | solution.py:102
  117.8 7.8 %fusion.27 = (f32[2,4096,64]{2,1,0:T(8,128)}, f32[2,4096,64]{2,1,0:T(8,128)}) fusion(f32[2,4096,128]{2,1,0:T(8,128)} %bitcast.104), kind=kLoop, calls=%fused_computation.54 | loop fusion | bytes 8388608 | tf_op jit(solution)/shard_map/slice | solution.py:50
  125.7 2.8 copy.17
  128.5 3.8 %copy.18 = f32[2,4096,64]{1,2,0:T(8,128)} copy(f32[2,4096,64]{2,1,0:T(8,128)} %get-tuple-element.84) | data formatting | bytes 4194304
  132.6 4.0 %collective-permute-start.3 = (f32[2,4096,64]{1,2,0:T(8,128)S(1)}, f32[2,4096,64]{1,2,0:T(8,128)S(1)}, u32[]{:S(2)}, u32[]{:S(2)}) collective-permute-start(f32[2,4096,64]{1,2,0:T(8,128)S(1)} %broadcast_select_fusion), channel_id=1, source_target_pairs={{0,4},{1,5},{2,6},{3,7},{4,0},{5,1},{6,2},{7,3},{8,12},{9,13},{10,... | collective-permute-start | bytes 6291464 | tf_op jit(solution)/shard_map/ppermute | solution.py:12
  136.6 44.1 %collective-permute-done.3 = f32[2,4096,64]{1,2,0:T(8,128)S(1)} collective-permute-done((f32[2,4096,64]{1,2,0:T(8,128)S(1)}, f32[2,4096,64]{1,2,0:T(8,128)S(1)}, u32[]{:S(2)}, u32[]{:S(2)}) %collective-permute-start.3) | collective-permute-done | bytes 2097184 | tf_op jit(solution)/shard_map/ppermute | solution.py:12
  181.2 2.8 collective-permute-start.4
  184.0 21.3 %collective-permute-done.4 = f32[2,4096,32]{1,2,0:T(8,128)S(1)} collective-permute-done((f32[2,4096,32]{1,2,0:T(8,128)S(1)}, f32[2,4096,32]{1,2,0:T(8,128)S(1)}, u32[]{:S(2)}, u32[]{:S(2)}) %collective-permute-start.4) | collective-permute-done | bytes 1048608 | tf_op jit(solution)/shard_map/ppermute | solution.py:12
  205.6 5.2 %collective-permute-start.5 = (f32[2,4096,16]{1,2,0:T(8,128)S(1)}, f32[2,4096,16]{1,2,0:T(8,128)S(1)}, u32[]{:S(2)}, u32[]{:S(2)}) collective-permute-start(f32[2,4096,16]{1,2,0:T(8,128)S(1)} %slice_select_fusion.1), channel_id=1, source_target_pairs={{0,1},{1,0},{2,3},{3,2},{4,5},{5,4},{6,7},{7,6},{8,9},{9,8},{10,11... | collective-permute-start | bytes 1572872 | tf_op jit(solution)/shard_map/ppermute | solution.py:12
  210.8 1.5 collective-permute-done.5
  212.3 0.9 select_add_fusion.2
  213.3 83.8 %reduce-scatter.2.cloned.1.call-done = f32[2,512,16]{1,2,0:T(8,128)} async-done(((f32[2,4096,16]{1,2,0:T(8,128)}), f32[2,512,16]{1,2,0:T(8,128)}) %reduce-scatter.2.cloned.1.call-update) | async-done | bytes 65552 | tf_op jit(solution)/shard_map/reduce_scatter | solution.py:119
  (61 shorter events, 5.4 us)
Async XLA Ops:
  7.2 62.0 %copy-start.3 = (bf16[512,128]{1,0:T(8,128)(2,1)S(1)}, bf16[512,128]{1,0:T(8,128)(2,1)}, u32[]{:S(2)}) copy-start(bf16[512,128]{1,0:T(8,128)(2,1)} %param.10) | copy-start | bytes 393220
  7.2 62.0 %copy-start.5 = (bf16[512,128]{1,0:T(8,128)(2,1)S(1)}, bf16[512,128]{1,0:T(8,128)(2,1)}, u32[]{:S(2)}) copy-start(bf16[512,128]{1,0:T(8,128)(2,1)} %param.9) | copy-start | bytes 393220
  7.2 289.9 %reduce-scatter.2.cloned.1.call-start = ((), (), s32[]{:S(2)}) async-start(), calls=%async_computation.1 | async-start | bytes 589824 | tf_op jit(solution)/shard_map/reduce_scatter | solution.py:119
  37.1 14.7 %collective-permute-start = (bf16[2,4096,16]{1,2,0:T(8,128)(2,1)S(1)}, bf16[2,4096,16]{1,2,0:T(8,128)(2,1)S(1)}, u32[]{:S(2)}, u32[]{:S(2)}) collective-permute-start(bf16[2,4096,16]{1,2,0:T(8,128)(2,1)S(1)} %all_gather.3), channel_id=1, source_target_pairs={{0,1},{1,0},{2,3},{3,2},{4,5},{5,4},{6,7},{7,6},{8,9},{9,8},{10,11... | collective-permute-start | bytes 786440 | tf_op jit(solution)/shard_map/ppermute | solution.py:12
  52.0 15.0 %collective-permute-start.1 = (bf16[2,4096,32]{1,2,0:T(8,128)(2,1)S(1)}, bf16[2,4096,32]{1,2,0:T(8,128)(2,1)S(1)}, u32[]{:S(2)}, u32[]{:S(2)}) collective-permute-start(bf16[2,4096,32]{1,2,0:T(8,128)(2,1)S(1)} %maximum_select_fusion.2), channel_id=1, source_target_pairs={{0,2},{1,3},{2,0},{3,1},{4,6},{5,7},{6,4},{7,5},{8,10},{9,11},{10,... | collective-permute-start | bytes 1572872 | tf_op jit(solution)/shard_map/ppermute | solution.py:12
  67.2 25.4 %collective-permute-start.2 = (bf16[2,4096,64]{1,2,0:T(8,128)(2,1)S(1)}, bf16[2,4096,64]{1,2,0:T(8,128)(2,1)S(1)}, u32[]{:S(2)}, u32[]{:S(2)}) collective-permute-start(bf16[2,4096,64]{1,2,0:T(8,128)(2,1)S(1)} %maximum_select_fusion.1), channel_id=1, source_target_pairs={{0,4},{1,5},{2,6},{3,7},{4,0},{5,1},{6,2},{7,3},{8,12},{9,13},{10,... | collective-permute-start | bytes 3145736 | tf_op jit(solution)/shard_map/ppermute | solution.py:12
  94.5 2.5 copy-start.4
  94.6 2.5 copy-start.6
  94.6 2.5 copy-start.7
  97.1 2.2 copy-start.1
  98.6 0.9 copy-start.8
  99.9 0.7 copy-start.9
  104.0 3.5 %copy-start.2 = (bf16[32,128,128]{2,1,0:T(8,128)(2,1)S(1)}, bf16[32,128,128]{2,1,0:T(8,128)(2,1)}, u32[]{:S(2)}) copy-start(bf16[32,128,128]{2,1,0:T(8,128)(2,1)} %copy-done.1) | copy-start | bytes 3145732 | tf_op jit(solution)/shard_map/while
  107.5 2.2 copy-start.1
  109.0 0.9 copy-start.8
  110.3 0.7 copy-start.9
  114.4 3.4 %copy-start.2 = (bf16[32,128,128]{2,1,0:T(8,128)(2,1)S(1)}, bf16[32,128,128]{2,1,0:T(8,128)(2,1)}, u32[]{:S(2)}) copy-start(bf16[32,128,128]{2,1,0:T(8,128)(2,1)} %copy-done.1) | copy-start | bytes 3145732 | tf_op jit(solution)/shard_map/while
  132.3 48.4 %copy-start = (f32[2,4096,64]{1,2,0:T(8,128)S(1)}, f32[2,4096,64]{1,2,0:T(8,128)}, u32[]{:S(2)}) copy-start(f32[2,4096,64]{1,2,0:T(8,128)} %copy.18) | copy-start | bytes 6291460
  132.6 48.1 %collective-permute-start.3 = (f32[2,4096,64]{1,2,0:T(8,128)S(1)}, f32[2,4096,64]{1,2,0:T(8,128)S(1)}, u32[]{:S(2)}, u32[]{:S(2)}) collective-permute-start(f32[2,4096,64]{1,2,0:T(8,128)S(1)} %broadcast_select_fusion), channel_id=1, source_target_pairs={{0,4},{1,5},{2,6},{3,7},{4,0},{5,1},{6,2},{7,3},{8,12},{9,13},{10,... | collective-permute-start | bytes 6291464 | tf_op jit(solution)/shard_map/ppermute | solution.py:12
  181.2 24.1 %collective-permute-start.4 = (f32[2,4096,32]{1,2,0:T(8,128)S(1)}, f32[2,4096,32]{1,2,0:T(8,128)S(1)}, u32[]{:S(2)}, u32[]{:S(2)}) collective-permute-start(f32[2,4096,32]{1,2,0:T(8,128)S(1)} %slice_select_fusion), channel_id=1, source_target_pairs={{0,2},{1,3},{2,0},{3,1},{4,6},{5,7},{6,4},{7,5},{8,10},{9,11},{10,... | collective-permute-start | bytes 3145736 | tf_op jit(solution)/shard_map/ppermute | solution.py:12
  205.6 6.8 %collective-permute-start.5 = (f32[2,4096,16]{1,2,0:T(8,128)S(1)}, f32[2,4096,16]{1,2,0:T(8,128)S(1)}, u32[]{:S(2)}, u32[]{:S(2)}) collective-permute-start(f32[2,4096,16]{1,2,0:T(8,128)S(1)} %slice_select_fusion.1), channel_id=1, source_target_pairs={{0,1},{1,0},{2,3},{3,2},{4,5},{5,4},{6,7},{7,6},{8,9},{9,8},{10,11... | collective-permute-start | bytes 1572872 | tf_op jit(solution)/shard_map/ppermute | solution.py:12
Sparse Core Ops, SparseCore 0:
  213.4 83.6 reduce-scatter.1
where the time goes:
time: 305 us; the launch traced here: 304 us
  waiting for transfers between devices  188 us (62%)
  blocking collectives  29.9 us (10%)
  starting transfers between devices  29.5 us (10%)
  local copies, waits for them, and re-layouts  22.1 us (7%)
  other arithmetic  16.6 us (5%)
  between operations  14.3 us (5%)
  matrix products  3.12 us (1%)
    ppermute x6, waiting for transfers between devices, from_partner(): lax.ppermute(value, axis, [(i, i ^ 1 << stride) for i in range(lax.axis_s...  104 us
    reduce_scatter x1, waiting for transfers between devices, shards(): kv_grad = lax.psum_scatter(current, 'ctx', scatter_dimension=1, tiled=True)  83.8 us
    all_gather x1, blocking collectives, shards(): current = lax.all_gather(keys_values, 'ctx', axis=1, tiled=True)  29.9 us
    ppermute x6, starting transfers between devices, from_partner(): lax.ppermute(value, axis, [(i, i ^ 1 << stride) for i in range(lax.axis_s...  29.5 us
    slice x1, local copies, waits for them, and re-layouts, split_halves(): high_half = current[:, :, half_width:]  7.83 us
    scatter-add x2, other arithmetic, pair_step(): carry = carry.at[1, flat_ids].add(value_grad.reshape(-1, BLOCK, DH))  6.92 us
    scatter-add x2, other arithmetic, pair_step(): carry = carry.at[0, flat_ids].add(key_grad.reshape(-1, BLOCK, DH))  6.9 us
    unnamed x14, local copies, waits for them, and re-layouts  6.68 us
  transfers between devices with their start and end apart: 7, of which 7 were waited for; matrix products, arithmetic and copies ran while one was open for 0% of the time, Pallas kernels for 0%

commit v1 on v0

v1 whole, which is shorter than its diff:
```python
import jax
import jax.numpy as jnp
from jax import lax
from jax.experimental import pallas as pl
from jax.experimental.pallas import tpu as pltpu
from jax.sharding import Mesh, PartitionSpec as P

KVH = 8
DH = 128
BLOCK = 128
F32 = jnp.float32
BF16 = jnp.bfloat16
I32 = jnp.int32
SCALE = DH ** -0.5
UNROLL = 4
CHIPS = ("yl", "zl", "x", "yh")
VMEM = pl.BlockSpec(memory_space=pltpu.VMEM)
SMEM = pl.BlockSpec(memory_space=pltpu.SMEM)
ROW_Q, ROW_G, ROW_O, ROW_S, ROW_KV, ROWS = 0, 512, 1024, 1536, 1552, 1616


def call(kernel, outs, in_specs, scratch=(), limit=24, name=None):
    return pl.pallas_call(
        kernel,
        out_shape=outs,
        in_specs=in_specs,
        out_specs=jax.tree.map(lambda _: VMEM, outs),
        scratch_shapes=list(scratch),
        compiler_params=pltpu.CompilerParams(vmem_limit_bytes=limit * 2**20),
        name=name,
    )


def pack_kernel(core_ref, q_ref, g_ref, o_ref, lse_ref, ids_ref, kv_ref, out_ref, small_ref):
    other = 1 - core_ref[0]
    out_ref[ROW_Q:ROW_G] = q_ref[...]
    out_ref[ROW_G:ROW_O] = g_ref[...]
    out_ref[ROW_O:ROW_S] = o_ref[...]
    lse = lse_ref[...]
    high = lse.astype(BF16).astype(F32)
    rest = lse - high
    middle = rest.astype(BF16).astype(F32)
    small_ref[...] = jnp.zeros((16, 128), F32)
    small_ref[0:4] = high
    small_ref[4:8] = middle
    small_ref[8:12] = rest - middle
    small_ref[12:16, 0:8] = ids_ref[...].astype(F32)
    out_ref[ROW_S:ROW_KV] = small_ref[...].astype(BF16)
    for which in range(2):
        for j in range(2):
            row = ROW_KV + (which * 2 + j) * 16
            out_ref[row : row + 16] = kv_ref[which, :, pl.ds(pl.multiple_of(other * 256 + j * 128, 128), 128)]


def spread_kernel(core_ref, kv_ref, pay_ref, out_ref):
    core = core_ref[0]
    for which in range(2):
        for j in range(2):
            own = kv_ref[which, :, pl.ds(pl.multiple_of(core * 256 + j * 128, 128), 128)]
            row = ROW_KV + (which * 2 + j) * 16
            got = pay_ref[row : row + 16]
            first = jnp.where(core == 0, own, got)
            second = jnp.where(core == 0, got, own)
            both = jnp.concatenate((first, second), 0)
            for chip in range(32):
                out_ref[chip, which, j] = both


def main_kernel(
    core_ref, ids_ref, q_ref, g_ref, o_ref, lse_ref, pay_ref, kv_ref,
    part_ref, dq_own_ref, dq_other_ref,
    q_all, g_all, q_t, g_t, lse_all, delta_all, acc, dq_acc, ids_v, ids_s, tiles, sem,
):
    core = core_ref[0]
    small = pay_ref[ROW_S:ROW_KV].astype(F32)
    ids_v[...] = small[8:16].astype(I32)
    copy = pltpu.make_async_copy(ids_v, ids_s, sem)
    copy.start()
    lse_other = small[0:4] + small[4:8] + small[8:12]
    lse_own = lse_ref[...]
    for b in range(8):
        rows = slice((b % 4) * 128, (b % 4) * 128 + 128)
        if b < 4:
            q, g, o = q_ref[rows], g_ref[rows], o_ref[rows]
            lse = lse_own[b : b + 1]
        else:
            at = (b - 4) * 128
            q = pay_ref[ROW_Q + at : ROW_Q + at + 128]
            g = pay_ref[ROW_G + at : ROW_G + at + 128]
            o = pay_ref[ROW_O + at : ROW_O + at + 128]
            lse = lse_other[b - 4 : b - 3]
        q_all[b] = q
        g_all[b] = g
        q_t[b] = q.T
        g_t[b] = g.T
        lse_all[b] = jnp.broadcast_to(lse, (128, 128)).T
        delta = jnp.sum(g.astype(F32) * o.astype(F32), axis=1, keepdims=True)
        delta_all[b] = jnp.broadcast_to(delta, (128, 128))
    acc[...] = jnp.zeros(acc.shape, F32)
    dq_acc[...] = jnp.zeros(dq_acc.shape, F32)
    copy.wait()
    count = jnp.int32(0)
    for b in range(8):
        for r in range(8):
            block = ids_ref[b, r] if b < 4 else ids_s[b, r]
            local = (block >> 2) * 2 + (block & 1)
            tiles[count] = b + local * 16 + b * 512 + local * 8192
            count = count + jnp.where(((block >> 1) & 1) == core, 1, 0)
    for u in range(UNROLL):
        tiles[count + u] = 8 * 512 + 16 * 8192

    def step(group, carry):
        items = []
        for u in range(UNROLL):
            word = tiles[group * UNROLL + u]
            b = word & 15
            local = (word >> 4) & 15
            yh, x, j = local >> 3, (local >> 1) & 3, local & 1
            k, v = (
                jnp.concatenate(
                    [kv_ref[yl, zl, x, yh, which, j] for zl in range(2) for yl in range(2)], 0
                )
                for which in range(2)
            )
            scores = jnp.dot(q_all[b], k, preferred_element_type=F32) * SCALE
            weights = jnp.exp(scores - lse_all[b])
            weight_grad = jnp.dot(g_all[b], v, preferred_element_type=F32)
            score_grad = (weights * (weight_grad - delta_all[b]) * SCALE).astype(BF16)
            weights_bf = weights.astype(BF16)
            dq = lax.dot_general(score_grad, k, (((1,), (1,)), ((), ())), preferred_element_type=F32)
            dk = jnp.dot(q_t[b], score_grad, preferred_element_type=F32)
            dv = jnp.dot(g_t[b], weights_bf, preferred_element_type=F32)
            items.append(((word >> 9) & 15, word >> 13, dq, dk, dv))
        for b, local, dq, dk, dv in items:
            dq_acc[b] += dq
            acc[local, 0] += dk
            acc[local, 1] += dv
        return carry

    lax.fori_loop(0, (count + UNROLL - 1) // UNROLL, step, 0)
    for b in range(4):
        dq_own_ref[b * 128 : b * 128 + 128] = dq_acc[b]
        dq_other_ref[b * 128 : b * 128 + 128] = dq_acc[b + 4]
    for yl in range(2):
        for zl in range(2):
            feature = (zl * 2 + yl) * 32
            for x in range(4):
                for yh in range(2):
                    for which in range(2):
                        for j in range(2):
                            local = (yh * 4 + x) * 2 + j
                            part_ref[yl, zl, x, yh, which, j] = acc[
                                local, which, feature : feature + 32
                            ].astype(BF16)


def sum_kernel(core_ref, got_ref, dq_other_ref, mine_ref, out_ref, total):
    core = core_ref[0]
    for t in range(4):
        value = got_ref[0, t].astype(F32)
        for chip in range(1, 32):
            value = value + got_ref[chip, t].astype(F32)
        total[t] = value
    out_ref[0:512] = dq_other_ref[...]
    for t in range(4):
        mine_ref[t] = total[t, pl.ds(pl.multiple_of(core * 16, 16), 16)]
        out_ref[512 + t * 16 : 528 + t * 16] = total[t, pl.ds(pl.multiple_of(16 - core * 16, 16), 16)]


def last_kernel(core_ref, mine_ref, got_ref, dq_ref, dq_out, kv_out):
    core = core_ref[0]
    dq_out[...] = (dq_ref[...] + got_ref[0:512]).astype(BF16)
    for which in range(2):
        for j in range(2):
            t = which * 2 + j
            own = mine_ref[t]
            got = got_ref[512 + t * 16 : 528 + t * 16]
            kv_out[which, :, j * 128 : j * 128 + 128] = jnp.where(core == 0, own, got)
            kv_out[which, :, 256 + j * 128 : 384 + j * 128] = jnp.where(core == 0, got, own)


def shards(queries, outputs, out_grad, keys_values, row_lse, collide):
    core = lax.axis_index("core").astype(I32).reshape(1)
    swap = [(0, 1), (1, 0)]
    kv = keys_values.transpose(0, 2, 1)
    lse = row_lse.reshape(4, BLOCK)
    ids = collide.reshape(4, 8)
    struct = jax.ShapeDtypeStruct
    packed = call(
        pack_kernel, struct((ROWS, DH), BF16), [SMEM] + [VMEM] * 6,
        [pltpu.VMEM((16, 128), F32)], name="pack",
    )(core, queries, out_grad, outputs, lse, ids, kv)
    pay = lax.ppermute(packed, "core", swap)
    spread = call(
        spread_kernel, struct((32, 2, 2, 32, 128), BF16), [SMEM, VMEM, VMEM], name="spread",
    )(core, kv, pay)
    gathered = lax.all_to_all(spread.reshape(32, 128, 128), CHIPS, 0, 0)
    part, dq_own, dq_other = call(
        main_kernel,
        (
            struct((2, 2, 4, 2, 2, 2, 32, 128), BF16),
            struct((512, DH), F32),
            struct((512, DH), F32),
        ),
        [SMEM, SMEM] + [VMEM] * 6,
        [pltpu.VMEM((8, 128, 128), BF16)] * 4
        + [pltpu.VMEM((8, 128, 128), F32)] * 2
        + [
            pltpu.VMEM((17, 2, 128, 128), F32),
            pltpu.VMEM((9, 128, 128), F32),
            pltpu.VMEM((8, 128), I32),
            pltpu.SMEM((8, 128), I32),
            pltpu.SMEM((72,), I32),
            pltpu.SemaphoreType.DMA,
        ],
        name="attend",
    )(core, ids, queries, out_grad, outputs, lse, pay, gathered.reshape(2, 2, 4, 2, 2, 2, 32, 128))
    got = lax.all_to_all(part.reshape(32, 128, 128), CHIPS, 0, 0)
    mine, back = call(
        sum_kernel, (struct((4, 16, 128), F32), struct((576, DH), F32)), [SMEM, VMEM, VMEM],
        [pltpu.VMEM((4, 32, 128), F32)], name="total",
    )(core, got.reshape(32, 4, 32, 128), dq_other)
    back = lax.ppermute(back, "core", swap)
    query_grad, kv_grad = call(
        last_kernel, (struct((512, DH), BF16), struct((2, 16, 512), F32)), [SMEM] + [VMEM] * 3,
        name="last",
    )(core, mine, back, dq_own)
    return query_grad, kv_grad.transpose(0, 2, 1)


def solution(mesh):
    fine = Mesh(
        mesh.devices.reshape(2, 4, KVH, 2, 2, 2), ("yh", "x", "group", "zl", "yl", "core")
    )
    ctx, head = ("yh", "x"), ("group", "zl", "yl", "core")
    placed = (
        P(ctx, head), P(ctx, head), P(ctx, head), P(None, ctx, head), P(head, ctx), P(head, ctx, None),
    )
    return jax.shard_map(
        shards, mesh=fine, in_specs=placed, out_specs=(P(ctx, head), P(None, ctx, head)),
        check_vma=False,
    )
```

time: 305 us -> 71.8 us (0.24)
  waiting for transfers between devices: 188 us -> 2.54 us
  local copies, waits for them, and re-layouts: 22.1 us -> 4.16 us
  other arithmetic: 16.6 us -> 0 us
  starting transfers between devices: 29.5 us -> 13.6 us
  between operations: 14.3 us -> 0.7 us
  Pallas kernels: 0 us -> 10.9 us
  blocking collectives: 29.9 us -> 39.6 us
  matrix products: 3.12 us -> 0 us
    ppermute x6 -> x2, waiting for transfers between devices: 104 us -> 2.54 us  [the longest x1 1.36 us: shards(): pay = lax.ppermute(packed, 'core', swap)]
    reduce_scatter x1 -> x0, waiting for transfers between devices: 83.8 us -> none  [shards(): kv_grad = lax.psum_scatter(current, 'ctx', scatter_dimension=1, tiled=True)]
    all_to_all x0 -> x2, blocking collectives: none -> 39.6 us  [the longest x1 20.4 us: shards(): gathered = lax.all_to_all(spread.reshape(32, 128, 128), CHIPS, 0, 0)]
    all_gather x1 -> x0, blocking collectives: 29.9 us -> none  [shards(): current = lax.all_gather(keys_values, 'ctx', axis=1, tiled=True)]
    ppermute x6 -> x2, starting transfers between devices: 29.5 us -> 13.6 us  [the longest x1 8.74 us: shards(): pay = lax.ppermute(packed, 'core', swap)]
    scatter-add x4 -> x0, other arithmetic: 13.8 us -> none  [the longest x2 6.92 us: pair_step(): carry = carry.at[1, flat_ids].add(value_grad.reshape(-1, BLOCK, DH))]
    pallas_call x0 -> x5, Pallas kernels: none -> 10.9 us  [the longest x1 9.81 us: shards(): call(main_kernel, (struct((2, 2, 4, 2, 2, 2, 32, 128), BF16), struct((512...]
    slice x4 -> x0, local copies, waits for them, and re-layouts: 9.29 us -> none  [the longest x1 7.83 us: split_halves(): high_half = current[:, :, half_width:]]
  transfers between devices with their start and end apart: 7 -> 2, of which waited for: 7 -> 2; matrix products, arithmetic and copies ran while one was open for 0% -> 0% of each run, Pallas kernels for 0% -> 0%
where the time goes in v1:
time: 71.8 us; the launch traced here: 71.5 us
  blocking collectives  39.6 us (55%)
  starting transfers between devices  13.6 us (19%)
  Pallas kernels  10.9 us (15%)
  local copies, waits for them, and re-layouts  4.16 us (6%)
  waiting for transfers between devices  2.54 us (4%)
    all_to_all x1, blocking collectives, shards(): gathered = lax.all_to_all(spread.reshape(32, 128, 128), CHIPS, 0, 0)  20.4 us
    all_to_all x1, blocking collectives, shards(): got = lax.all_to_all(part.reshape(32, 128, 128), CHIPS, 0, 0)  19.2 us
    pallas_call x1, Pallas kernels, shards(): call(main_kernel, (struct((2, 2, 4, 2, 2, 2, 32, 128), BF16), struct((512...  9.81 us
    ppermute x1, starting transfers between devices, shards(): pay = lax.ppermute(packed, 'core', swap)  8.74 us
    ppermute x1, starting transfers between devices, shards(): back = lax.ppermute(back, 'core', swap)  4.83 us
    unnamed x14, local copies, waits for them, and re-layouts  4.16 us
  transfers between devices with their start and end apart: 2, of which 2 were waited for; matrix products, arithmetic and copies ran while one was open for 0% of the time, Pallas kernels for 0%

profile of v1, /device:TPU:1, one launch (start us, length us, event | category | flops | bytes accessed | tf_op | source)
XLA Modules:
  0.0 71.5 jit_solution(13097580101335686095)
XLA Ops:
  0.6 0.0 copy-start.6
  0.6 0.0 copy-start.5
  0.7 0.7 copy-done.6
  1.3 0.0 copy-done.5
  1.3 0.0 copy-start
  1.3 0.9 %copy-done = bf16[512,128]{1,0:T(8,128)(2,1)S(1)} copy-done((bf16[512,128]{1,0:T(8,128)(2,1)S(1)}, bf16[512,128]{1,0:T(8,128)(2,1)}, u32[]{:S(2)}) %copy-start) | copy-done | bytes 131096
  2.2 0.0 copy-start.2
  2.2 0.9 %copy-done.2 = bf16[512,128]{1,0:T(8,128)(2,1)S(1)} copy-done((bf16[512,128]{1,0:T(8,128)(2,1)S(1)}, bf16[512,128]{1,0:T(8,128)(2,1)}, u32[]{:S(2)}) %copy-start.2) | copy-done | bytes 131096
  3.1 0.0 copy-start.3
  3.1 0.9 %copy-done.3 = bf16[512,128]{1,0:T(8,128)(2,1)S(1)} copy-done((bf16[512,128]{1,0:T(8,128)(2,1)S(1)}, bf16[512,128]{1,0:T(8,128)(2,1)}, u32[]{:S(2)}) %copy-start.3) | copy-done | bytes 131096
  4.0 0.0 copy-start.4
  4.1 0.8 %copy-done.4 = bf16[2,512,16]{1,2,0:T(8,128)(2,1)S(1)} copy-done((bf16[2,512,16]{1,2,0:T(8,128)(2,1)S(1)}, bf16[2,512,16]{1,2,0:T(8,128)(2,1)}, u32[]{:S(2)}) %copy-start.4) | copy-done | bytes 32792
  4.8 8.7 %collective-permute-start = (bf16[1616,128]{1,0:T(8,128)(2,1)S(1)}, bf16[1616,128]{1,0:T(8,128)(2,1)S(1)}, u32[]{:S(2)}, u32[]{:S(2)}) collective-permute-start(bf16[1616,128]{1,0:T(8,128)(2,1)S(1)} %pack.1), channel_id=1, source_target_pairs={{0,1},{1,0},{2,3},{3,2},{4,5},{5,4},{6,7},{7,6},{8,9},{9,8},{10,11... | collective-permute-start | bytes 1241096 | tf_op jit(solution)/shard_map/ppermute | solution.py:193
  13.6 1.4 %collective-permute-done.pay_ref = bf16[1616,128]{1,0:T(8,128)(2,1)S(1)} collective-permute-done((bf16[1616,128]{1,0:T(8,128)(2,1)S(1)}, bf16[1616,128]{1,0:T(8,128)(2,1)S(1)}, u32[]{:S(2)}, u32[]{:S(2)}) %collective-permute-start) | collective-permute-done | bytes 413728 | tf_op jit(solution)/shard_map/ppermute | solution.py:193
  15.0 0.2 spread.1
  15.2 0.0 copy-start.1
  15.2 20.4 %all_to_all.10 = bf16[32,128,128]{2,1,0:T(8,128)(2,1)S(1)} all-to-all(bf16[32,128,128]{2,1,0:T(8,128)(2,1)S(1)} %bitcast.11), channel_id=1, replica_groups=mesh['yh'=2,'x'=4,'group'=8,'zl'=2,'yl'=2,'core'=2] {'yl','zl','x','yh'}, dimensions={0} | all-to-all | bytes 2097152 | tf_op jit(solution)/shard_map/all_to_all | solution.py:197
  35.6 0.0 copy-done.1
  35.6 9.8 %attend.1 = (bf16[2,2,4,2,2,2,32,128]{7,6,5,4,3,2,1,0:T(8,128)(2,1)S(1)}, f32[512,128]{1,0:T(8,128)S(1)}, f32[512,128]{1,0:T(8,128)S(1)}) custom-call(s32[1]{0:T(128)} %bitcast.core_ref, s32[4,8]{1,0:T(4,128)S(1)} %bitcast.16, bf16[512,128]{1,0:T(8,128)(2,1)S(1)} %copy-done.1, bf16[512,128]{1,0:T(8,128)(2,1)S(1)} %copy-done.2, ...), custom_call_target="tpu_custom_call" | custom-call | tf_op jit(solution)/shard_map/attend/pallas_call | solution.py:198
  45.4 19.2 %all_to_all.11 = bf16[32,128,128]{2,1,0:T(8,128)(2,1)S(1)} all-to-all(bf16[32,128,128]{2,1,0:T(8,128)(2,1)S(1)} %bitcast.12), channel_id=1, replica_groups=mesh['yh'=2,'x'=4,'group'=8,'zl'=2,'yl'=2,'core'=2] {'yl','zl','x','yh'}, dimensions={0} | all-to-all | bytes 2097152 | tf_op jit(solution)/shard_map/all_to_all | solution.py:218
  64.6 0.1 total.1
  64.7 4.8 %collective-permute-start.1 = (f32[576,128]{1,0:T(8,128)S(1)}, f32[576,128]{1,0:T(8,128)S(1)}, u32[]{:S(2)}, u32[]{:S(2)}) collective-permute-start(f32[576,128]{1,0:T(8,128)S(1)} %get-tuple-element.12), channel_id=1, source_target_pairs={{0,1},{1,0},{2,3},{3,2},{4,5},{5,4},{6,7},{7,6},{8,9},{9,8},{10,11... | collective-permute-start | bytes 884744 | tf_op jit(solution)/shard_map/ppermute | solution.py:223
  69.6 1.2 %collective-permute-done.1.got_ref = f32[576,128]{1,0:T(8,128)S(1)} collective-permute-done((f32[576,128]{1,0:T(8,128)S(1)}, f32[576,128]{1,0:T(8,128)S(1)}, u32[]{:S(2)}, u32[]{:S(2)}) %collective-permute-start.1) | collective-permute-done | bytes 294944 | tf_op jit(solution)/shard_map/ppermute | solution.py:223
  70.8 0.7 %last.1 = (bf16[512,128]{1,0:T(8,128)(2,1)}, f32[2,16,512]{2,1,0:T(8,128)}) custom-call(s32[1]{0:T(128)} %bitcast.core_ref, f32[4,16,128]{2,1,0:T(8,128)S(1)} %get-tuple-element.11.mine_ref, f32[576,128]{1,0:T(8,128)S(1)} %collective-permute-done.1.got_ref, f32[512,128]{1,0:T(8,128)S(1)} %get-tuple-element.13.dq_ref), custom_call_target="tpu_custom_call" | custom-call | tf_op jit(solution)/shard_map/last/pallas_call | solution.py:224
  (1 shorter events, 0.0 us)
Async XLA Ops:
  0.6 0.7 copy-start.6
  0.6 0.7 copy-start.5
  1.3 0.9 %copy-start = (bf16[512,128]{1,0:T(8,128)(2,1)S(1)}, bf16[512,128]{1,0:T(8,128)(2,1)}, u32[]{:S(2)}) copy-start(bf16[512,128]{1,0:T(8,128)(2,1)} %q_ref.3) | copy-start | bytes 393220
  2.2 0.9 %copy-start.2 = (bf16[512,128]{1,0:T(8,128)(2,1)S(1)}, bf16[512,128]{1,0:T(8,128)(2,1)}, u32[]{:S(2)}) copy-start(bf16[512,128]{1,0:T(8,128)(2,1)} %g_ref.3) | copy-start | bytes 393220
  3.1 0.9 %copy-start.3 = (bf16[512,128]{1,0:T(8,128)(2,1)S(1)}, bf16[512,128]{1,0:T(8,128)(2,1)}, u32[]{:S(2)}) copy-start(bf16[512,128]{1,0:T(8,128)(2,1)} %o_ref.3) | copy-start | bytes 393220
  4.0 0.8 %copy-start.4 = (bf16[2,512,16]{1,2,0:T(8,128)(2,1)S(1)}, bf16[2,512,16]{1,2,0:T(8,128)(2,1)}, u32[]{:S(2)}) copy-start(bf16[2,512,16]{1,2,0:T(8,128)(2,1)} %param.9) | copy-start | bytes 98308
  4.8 10.1 %collective-permute-start = (bf16[1616,128]{1,0:T(8,128)(2,1)S(1)}, bf16[1616,128]{1,0:T(8,128)(2,1)S(1)}, u32[]{:S(2)}, u32[]{:S(2)}) collective-permute-start(bf16[1616,128]{1,0:T(8,128)(2,1)S(1)} %pack.1), channel_id=1, source_target_pairs={{0,1},{1,0},{2,3},{3,2},{4,5},{5,4},{6,7},{7,6},{8,9},{9,8},{10,11... | collective-permute-start | bytes 1241096 | tf_op jit(solution)/shard_map/ppermute | solution.py:193
  15.2 20.4 %copy-start.1 = (bf16[512,128]{1,0:T(8,128)(2,1)S(1)}, bf16[512,128]{1,0:T(8,128)(2,1)}, u32[]{:S(2)}) copy-start(bf16[512,128]{1,0:T(8,128)(2,1)} %q_ref.3) | copy-start | bytes 393220
  64.7 6.0 %collective-permute-start.1 = (f32[576,128]{1,0:T(8,128)S(1)}, f32[576,128]{1,0:T(8,128)S(1)}, u32[]{:S(2)}, u32[]{:S(2)}) collective-permute-start(f32[576,128]{1,0:T(8,128)S(1)} %get-tuple-element.12), channel_id=1, source_target_pairs={{0,1},{1,0},{2,3},{3,2},{4,5},{5,4},{6,7},{7,6},{8,9},{9,8},{10,11... | collective-permute-start | bytes 884744 | tf_op jit(solution)/shard_map/ppermute | solution.py:223

commit v2 on v1

v2 whole, which is shorter than its diff:
```python
import jax
import jax.numpy as jnp
from jax import lax
from jax.experimental import pallas as pl
from jax.experimental.pallas import tpu as pltpu
from jax.sharding import Mesh, PartitionSpec as P

KVH = 8
DH = 128
BLOCK = 128
F32 = jnp.float32
BF16 = jnp.bfloat16
I32 = jnp.int32
SCALE = DH ** -0.5
PAIRS = 2
CHIPS = ("x", "yl", "zl", "yh")
HBM = pl.BlockSpec(memory_space=pltpu.MemorySpace.HBM)
VMEM = pl.BlockSpec(memory_space=pltpu.VMEM)
ROW_Q, ROW_G, ROW_S, ROWS = 0, 512, 1024, 1056


def call(kernel, outs, in_specs, scratch=(), limit=4, name=None):
    return pl.pallas_call(
        kernel,
        out_shape=outs,
        in_specs=in_specs,
        out_specs=jax.tree.map(lambda _: VMEM, outs),
        scratch_shapes=list(scratch),
        compiler_params=pltpu.CompilerParams(vmem_limit_bytes=limit * 2**20),
        name=name,
    )


def pieces(value):
    high = value.astype(BF16).astype(F32)
    rest = value - high
    middle = rest.astype(BF16).astype(F32)
    return high, middle, rest - middle


def pack_kernel(q_ref, g_ref, o_ref, lse_ref, ids_ref, out_ref, o_v, lse_v, ids_v, small, sems):
    copies = [
        pltpu.make_async_copy(source, target, sems.at[n])
        for n, (source, target) in enumerate((
            (lse_ref, lse_v),
            (ids_ref, ids_v),
            (q_ref, out_ref.at[ROW_Q:ROW_G]),
            (g_ref, out_ref.at[ROW_G:ROW_S]),
            (o_ref, o_v),
        ))
    ]
    for copy in copies:
        copy.start()
    small[...] = jnp.zeros((32, 128), F32)
    for copy in copies:
        copy.wait()
    lane = lax.broadcasted_iota(I32, (128, 128), 1)
    columns = jnp.zeros((128, 128), F32)
    for b in range(4):
        rows = slice(b * 128, b * 128 + 128)
        g = out_ref[ROW_G + b * 128 : ROW_G + b * 128 + 128]
        delta = jnp.sum(g.astype(F32) * o_v[rows].astype(F32), axis=1, keepdims=True)
        columns = jnp.where(lane == b, delta, columns)
    for n, piece in enumerate(pieces(lse_v[...]) + pieces(columns.T[0:4])):
        small[n * 4 : n * 4 + 4] = piece
    small[24:28, 0:8] = ids_v[...].astype(F32)
    out_ref[ROW_S:ROWS] = small[...].astype(BF16)


def stage_kernel(kv_ref, out_ref, sem):
    copy = pltpu.make_async_copy(kv_ref, out_ref, sem)
    copy.start()
    copy.wait()


def spread_kernel(own_ref, got_ref, out_ref):
    core = lax.axis_index("core")
    for which in range(2):
        for j in range(2):
            own_low, got_low = (ref[which, :, j * 128 : j * 128 + 128] for ref in (own_ref, got_ref))
            own_high, got_high = (ref[which, :, 256 + j * 128 : 384 + j * 128] for ref in (own_ref, got_ref))
            first = jnp.where(core == 0, own_low, got_high)
            second = jnp.where(core == 0, got_low, own_high)
            both = jnp.concatenate((first, second), 0)
            for chip in range(32):
                out_ref[chip, which, j] = both


NONE = 16
NO_PAIR = NONE + (8 << 14)


def ready_kernel(own_ref, got_ref, qg_ref, columns_ref, words_ref, table):
    core = lax.axis_index("core")
    table[...] = jnp.zeros((128, 128), F32)
    blocks = []
    for n, ref in enumerate((own_ref, got_ref)):
        small = ref[ROW_S:ROWS].astype(F32)
        table[n * 4 : n * 4 + 4] = small[0:4] + small[4:8] + small[8:12]
        table[8 + n * 4 : 12 + n * 4] = small[12:16] + small[16:20] + small[20:24]
        blocks.append(small[24:28])
        for b in range(4):
            qg_ref[n * 8 + b * 2] = ref[ROW_Q + b * 128 : ROW_Q + b * 128 + 128]
            qg_ref[n * 8 + b * 2 + 1] = ref[ROW_G + b * 128 : ROW_G + b * 128 + 128]
    columns_ref[...] = table[...].T
    block = jnp.concatenate(blocks, 0).astype(I32)
    row = lax.broadcasted_iota(I32, block.shape, 0)
    word = ((block >> 2) & 3) * 1024 + (block >> 4) * 128 + (block & 1) * 32
    word = word + (block >> 2) * 2 + (block & 1) + (row << 14) + (1 << 20)
    words_ref[...] = jnp.where(((block >> 1) & 1) == core, word, NONE)


def main_kernel(
    kv_ref, qg_ref, columns_ref, words_ref, part_ref, dq_own_ref, dq_other_ref,
    q_t, g_t, lse_all, delta_all, acc, dq_acc, held_w, held_s, words_s, slots, sem,
):
    copy = pltpu.make_async_copy(words_ref, words_s, sem)
    copy.start()
    for b in range(8):
        q_t[b] = qg_ref[b * 2].T
        g_t[b] = qg_ref[b * 2 + 1].T
    copy.wait()
    acc[...] = jnp.zeros(acc.shape, F32)
    dq_acc[...] = jnp.zeros(dq_acc.shape, F32)
    for b in range(8):
        lse_all[b] = jnp.broadcast_to(columns_ref[:, b : b + 1], (128, 128))
        delta_all[b] = jnp.broadcast_to(columns_ref[:, 8 + b : 9 + b], (128, 128))
    slot = jnp.int32(0)
    for b in range(8):
        for r in range(8):
            word = words_s[b, r]
            slots[slot] = word
            slot = slot + (word >> 20)
        slots[slot] = NONE
        slot = (slot + 1) & -2
    for p in range(4 * PAIRS):
        slots[slot + p] = NO_PAIR

    def tile(word, which):
        base = pl.multiple_of(word & 4064, 32)
        return jnp.concatenate(
            [
                kv_ref[pl.ds(base + yl * 512 + zl * 256 + which * 64, 32)]
                for zl in range(2)
                for yl in range(2)
            ],
            0,
        )

    def step(group, before):
        after, begun = [], []
        for u in range(PAIRS):
            at = (group * PAIRS + u) * 2
            one, two = slots[at], slots[at + 1]
            after += [one, two]
            b = (one >> 14) & 7
            k = jnp.concatenate((tile(one, 0), tile(two, 0)), 1)
            v = jnp.concatenate((tile(one, 1), tile(two, 1)), 1)
            scores = jnp.dot(qg_ref[b * 2], k, preferred_element_type=F32) * SCALE
            weight_grad = jnp.dot(qg_ref[b * 2 + 1], v, preferred_element_type=F32)
            lse, delta = lse_all[b], delta_all[b]
            for n in range(2):
                cols = slice(n * 128, n * 128 + 128)
                weights = jnp.exp(scores[:, cols] - lse)
                score_grad = (weights * (weight_grad[:, cols] - delta) * SCALE).astype(BF16)
                if n:
                    score_grad = jnp.where((two & 31) < NONE, score_grad, jnp.zeros_like(score_grad))
                begun.append((u, cols, weights.astype(BF16), score_grad))
        for u in range(PAIRS):
            one, two = before[u * 2 : u * 2 + 2]
            b = (one >> 14) & 15
            k = jnp.concatenate((tile(one, 0), tile(two, 0)), 1)
            score_grad = held_s[u]
            dq = lax.dot_general(score_grad, k, (((1,), (1,)), ((), ())), preferred_element_type=F32)
            dk = jnp.dot(q_t[b & 7], score_grad, preferred_element_type=F32)
            dv = jnp.dot(g_t[b & 7], held_w[u], preferred_element_type=F32)
            dq_acc[b] += dq
            first, second = one & 31, two & 31
            old = [acc[n, which] for n in (first, second) for which in range(2)]
            new = [dk[:, :128], dv[:, :128], dk[:, 128:], dv[:, 128:]]
            new = [x + y for x, y in zip(old, new)]
            acc[first, 0], acc[first, 1], acc[second, 0], acc[second, 1] = new
        for u, cols, weights, score_grad in begun:
            held_w[u, :, cols] = weights
            held_s[u, :, cols] = score_grad
        return tuple(after)

    steps = ((slot >> 1) + PAIRS - 1) // PAIRS + 1
    lax.fori_loop(0, steps, step, (jnp.int32(NO_PAIR),) * (2 * PAIRS))
    for b in range(4):
        dq_own_ref[b * 128 : b * 128 + 128] = dq_acc[b]
        dq_other_ref[b * 128 : b * 128 + 128] = dq_acc[b + 4]
    for x in range(4):
        for yl in range(2):
            for yh in range(2):
                for zl in range(2):
                    for which in range(2):
                        for j in range(2):
                            local = (yh * 4 + x) * 2 + j
                            at = x * 1024 + yl * 512 + zl * 256 + yh * 128 + which * 64 + j * 32
                            feature = (zl * 2 + yl) * 32
                            part_ref[at : at + 32] = acc[local, which, feature : feature + 32].astype(BF16)


def dq_kernel(own_ref, got_ref, out_ref):
    out_ref[...] = (own_ref[...] + got_ref[...]).astype(BF16)


def sum_kernel(got_ref, mine_ref, out_ref, total):
    core = lax.axis_index("core")
    for t in range(4):
        value = got_ref[0, t].astype(F32)
        for chip in range(1, 32):
            value = value + got_ref[chip, t].astype(F32)
        total[t] = value
    for t in range(4):
        mine_ref[t] = total[t, pl.ds(pl.multiple_of(core * 16, 16), 16)]
        out_ref[t] = total[t, pl.ds(pl.multiple_of(16 - core * 16, 16), 16)]


def last_kernel(mine_ref, got_ref, kv_out):
    core = lax.axis_index("core")
    for which in range(2):
        for j in range(2):
            own, got = mine_ref[which * 2 + j], got_ref[which * 2 + j]
            kv_out[which, :, j * 128 : j * 128 + 128] = jnp.where(core == 0, own, got)
            kv_out[which, :, 256 + j * 128 : 384 + j * 128] = jnp.where(core == 0, got, own)


def shards(queries, outputs, out_grad, keys_values, row_lse, collide):
    swap = [(0, 1), (1, 0)]
    struct = jax.ShapeDtypeStruct
    kv = keys_values.transpose(0, 2, 1)
    got_kv = lax.ppermute(kv, "core", swap)
    own_kv = call(stage_kernel, struct((2, 16, 512), BF16), [HBM], [pltpu.SemaphoreType.DMA], name="stage")(kv)
    spread = call(spread_kernel, struct((32, 2, 2, 32, 128), BF16), [VMEM] * 2, name="spread")(own_kv, got_kv)
    gathered = lax.all_to_all(spread.reshape(32, 128, 128), CHIPS, 0, 0)
    packed = call(
        pack_kernel, struct((ROWS, DH), BF16), [HBM] * 5,
        [
            pltpu.VMEM((512, DH), BF16),
            pltpu.VMEM((4, 128), F32),
            pltpu.VMEM((4, 8), I32),
            pltpu.VMEM((32, 128), F32),
            pltpu.SemaphoreType.DMA((5,)),
        ],
        name="pack",
    )(queries, out_grad, outputs, row_lse.reshape(4, BLOCK), collide.reshape(4, 8))
    pay = lax.ppermute(packed, "core", swap)
    ready = call(
        ready_kernel,
        (struct((16, 128, 128), BF16), struct((128, 128), F32), struct((8, 128), I32)),
        [VMEM] * 2, [pltpu.VMEM((128, 128), F32)], name="ready",
    )(packed, pay)
    part, dq_own, dq_other = call(
        main_kernel,
        (struct((4096, DH), BF16), struct((512, DH), F32), struct((512, DH), F32)),
        [VMEM] * 4,
        [pltpu.VMEM((8, 128, 128), BF16)] * 2
        + [pltpu.VMEM((8, 128, 128), F32)] * 2
        + [
            pltpu.VMEM((17, 2, 128, 128), F32),
            pltpu.VMEM((9, 128, 128), F32),
            pltpu.VMEM((PAIRS, 128, 256), BF16),
            pltpu.VMEM((PAIRS, 128, 256), BF16),
            pltpu.SMEM((8, 128), I32),
            pltpu.SMEM((64 + 16 + 4 * PAIRS,), I32),
            pltpu.SemaphoreType.DMA,
        ],
        name="attend",
        limit=16,
    )(gathered.reshape(4096, 128), *ready)
    got = lax.all_to_all(part.reshape(32, 128, 128), CHIPS, 0, 0)
    query_grad = call(dq_kernel, struct((512, DH), BF16), [VMEM] * 2, name="dq")(
        dq_own, lax.ppermute(dq_other, "core", swap)
    )
    mine, other = call(
        sum_kernel, (struct((4, 16, 128), F32),) * 2, [VMEM], [pltpu.VMEM((4, 32, 128), F32)], name="total",
    )(got.reshape(32, 4, 32, 128))
    kv_grad = call(last_kernel, struct((2, 16, 512), F32), [VMEM] * 2, name="last")(
        mine, lax.ppermute(other, "core", swap)
    )
    return query_grad, kv_grad.transpose(0, 2, 1)


def solution(mesh):
    fine = Mesh(
        mesh.devices.reshape(2, 4, KVH, 2, 2, 2), ("yh", "x", "group", "zl", "yl", "core")
    )
    ctx, head = ("yh", "x"), ("group", "zl", "yl", "core")
    placed = (
        P(ctx, head), P(ctx, head), P(ctx, head), P(None, ctx, head), P(head, ctx), P(head, ctx, None),
    )
    return jax.shard_map(
        shards, mesh=fine, in_specs=placed, out_specs=(P(ctx, head), P(None, ctx, head)),
        check_vma=False,
    )
```

time: 71.8 us -> 65.6 us (0.914)
  blocking collectives: 39.6 us -> 0 us
  waiting for transfers between devices: 2.54 us -> 25.8 us
  starting transfers between devices: 13.6 us -> 28 us
  local copies, waits for them, and re-layouts: 4.16 us -> 1.4 us
  Pallas kernels: 10.9 us -> 9.5 us
    all_to_all x2 -> x0, blocking collectives: 39.6 us -> none  [the longest x1 20.4 us: shards(): gathered = lax.all_to_all(spread.reshape(32, 128, 128), CHIPS, 0, 0)]
    all_to_all x0 -> x2, waiting for transfers between devices: none -> 24.2 us  [the longest x1 12.3 us: shards(): got = lax.all_to_all(part.reshape(32, 128, 128), CHIPS, 0, 0)]
    ppermute x1 -> x3, starting transfers between devices: 4.83 us -> 17.2 us  [the longest x1 8.75 us: shards(): got_kv = lax.ppermute(kv, 'core', swap)]
    all_to_all x0 -> x2, starting transfers between devices: none -> 8.57 us  [the longest x1 4.5 us: shards(): got = lax.all_to_all(part.reshape(32, 128, 128), CHIPS, 0, 0)]
    ppermute x1, starting transfers between devices: 8.74 us -> 2.26 us  [shards(): pay = lax.ppermute(packed, 'core', swap)]
    unnamed x14 -> x12, local copies, waits for them, and re-layouts: 4.16 us -> 1.4 us
    pallas_call x5 -> x8, Pallas kernels: 10.9 us -> 9.5 us  [the longest x1 5.93 us: shards(): call(main_kernel, (struct((4096, DH), BF16), struct((512, DH), F32), stru...]
    ppermute x1 -> x3, waiting for transfers between devices: 1.19 us -> 0.41 us  [the longest x1 0.26 us: shards(): got_kv = lax.ppermute(kv, 'core', swap)]
  transfers between devices with their start and end apart: 2 -> 6, of which waited for: 2 -> 5; matrix products, arithmetic and copies ran while one was open for 0% -> 0% of each run, Pallas kernels for 0% -> 3%
where the time goes in v2:
time: 65.6 us; the launch traced here: 65.5 us
  starting transfers between devices  28 us (43%)
  waiting for transfers between devices  25.8 us (39%)
  Pallas kernels  9.5 us (14%)
  local copies, waits for them, and re-layouts  1.4 us (2%)
  between operations  0.77 us (1%)
    all_to_all x1, waiting for transfers between devices, shards(): got = lax.all_to_all(part.reshape(32, 128, 128), CHIPS, 0, 0)  12.3 us
    all_to_all x1, waiting for transfers between devices, shards(): gathered = lax.all_to_all(spread.reshape(32, 128, 128), CHIPS, 0, 0)  12 us
    ppermute x1, starting transfers between devices, shards(): got_kv = lax.ppermute(kv, 'core', swap)  8.75 us
    pallas_call x1, Pallas kernels, shards(): call(main_kernel, (struct((4096, DH), BF16), struct((512, DH), F32), stru...  5.93 us
    ppermute x1, starting transfers between devices, shards(): lax.ppermute(other, 'core', swap)  5.13 us
    all_to_all x1, starting transfers between devices, shards(): got = lax.all_to_all(part.reshape(32, 128, 128), CHIPS, 0, 0)  4.5 us
    all_to_all x1, starting transfers between devices, shards(): gathered = lax.all_to_all(spread.reshape(32, 128, 128), CHIPS, 0, 0)  4.07 us
    ppermute x1, starting transfers between devices, shards(): lax.ppermute(dq_other, 'core', swap)  3.3 us
  transfers between devices with their start and end apart: 6, of which 5 were waited for; matrix products, arithmetic and copies ran while one was open for 0% of the time, Pallas kernels for 3%

profile of v2, /device:TPU:1, one launch (start us, length us, event | category | flops | bytes accessed | tf_op | source)
XLA Modules:
  0.0 65.5 jit_solution(14299664161935785627)
XLA Ops:
  0.6 8.7 %collective-permute-start = (bf16[2,16,512]{2,1,0:T(8,128)(2,1)}, bf16[2,16,512]{2,1,0:T(8,128)(2,1)S(1)}, u32[]{:S(2)}, u32[]{:S(2)}) collective-permute-start(bf16[2,16,512]{2,1,0:T(8,128)(2,1)} %bitcast.10), channel_id=1, source_target_pairs={{0,1},{1,0},{2,3},{3,2},{4,5},{5,4},{6,7},{7,6},{8,9},{9,8},{10,11... | collective-permute-start | bytes 98312 | tf_op jit(solution)/shard_map/ppermute | solution.py:234
  9.4 0.0 copy-start.3
  9.4 0.7 %copy-done.3 = bf16[2,512,16]{1,2,0:T(8,128)(2,1)S(1)} copy-done((bf16[2,512,16]{1,2,0:T(8,128)(2,1)S(1)}, bf16[2,512,16]{1,2,0:T(8,128)(2,1)}, u32[]{:S(2)}) %copy-start.3) | copy-done | bytes 32792
  10.2 0.3 collective-permute-done.got_ref
  10.4 1.2 %spread.1 = bf16[32,2,2,32,128]{4,3,2,1,0:T(8,128)(2,1)} custom-call(bf16[2,16,512]{2,1,0:T(8,128)(2,1)S(1)} %stage.1.own_ref, bf16[2,16,512]{2,1,0:T(8,128)(2,1)S(1)} %collective-permute-done.got_ref), custom_call_target="tpu_custom_call" | custom-call | tf_op jit(solution)/shard_map/spread/pallas_call | solution.py:236
  11.6 0.0 copy-start
  11.7 0.0 copy-start.1
  11.7 0.0 copy-start.2
  11.7 0.0 copy-start.5
  11.7 4.1 %all-to-all-start = ((bf16[32,128,128]{2,1,0:T(8,128)(2,1)}), bf16[32,128,128]{2,1,0:T(8,128)(2,1)S(1)}, u32[]{:S(2)}, u32[]{:S(2)}) async-start(bf16[32,128,128]{2,1,0:T(8,128)(2,1)} %bitcast.1), calls=%async_computation | async-start | bytes 2097152 | tf_op jit(solution)/shard_map/all_to_all | solution.py:237
  15.7 0.0 copy-start.4
  15.8 0.0 copy-done
  15.8 0.0 copy-done.1
  15.8 0.0 copy-done.2
  15.8 0.0 copy-done.5
  15.8 0.6 copy-done.4
  16.4 0.7 %pack.1.own_ref = bf16[1056,128]{1,0:T(8,128)(2,1)S(1)} custom-call(bf16[512,128]{1,0:T(8,128)(2,1)S(1)} %copy-done, bf16[512,128]{1,0:T(8,128)(2,1)S(1)} %copy-done.1, bf16[512,128]{1,0:T(8,128)(2,1)S(1)} %copy-done.2, f32[4,128]{1,0:T(4,128)S(1)} %bitcast.12, s32[4,8]{1,0:T(4,128)S(1)} %bitcast.13), custom_call_target="tpu_custom_call" | custom-call | tf_op jit(solution)/shard_map/pack/pallas_call | solution.py:238
  17.2 2.3 %collective-permute-start.1 = (bf16[1056,128]{1,0:T(8,128)(2,1)S(1)}, bf16[1056,128]{1,0:T(8,128)(2,1)S(1)}, u32[]{:S(2)}, u32[]{:S(2)}) collective-permute-start(bf16[1056,128]{1,0:T(8,128)(2,1)S(1)} %pack.1.own_ref), channel_id=1, source_target_pairs={{0,1},{1,0},{2,3},{3,2},{4,5},{5,4},{6,7},{7,6},{8,9},{9,8},{10,11... | collective-permute-start | bytes 811016 | tf_op jit(solution)/shard_map/ppermute | solution.py:249
  19.4 1.2 %collective-permute-done.1.got_ref = bf16[1056,128]{1,0:T(8,128)(2,1)S(1)} collective-permute-done((bf16[1056,128]{1,0:T(8,128)(2,1)S(1)}, bf16[1056,128]{1,0:T(8,128)(2,1)S(1)}, u32[]{:S(2)}, u32[]{:S(2)}) %collective-permute-start.1) | collective-permute-done | bytes 270368 | tf_op jit(solution)/shard_map/ppermute | solution.py:249
  20.6 0.1 ready.1
  20.8 12.0 %all-to-all-done = bf16[32,128,128]{2,1,0:T(8,128)(2,1)S(1)} async-done(((bf16[32,128,128]{2,1,0:T(8,128)(2,1)}), bf16[32,128,128]{2,1,0:T(8,128)(2,1)S(1)}, u32[]{:S(2)}, u32[]{:S(2)}) %all-to-all-start) | async-done | bytes 1048608 | tf_op jit(solution)/shard_map/all_to_all | solution.py:237
  32.7 5.9 %attend.1 = (bf16[4096,128]{1,0:T(8,128)(2,1)}, f32[512,128]{1,0:T(8,128)S(1)}, f32[512,128]{1,0:T(8,128)S(1)}) custom-call(bf16[4096,128]{1,0:T(8,128)(2,1)S(1)} %bitcast.8, bf16[16,128,128]{2,1,0:T(8,128)(2,1)S(1)} %get-tuple-element.10.qg_ref, f32[128,128]{1,0:T(8,128)S(1)} %get-tuple-element.11.columns_ref, s32[8,128]{1,0:T(8,128)S(1)} %get-tuple-element.12.words_ref), custom_call_target="tpu_custom_call" | custom-call | tf_op jit(solution)/shard_map/attend/pallas_call | solution.py:255
  38.6 4.5 %all-to-all-start.1 = ((bf16[32,128,128]{2,1,0:T(8,128)(2,1)}), bf16[32,128,128]{2,1,0:T(8,128)(2,1)S(1)}, u32[]{:S(2)}, u32[]{:S(2)}) async-start(bf16[32,128,128]{2,1,0:T(8,128)(2,1)} %bitcast.5), calls=%async_computation.1 | async-start | bytes 2097152 | tf_op jit(solution)/shard_map/all_to_all | solution.py:273
  43.2 3.3 %collective-permute-start.2 = (f32[512,128]{1,0:T(8,128)S(1)}, f32[512,128]{1,0:T(8,128)S(1)}, u32[]{:S(2)}, u32[]{:S(2)}) collective-permute-start(f32[512,128]{1,0:T(8,128)S(1)} %get-tuple-element.14), channel_id=1, source_target_pairs={{0,1},{1,0},{2,3},{3,2},{4,5},{5,4},{6,7},{7,6},{8,9},{9,8},{10,11... | collective-permute-start | bytes 786440 | tf_op jit(solution)/shard_map/ppermute | solution.py:275
  46.5 12.3 %all-to-all-done.1 = bf16[32,128,128]{2,1,0:T(8,128)(2,1)S(1)} async-done(((bf16[32,128,128]{2,1,0:T(8,128)(2,1)}), bf16[32,128,128]{2,1,0:T(8,128)(2,1)S(1)}, u32[]{:S(2)}, u32[]{:S(2)}) %all-to-all-start.1) | async-done | bytes 1048608 | tf_op jit(solution)/shard_map/all_to_all | solution.py:273
  58.7 0.1 total.1
  58.9 5.1 %collective-permute-start.3 = (f32[4,16,128]{2,1,0:T(8,128)S(1)}, f32[4,16,128]{2,1,0:T(8,128)S(1)}, u32[]{:S(2)}, u32[]{:S(2)}) collective-permute-start(f32[4,16,128]{2,1,0:T(8,128)S(1)} %get-tuple-element.17), channel_id=1, source_target_pairs={{0,1},{1,0},{2,3},{3,2},{4,5},{5,4},{6,7},{7,6},{8,9},{9,8},{10,11... | collective-permute-start | bytes 98312 | tf_op jit(solution)/shard_map/ppermute | solution.py:281
  64.0 0.0 collective-permute-done.2.got_ref
  64.0 0.7 %dq.1 = bf16[512,128]{1,0:T(8,128)(2,1)} custom-call(f32[512,128]{1,0:T(8,128)S(1)} %get-tuple-element.13.own_ref, f32[512,128]{1,0:T(8,128)S(1)} %collective-permute-done.2.got_ref), custom_call_target="tpu_custom_call" | custom-call | tf_op jit(solution)/shard_map/dq/pallas_call | solution.py:274
  64.7 0.1 collective-permute-done.3.got_ref
  64.8 0.6 last.1
  (1 shorter events, 0.0 us)
Async XLA Ops:
  0.6 9.8 %collective-permute-start = (bf16[2,16,512]{2,1,0:T(8,128)(2,1)}, bf16[2,16,512]{2,1,0:T(8,128)(2,1)S(1)}, u32[]{:S(2)}, u32[]{:S(2)}) collective-permute-start(bf16[2,16,512]{2,1,0:T(8,128)(2,1)} %bitcast.10), channel_id=1, source_target_pairs={{0,1},{1,0},{2,3},{3,2},{4,5},{5,4},{6,7},{7,6},{8,9},{9,8},{10,11... | collective-permute-start | bytes 98312 | tf_op jit(solution)/shard_map/ppermute | solution.py:234
  9.4 0.8 %copy-start.3 = (bf16[2,512,16]{1,2,0:T(8,128)(2,1)S(1)}, bf16[2,512,16]{1,2,0:T(8,128)(2,1)}, u32[]{:S(2)}) copy-start(bf16[2,512,16]{1,2,0:T(8,128)(2,1)} %param.9) | copy-start | bytes 98308
  11.6 4.1 %copy-start = (bf16[512,128]{1,0:T(8,128)(2,1)S(1)}, bf16[512,128]{1,0:T(8,128)(2,1)}, u32[]{:S(2)}) copy-start(bf16[512,128]{1,0:T(8,128)(2,1)} %q_ref.1) | copy-start | bytes 393220
  11.7 4.1 %copy-start.1 = (bf16[512,128]{1,0:T(8,128)(2,1)S(1)}, bf16[512,128]{1,0:T(8,128)(2,1)}, u32[]{:S(2)}) copy-start(bf16[512,128]{1,0:T(8,128)(2,1)} %g_ref.1) | copy-start | bytes 393220
  11.7 4.1 %copy-start.2 = (bf16[512,128]{1,0:T(8,128)(2,1)S(1)}, bf16[512,128]{1,0:T(8,128)(2,1)}, u32[]{:S(2)}) copy-start(bf16[512,128]{1,0:T(8,128)(2,1)} %o_ref.1) | copy-start | bytes 393220
  11.7 4.1 %copy-start.5 = (s32[1,4,8]{2,1,0:T(4,128)S(1)}, s32[1,4,8]{2,1,0:T(4,128)}, u32[]{:S(2)}) copy-start(s32[1,4,8]{2,1,0:T(4,128)} %param.11) | copy-start | bytes 388
  11.7 21.0 %all-to-all-start = ((bf16[32,128,128]{2,1,0:T(8,128)(2,1)}), bf16[32,128,128]{2,1,0:T(8,128)(2,1)S(1)}, u32[]{:S(2)}, u32[]{:S(2)}) async-start(bf16[32,128,128]{2,1,0:T(8,128)(2,1)} %bitcast.1), calls=%async_computation | async-start | bytes 2097152 | tf_op jit(solution)/shard_map/all_to_all | solution.py:237
  15.7 0.7 %copy-start.4 = (f32[1,512]{1,0:T(1,128)S(1)}, f32[1,512]{1,0:T(1,128)}, u32[]{:S(2)}) copy-start(f32[1,512]{1,0:T(1,128)} %param.10) | copy-start | bytes 6148
  17.2 3.4 %collective-permute-start.1 = (bf16[1056,128]{1,0:T(8,128)(2,1)S(1)}, bf16[1056,128]{1,0:T(8,128)(2,1)S(1)}, u32[]{:S(2)}, u32[]{:S(2)}) collective-permute-start(bf16[1056,128]{1,0:T(8,128)(2,1)S(1)} %pack.1.own_ref), channel_id=1, source_target_pairs={{0,1},{1,0},{2,3},{3,2},{4,5},{5,4},{6,7},{7,6},{8,9},{9,8},{10,11... | collective-permute-start | bytes 811016 | tf_op jit(solution)/shard_map/ppermute | solution.py:249
  38.6 20.1 %all-to-all-start.1 = ((bf16[32,128,128]{2,1,0:T(8,128)(2,1)}), bf16[32,128,128]{2,1,0:T(8,128)(2,1)S(1)}, u32[]{:S(2)}, u32[]{:S(2)}) async-start(bf16[32,128,128]{2,1,0:T(8,128)(2,1)} %bitcast.5), calls=%async_computation.1 | async-start | bytes 2097152 | tf_op jit(solution)/shard_map/all_to_all | solution.py:273
  43.2 20.8 %collective-permute-start.2 = (f32[512,128]{1,0:T(8,128)S(1)}, f32[512,128]{1,0:T(8,128)S(1)}, u32[]{:S(2)}, u32[]{:S(2)}) collective-permute-start(f32[512,128]{1,0:T(8,128)S(1)} %get-tuple-element.14), channel_id=1, source_target_pairs={{0,1},{1,0},{2,3},{3,2},{4,5},{5,4},{6,7},{7,6},{8,9},{9,8},{10,11... | collective-permute-start | bytes 786440 | tf_op jit(solution)/shard_map/ppermute | solution.py:275
  58.9 6.0 %collective-permute-start.3 = (f32[4,16,128]{2,1,0:T(8,128)S(1)}, f32[4,16,128]{2,1,0:T(8,128)S(1)}, u32[]{:S(2)}, u32[]{:S(2)}) collective-permute-start(f32[4,16,128]{2,1,0:T(8,128)S(1)} %get-tuple-element.17), channel_id=1, source_target_pairs={{0,1},{1,0},{2,3},{3,2},{4,5},{5,4},{6,7},{7,6},{8,9},{9,8},{10,11... | collective-permute-start | bytes 98312 | tf_op jit(solution)/shard_map/ppermute | solution.py:281

commit v3 on v2

--- a/solution.py
+++ b/solution.py
@@ -12,7 +12,8 @@
 BF16 = jnp.bfloat16
 I32 = jnp.int32
 SCALE = DH ** -0.5
-PAIRS = 2
+PAIRS = 6
+LOG2E = 1.4426950408889634
 CHIPS = ("x", "yl", "zl", "yh")
 HBM = pl.BlockSpec(memory_space=pltpu.MemorySpace.HBM)
 VMEM = pl.BlockSpec(memory_space=pltpu.VMEM)
@@ -90,18 +91,20 @@
 NO_PAIR = NONE + (8 << 14)
 
 
-def ready_kernel(own_ref, got_ref, qg_ref, columns_ref, words_ref, table):
+def ready_kernel(own_ref, got_ref, operands_ref, columns_ref, words_ref, table):
     core = lax.axis_index("core")
     table[...] = jnp.zeros((128, 128), F32)
     blocks = []
     for n, ref in enumerate((own_ref, got_ref)):
         small = ref[ROW_S:ROWS].astype(F32)
-        table[n * 4 : n * 4 + 4] = small[0:4] + small[4:8] + small[8:12]
+        table[n * 4 : n * 4 + 4] = (small[0:4] + small[4:8] + small[8:12]) * LOG2E
         table[8 + n * 4 : 12 + n * 4] = small[12:16] + small[16:20] + small[20:24]
         blocks.append(small[24:28])
         for b in range(4):
-            qg_ref[n * 8 + b * 2] = ref[ROW_Q + b * 128 : ROW_Q + b * 128 + 128]
-            qg_ref[n * 8 + b * 2 + 1] = ref[ROW_G + b * 128 : ROW_G + b * 128 + 128]
+            for which, row in enumerate((ROW_Q, ROW_G)):
+                value = ref[row + b * 128 : row + b * 128 + 128]
+                operands_ref[n * 4 + b, which] = value
+                operands_ref[n * 4 + b, 2 + which] = value.T
     columns_ref[...] = table[...].T
     block = jnp.concatenate(blocks, 0).astype(I32)
     row = lax.broadcasted_iota(I32, block.shape, 0)
@@ -111,20 +114,17 @@
 
 
 def main_kernel(
-    kv_ref, qg_ref, columns_ref, words_ref, part_ref, dq_own_ref, dq_other_ref,
-    q_t, g_t, lse_all, delta_all, acc, dq_acc, held_w, held_s, words_s, slots, sem,
+    kv_ref, operands_ref, columns_ref, words_ref, part_ref, dq_own_ref, dq_other_ref,
+    lse_all, delta_all, acc, dq_acc, words_s, slots, sem,
 ):
     copy = pltpu.make_async_copy(words_ref, words_s, sem)
     copy.start()
     for b in range(8):
-        q_t[b] = qg_ref[b * 2].T
-        g_t[b] = qg_ref[b * 2 + 1].T
+        lse_all[b] = jnp.broadcast_to(columns_ref[:, b : b + 1], (128, 128))
+        delta_all[b] = jnp.broadcast_to(columns_ref[:, 8 + b : 9 + b], (128, 128))
     copy.wait()
     acc[...] = jnp.zeros(acc.shape, F32)
     dq_acc[...] = jnp.zeros(dq_acc.shape, F32)
-    for b in range(8):
-        lse_all[b] = jnp.broadcast_to(columns_ref[:, b : b + 1], (128, 128))
-        delta_all[b] = jnp.broadcast_to(columns_ref[:, 8 + b : 9 + b], (128, 128))
     slot = jnp.int32(0)
     for b in range(8):
         for r in range(8):
@@ -133,60 +133,54 @@
             slot = slot + (word >> 20)
         slots[slot] = NONE
         slot = (slot + 1) & -2
-    for p in range(4 * PAIRS):
+    for p in range(2 * PAIRS):
         slots[slot + p] = NO_PAIR
 
-    def tile(word, which):
-        base = pl.multiple_of(word & 4064, 32)
-        return jnp.concatenate(
-            [
+    def tiles(words, which):
+        columns = []
+        for word in words:
+            base = pl.multiple_of(word & 4064, 32)
+            rows = [
                 kv_ref[pl.ds(base + yl * 512 + zl * 256 + which * 64, 32)]
                 for zl in range(2)
                 for yl in range(2)
-            ],
-            0,
-        )
-
-    def step(group, before):
-        after, begun = [], []
+            ]
+            columns.append(jnp.concatenate(rows, 0))
+        return jnp.concatenate(columns, 1)
+
+    def step(group, carry):
+        begun = []
         for u in range(PAIRS):
             at = (group * PAIRS + u) * 2
-            one, two = slots[at], slots[at + 1]
-            after += [one, two]
-            b = (one >> 14) & 7
-            k = jnp.concatenate((tile(one, 0), tile(two, 0)), 1)
-            v = jnp.concatenate((tile(one, 1), tile(two, 1)), 1)
-            scores = jnp.dot(qg_ref[b * 2], k, preferred_element_type=F32) * SCALE
-            weight_grad = jnp.dot(qg_ref[b * 2 + 1], v, preferred_element_type=F32)
+            words = slots[at], slots[at + 1]
+            b = (words[0] >> 14) & 7
+            k = tiles(words, 0)
+            scores = jnp.dot(operands_ref[b, 0], k, preferred_element_type=F32)
+            weight_grad = jnp.dot(operands_ref[b, 1], tiles(words, 1), preferred_element_type=F32)
             lse, delta = lse_all[b], delta_all[b]
+            weights, score_grads = [], []
             for n in range(2):
                 cols = slice(n * 128, n * 128 + 128)
-                weights = jnp.exp(scores[:, cols] - lse)
-                score_grad = (weights * (weight_grad[:, cols] - delta) * SCALE).astype(BF16)
+                weight = jnp.exp2(scores[:, cols] * (SCALE * LOG2E) - lse)
+                score_grad = (weight * (weight_grad[:, cols] - delta) * SCALE).astype(BF16)
                 if n:
-                    score_grad = jnp.where((two & 31) < NONE, score_grad, jnp.zeros_like(score_grad))
-                begun.append((u, cols, weights.astype(BF16), score_grad))
-        for u in range(PAIRS):
-            one, two = before[u * 2 : u * 2 + 2]
-            b = (one >> 14) & 15
-            k = jnp.concatenate((tile(one, 0), tile(two, 0)), 1)
-            score_grad = held_s[u]
+                    score_grad = jnp.where((words[1] & 31) < NONE, score_grad, jnp.zeros_like(score_grad))
+                weights.append(weight.astype(BF16))
+                score_grads.append(score_grad)
+            begun.append((words, b, k, jnp.concatenate(weights, 1), jnp.concatenate(score_grads, 1)))
+        for words, b, k, weights, score_grad in begun:
             dq = lax.dot_general(score_grad, k, (((1,), (1,)), ((), ())), preferred_element_type=F32)
-            dk = jnp.dot(q_t[b & 7], score_grad, preferred_element_type=F32)
-            dv = jnp.dot(g_t[b & 7], held_w[u], preferred_element_type=F32)
-            dq_acc[b] += dq
-            first, second = one & 31, two & 31
+            dk = jnp.dot(operands_ref[b, 2], score_grad, preferred_element_type=F32)
+            dv = jnp.dot(operands_ref[b, 3], weights, preferred_element_type=F32)
+            dq_acc[(words[0] >> 14) & 15] += dq
+            first, second = words[0] & 31, words[1] & 31
             old = [acc[n, which] for n in (first, second) for which in range(2)]
             new = [dk[:, :128], dv[:, :128], dk[:, 128:], dv[:, 128:]]
             new = [x + y for x, y in zip(old, new)]
             acc[first, 0], acc[first, 1], acc[second, 0], acc[second, 1] = new
-        for u, cols, weights, score_grad in begun:
-            held_w[u, :, cols] = weights
-            held_s[u, :, cols] = score_grad
-        return tuple(after)
-
-    steps = ((slot >> 1) + PAIRS - 1) // PAIRS + 1
-    lax.fori_loop(0, steps, step, (jnp.int32(NO_PAIR),) * (2 * PAIRS))
+        return carry
+
+    lax.fori_loop(0, ((slot >> 1) + PAIRS - 1) // PAIRS, step, 0)
     for b in range(4):
         dq_own_ref[b * 128 : b * 128 + 128] = dq_acc[b]
         dq_other_ref[b * 128 : b * 128 + 128] = dq_acc[b + 4]
@@ -249,22 +243,20 @@
     pay = lax.ppermute(packed, "core", swap)
     ready = call(
         ready_kernel,
-        (struct((16, 128, 128), BF16), struct((128, 128), F32), struct((8, 128), I32)),
+        (struct((8, 4, 128, 128), BF16), struct((128, 128), F32), struct((8, 128), I32)),
         [VMEM] * 2, [pltpu.VMEM((128, 128), F32)], name="ready",
     )(packed, pay)
     part, dq_own, dq_other = call(
         main_kernel,
         (struct((4096, DH), BF16), struct((512, DH), F32), struct((512, DH), F32)),
         [VMEM] * 4,
-        [pltpu.VMEM((8, 128, 128), BF16)] * 2
-        + [pltpu.VMEM((8, 128, 128), F32)] * 2
-        + [
+        [
+            pltpu.VMEM((8, 128, 128), F32),
+            pltpu.VMEM((8, 128, 128), F32),
             pltpu.VMEM((17, 2, 128, 128), F32),
             pltpu.VMEM((9, 128, 128), F32),
-            pltpu.VMEM((PAIRS, 128, 256), BF16),
-            pltpu.VMEM((PAIRS, 128, 256), BF16),
             pltpu.SMEM((8, 128), I32),
-            pltpu.SMEM((64 + 16 + 4 * PAIRS,), I32),
+            pltpu.SMEM((64 + 16 + 2 * PAIRS,), I32),
             pltpu.SemaphoreType.DMA,
         ],
         name="attend",

time: 65.6 us -> 64.1 us (0.977)
  waiting for transfers between devices: 25.8 us -> 24.6 us
  Pallas kernels: 9.5 us -> 8.38 us
    pallas_call x1, Pallas kernels: 5.93 us -> 4.68 us  [shards(): call(main_kernel, (struct((4096, DH), BF16), struct((512, DH), F32), stru...]
    all_to_all x1, waiting for transfers between devices: 12.3 us -> 11.2 us  [shards(): got = lax.all_to_all(part.reshape(32, 128, 128), CHIPS, 0, 0)]
where the time goes in v3:
time: 64.1 us; the launch traced here: 63.7 us
  starting transfers between devices  28.6 us (45%)
  waiting for transfers between devices  24.6 us (38%)
  Pallas kernels  8.38 us (13%)
  local copies, waits for them, and re-layouts  1.4 us (2%)
  between operations  0.77 us (1%)
    all_to_all x1, waiting for transfers between devices, shards(): gathered = lax.all_to_all(spread.reshape(32, 128, 128), CHIPS, 0, 0)  11.8 us
    all_to_all x1, waiting for transfers between devices, shards(): got = lax.all_to_all(part.reshape(32, 128, 128), CHIPS, 0, 0)  11.2 us
    ppermute x1, starting transfers between devices, shards(): got_kv = lax.ppermute(kv, 'core', swap)  8.75 us
    ppermute x1, starting transfers between devices, shards(): lax.ppermute(other, 'core', swap)  5.71 us
    pallas_call x1, Pallas kernels, shards(): call(main_kernel, (struct((4096, DH), BF16), struct((512, DH), F32), stru...  4.68 us
    all_to_all x1, starting transfers between devices, shards(): gathered = lax.all_to_all(spread.reshape(32, 128, 128), CHIPS, 0, 0)  4.07 us
    all_to_all x1, starting transfers between devices, shards(): got = lax.all_to_all(part.reshape(32, 128, 128), CHIPS, 0, 0)  3.94 us
    ppermute x1, starting transfers between devices, shards(): lax.ppermute(dq_other, 'core', swap)  3.83 us
  transfers between devices with their start and end apart: 6, of which 5 were waited for; matrix products, arithmetic and copies ran while one was open for 0% of the time, Pallas kernels for 3%

profile of v3, /device:TPU:1, one launch (start us, length us, event | category | flops | bytes accessed | tf_op | source)
XLA Modules:
  0.0 63.7 jit_solution(5522403033610890899)
XLA Ops:
  0.6 8.7 %collective-permute-start = (bf16[2,16,512]{2,1,0:T(8,128)(2,1)}, bf16[2,16,512]{2,1,0:T(8,128)(2,1)S(1)}, u32[]{:S(2)}, u32[]{:S(2)}) collective-permute-start(bf16[2,16,512]{2,1,0:T(8,128)(2,1)} %bitcast.10), channel_id=1, source_target_pairs={{0,1},{1,0},{2,3},{3,2},{4,5},{5,4},{6,7},{7,6},{8,9},{9,8},{10,11... | collective-permute-start | bytes 98312 | tf_op jit(solution)/shard_map/ppermute | solution.py:228
  9.4 0.0 copy-start.3
  9.4 0.7 %copy-done.3 = bf16[2,512,16]{1,2,0:T(8,128)(2,1)S(1)} copy-done((bf16[2,512,16]{1,2,0:T(8,128)(2,1)S(1)}, bf16[2,512,16]{1,2,0:T(8,128)(2,1)}, u32[]{:S(2)}) %copy-start.3) | copy-done | bytes 32792
  10.2 0.3 collective-permute-done.got_ref
  10.4 1.2 %spread.1 = bf16[32,2,2,32,128]{4,3,2,1,0:T(8,128)(2,1)} custom-call(bf16[2,16,512]{2,1,0:T(8,128)(2,1)S(1)} %stage.1.own_ref, bf16[2,16,512]{2,1,0:T(8,128)(2,1)S(1)} %collective-permute-done.got_ref), custom_call_target="tpu_custom_call" | custom-call | tf_op jit(solution)/shard_map/spread/pallas_call | solution.py:230
  11.6 0.0 copy-start
  11.7 0.0 copy-start.1
  11.7 0.0 copy-start.2
  11.7 0.0 copy-start.5
  11.7 4.1 %all-to-all-start = ((bf16[32,128,128]{2,1,0:T(8,128)(2,1)}), bf16[32,128,128]{2,1,0:T(8,128)(2,1)S(1)}, u32[]{:S(2)}, u32[]{:S(2)}) async-start(bf16[32,128,128]{2,1,0:T(8,128)(2,1)} %bitcast.1), calls=%async_computation | async-start | bytes 2097152 | tf_op jit(solution)/shard_map/all_to_all | solution.py:231
  15.7 0.0 copy-start.4
  15.8 0.0 copy-done
  15.8 0.0 copy-done.1
  15.8 0.0 copy-done.2
  15.8 0.0 copy-done.5
  15.8 0.6 copy-done.4
  16.4 0.7 %pack.1.own_ref = bf16[1056,128]{1,0:T(8,128)(2,1)S(1)} custom-call(bf16[512,128]{1,0:T(8,128)(2,1)S(1)} %copy-done, bf16[512,128]{1,0:T(8,128)(2,1)S(1)} %copy-done.1, bf16[512,128]{1,0:T(8,128)(2,1)S(1)} %copy-done.2, f32[4,128]{1,0:T(4,128)S(1)} %bitcast.12, s32[4,8]{1,0:T(4,128)S(1)} %bitcast.13), custom_call_target="tpu_custom_call" | custom-call | tf_op jit(solution)/shard_map/pack/pallas_call | solution.py:232
  17.2 2.3 %collective-permute-start.1 = (bf16[1056,128]{1,0:T(8,128)(2,1)S(1)}, bf16[1056,128]{1,0:T(8,128)(2,1)S(1)}, u32[]{:S(2)}, u32[]{:S(2)}) collective-permute-start(bf16[1056,128]{1,0:T(8,128)(2,1)S(1)} %pack.1.own_ref), channel_id=1, source_target_pairs={{0,1},{1,0},{2,3},{3,2},{4,5},{5,4},{6,7},{7,6},{8,9},{9,8},{10,11... | collective-permute-start | bytes 811016 | tf_op jit(solution)/shard_map/ppermute | solution.py:243
  19.4 1.2 %collective-permute-done.1.got_ref = bf16[1056,128]{1,0:T(8,128)(2,1)S(1)} collective-permute-done((bf16[1056,128]{1,0:T(8,128)(2,1)S(1)}, bf16[1056,128]{1,0:T(8,128)(2,1)S(1)}, u32[]{:S(2)}, u32[]{:S(2)}) %collective-permute-start.1) | collective-permute-done | bytes 270368 | tf_op jit(solution)/shard_map/ppermute | solution.py:243
  20.6 0.3 ready.1
  20.9 11.8 %all-to-all-done = bf16[32,128,128]{2,1,0:T(8,128)(2,1)S(1)} async-done(((bf16[32,128,128]{2,1,0:T(8,128)(2,1)}), bf16[32,128,128]{2,1,0:T(8,128)(2,1)S(1)}, u32[]{:S(2)}, u32[]{:S(2)}) %all-to-all-start) | async-done | bytes 1048608 | tf_op jit(solution)/shard_map/all_to_all | solution.py:231
  32.7 4.7 %attend.1 = (bf16[4096,128]{1,0:T(8,128)(2,1)}, f32[512,128]{1,0:T(8,128)S(1)}, f32[512,128]{1,0:T(8,128)S(1)}) custom-call(bf16[4096,128]{1,0:T(8,128)(2,1)S(1)} %bitcast.8, bf16[8,4,128,128]{3,2,1,0:T(8,128)(2,1)S(1)} %get-tuple-element.10.operands_ref, f32[128,128]{1,0:T(8,128)S(1)} %get-tuple-element.11.columns_ref, s32[8,128]{1,0:T(8,128)S(1)} %get-tuple-element.12.words_ref), custom_call_target="tpu_custom_call" | custom-call | tf_op jit(solution)/shard_map/attend/pallas_call | solution.py:249
  37.4 3.9 %all-to-all-start.1 = ((bf16[32,128,128]{2,1,0:T(8,128)(2,1)}), bf16[32,128,128]{2,1,0:T(8,128)(2,1)S(1)}, u32[]{:S(2)}, u32[]{:S(2)}) async-start(bf16[32,128,128]{2,1,0:T(8,128)(2,1)} %bitcast.5), calls=%async_computation.1 | async-start | bytes 2097152 | tf_op jit(solution)/shard_map/all_to_all | solution.py:265
  41.3 3.8 %collective-permute-start.2 = (f32[512,128]{1,0:T(8,128)S(1)}, f32[512,128]{1,0:T(8,128)S(1)}, u32[]{:S(2)}, u32[]{:S(2)}) collective-permute-start(f32[512,128]{1,0:T(8,128)S(1)} %get-tuple-element.14), channel_id=1, source_target_pairs={{0,1},{1,0},{2,3},{3,2},{4,5},{5,4},{6,7},{7,6},{8,9},{9,8},{10,11... | collective-permute-start | bytes 786440 | tf_op jit(solution)/shard_map/ppermute | solution.py:267
  45.2 11.2 %all-to-all-done.1 = bf16[32,128,128]{2,1,0:T(8,128)(2,1)S(1)} async-done(((bf16[32,128,128]{2,1,0:T(8,128)(2,1)}), bf16[32,128,128]{2,1,0:T(8,128)(2,1)S(1)}, u32[]{:S(2)}, u32[]{:S(2)}) %all-to-all-start.1) | async-done | bytes 1048608 | tf_op jit(solution)/shard_map/all_to_all | solution.py:265
  56.4 0.1 total.1
  56.5 5.7 %collective-permute-start.3 = (f32[4,16,128]{2,1,0:T(8,128)S(1)}, f32[4,16,128]{2,1,0:T(8,128)S(1)}, u32[]{:S(2)}, u32[]{:S(2)}) collective-permute-start(f32[4,16,128]{2,1,0:T(8,128)S(1)} %get-tuple-element.17), channel_id=1, source_target_pairs={{0,1},{1,0},{2,3},{3,2},{4,5},{5,4},{6,7},{7,6},{8,9},{9,8},{10,11... | collective-permute-start | bytes 98312 | tf_op jit(solution)/shard_map/ppermute | solution.py:273
  62.2 0.0 collective-permute-done.2.got_ref
  62.2 0.7 %dq.1 = bf16[512,128]{1,0:T(8,128)(2,1)} custom-call(f32[512,128]{1,0:T(8,128)S(1)} %get-tuple-element.13.own_ref, f32[512,128]{1,0:T(8,128)S(1)} %collective-permute-done.2.got_ref), custom_call_target="tpu_custom_call" | custom-call | tf_op jit(solution)/shard_map/dq/pallas_call | solution.py:266
  62.9 0.1 collective-permute-done.3.got_ref
  63.1 0.6 %last.1 = f32[2,16,512]{2,1,0:T(8,128)} custom-call(f32[4,16,128]{2,1,0:T(8,128)S(1)} %get-tuple-element.16.mine_ref, f32[4,16,128]{2,1,0:T(8,128)S(1)} %collective-permute-done.3.got_ref), custom_call_target="tpu_custom_call" | custom-call | tf_op jit(solution)/shard_map/last/pallas_call | solution.py:272
  (1 shorter events, 0.0 us)
Async XLA Ops:
  0.6 9.8 %collective-permute-start = (bf16[2,16,512]{2,1,0:T(8,128)(2,1)}, bf16[2,16,512]{2,1,0:T(8,128)(2,1)S(1)}, u32[]{:S(2)}, u32[]{:S(2)}) collective-permute-start(bf16[2,16,512]{2,1,0:T(8,128)(2,1)} %bitcast.10), channel_id=1, source_target_pairs={{0,1},{1,0},{2,3},{3,2},{4,5},{5,4},{6,7},{7,6},{8,9},{9,8},{10,11... | collective-permute-start | bytes 98312 | tf_op jit(solution)/shard_map/ppermute | solution.py:228
  9.4 0.8 %copy-start.3 = (bf16[2,512,16]{1,2,0:T(8,128)(2,1)S(1)}, bf16[2,512,16]{1,2,0:T(8,128)(2,1)}, u32[]{:S(2)}) copy-start(bf16[2,512,16]{1,2,0:T(8,128)(2,1)} %param.9) | copy-start | bytes 98308
  11.6 4.1 %copy-start = (bf16[512,128]{1,0:T(8,128)(2,1)S(1)}, bf16[512,128]{1,0:T(8,128)(2,1)}, u32[]{:S(2)}) copy-start(bf16[512,128]{1,0:T(8,128)(2,1)} %q_ref.1) | copy-start | bytes 393220
  11.7 4.1 %copy-start.1 = (bf16[512,128]{1,0:T(8,128)(2,1)S(1)}, bf16[512,128]{1,0:T(8,128)(2,1)}, u32[]{:S(2)}) copy-start(bf16[512,128]{1,0:T(8,128)(2,1)} %g_ref.1) | copy-start | bytes 393220
  11.7 4.1 %copy-start.2 = (bf16[512,128]{1,0:T(8,128)(2,1)S(1)}, bf16[512,128]{1,0:T(8,128)(2,1)}, u32[]{:S(2)}) copy-start(bf16[512,128]{1,0:T(8,128)(2,1)} %o_ref.1) | copy-start | bytes 393220
  11.7 4.1 %copy-start.5 = (s32[1,4,8]{2,1,0:T(4,128)S(1)}, s32[1,4,8]{2,1,0:T(4,128)}, u32[]{:S(2)}) copy-start(s32[1,4,8]{2,1,0:T(4,128)} %param.11) | copy-start | bytes 388
  11.7 21.0 %all-to-all-start = ((bf16[32,128,128]{2,1,0:T(8,128)(2,1)}), bf16[32,128,128]{2,1,0:T(8,128)(2,1)S(1)}, u32[]{:S(2)}, u32[]{:S(2)}) async-start(bf16[32,128,128]{2,1,0:T(8,128)(2,1)} %bitcast.1), calls=%async_computation | async-start | bytes 2097152 | tf_op jit(solution)/shard_map/all_to_all | solution.py:231
  15.7 0.7 %copy-start.4 = (f32[1,512]{1,0:T(1,128)S(1)}, f32[1,512]{1,0:T(1,128)}, u32[]{:S(2)}) copy-start(f32[1,512]{1,0:T(1,128)} %param.10) | copy-start | bytes 6148
  17.2 3.4 %collective-permute-start.1 = (bf16[1056,128]{1,0:T(8,128)(2,1)S(1)}, bf16[1056,128]{1,0:T(8,128)(2,1)S(1)}, u32[]{:S(2)}, u32[]{:S(2)}) collective-permute-start(bf16[1056,128]{1,0:T(8,128)(2,1)S(1)} %pack.1.own_ref), channel_id=1, source_target_pairs={{0,1},{1,0},{2,3},{3,2},{4,5},{5,4},{6,7},{7,6},{8,9},{9,8},{10,11... | collective-permute-start | bytes 811016 | tf_op jit(solution)/shard_map/ppermute | solution.py:243
  37.4 19.0 %all-to-all-start.1 = ((bf16[32,128,128]{2,1,0:T(8,128)(2,1)}), bf16[32,128,128]{2,1,0:T(8,128)(2,1)S(1)}, u32[]{:S(2)}, u32[]{:S(2)}) async-start(bf16[32,128,128]{2,1,0:T(8,128)(2,1)} %bitcast.5), calls=%async_computation.1 | async-start | bytes 2097152 | tf_op jit(solution)/shard_map/all_to_all | solution.py:265
  41.3 20.9 %collective-permute-start.2 = (f32[512,128]{1,0:T(8,128)S(1)}, f32[512,128]{1,0:T(8,128)S(1)}, u32[]{:S(2)}, u32[]{:S(2)}) collective-permute-start(f32[512,128]{1,0:T(8,128)S(1)} %get-tuple-element.14), channel_id=1, source_target_pairs={{0,1},{1,0},{2,3},{3,2},{4,5},{5,4},{6,7},{7,6},{8,9},{9,8},{10,11... | collective-permute-start | bytes 786440 | tf_op jit(solution)/shard_map/ppermute | solution.py:267
  56.5 6.6 %collective-permute-start.3 = (f32[4,16,128]{2,1,0:T(8,128)S(1)}, f32[4,16,128]{2,1,0:T(8,128)S(1)}, u32[]{:S(2)}, u32[]{:S(2)}) collective-permute-start(f32[4,16,128]{2,1,0:T(8,128)S(1)} %get-tuple-element.17), channel_id=1, source_target_pairs={{0,1},{1,0},{2,3},{3,2},{4,5},{5,4},{6,7},{7,6},{8,9},{9,8},{10,11... | collective-permute-start | bytes 98312 | tf_op jit(solution)/shard_map/ppermute | solution.py:273

commit v4 on v3

v4 whole, which is shorter than its diff:
```python
import jax
import jax.numpy as jnp
from jax import lax
from jax.experimental import pallas as pl
from jax.experimental.pallas import tpu as pltpu
from jax.sharding import Mesh, PartitionSpec as P

KVH = 8
DH = 128
BLOCK = 128
F32 = jnp.float32
BF16 = jnp.bfloat16
I32 = jnp.int32
SCALE = DH ** -0.5
PAIRS = 6
LOG2E = 1.4426950408889634
DEVICES = ("x", "yl", "zl", "yh", "core")
HBM = pl.BlockSpec(memory_space=pltpu.MemorySpace.HBM)
VMEM = pl.BlockSpec(memory_space=pltpu.VMEM)
ROW_Q, ROW_G, ROW_S, ROWS = 0, 512, 1024, 1056


def call(kernel, outs, in_specs, scratch=(), limit=4, name=None, outs_at=None):
    return pl.pallas_call(
        kernel,
        out_shape=outs,
        in_specs=in_specs,
        out_specs=outs_at or jax.tree.map(lambda _: VMEM, outs),
        scratch_shapes=list(scratch),
        compiler_params=pltpu.CompilerParams(vmem_limit_bytes=limit * 2**20),
        name=name,
    )


def pieces(value):
    high = value.astype(BF16).astype(F32)
    rest = value - high
    middle = rest.astype(BF16).astype(F32)
    return high, middle, rest - middle


def pack_kernel(q_ref, g_ref, o_ref, lse_ref, ids_ref, out_ref, o_v, lse_v, ids_v, small, sems):
    copies = [
        pltpu.make_async_copy(source, target, sems.at[n])
        for n, (source, target) in enumerate((
            (lse_ref, lse_v),
            (ids_ref, ids_v),
            (q_ref, out_ref.at[ROW_Q:ROW_G]),
            (g_ref, out_ref.at[ROW_G:ROW_S]),
            (o_ref, o_v),
        ))
    ]
    for copy in copies:
        copy.start()
    small[...] = jnp.zeros((32, 128), F32)
    for copy in copies:
        copy.wait()
    lane = lax.broadcasted_iota(I32, (128, 128), 1)
    columns = jnp.zeros((128, 128), F32)
    for b in range(4):
        rows = slice(b * 128, b * 128 + 128)
        g = out_ref[ROW_G + b * 128 : ROW_G + b * 128 + 128]
        delta = jnp.sum(g.astype(F32) * o_v[rows].astype(F32), axis=1, keepdims=True)
        columns = jnp.where(lane == b, delta, columns)
    for n, piece in enumerate(pieces(lse_v[...]) + pieces(columns.T[0:4])):
        small[n * 4 : n * 4 + 4] = piece
    small[24:28, 0:8] = ids_v[...].astype(F32)
    out_ref[ROW_S:ROWS] = small[...].astype(BF16)


def spread_kernel(kv_ref, out_ref, chunk, sems):
    for half in range(2):
        for which in range(2):
            for j in range(2):
                at = half * 64 + which * 32 + j * 16
                column = half * 256 + j * 128
                value = kv_ref[which, :, column : column + 128]
                for chip in range(8):
                    chunk[chip, at : at + 16] = value
    copies = [
        pltpu.make_async_copy(chunk, out_ref.at[n * 8 : n * 8 + 8], sems.at[n]) for n in range(4)
    ]
    for copy in copies:
        copy.start()
    for copy in copies:
        copy.wait()


SPAN = 880
NONE = 16
NO_PAIR = NONE + (8 << 14)


def ready_kernel(own_ref, got_ref, operands_ref, columns_ref, words_ref, table):
    core = lax.axis_index("core")
    table[...] = jnp.zeros((128, 128), F32)
    blocks = []
    for n, ref in enumerate((own_ref, got_ref)):
        small = ref[ROW_S:ROWS].astype(F32)
        lse = (small[0:4] + small[4:8] + small[8:12]) * LOG2E
        delta = small[12:16] + small[16:20] + small[20:24]
        blocks.append(small[24:28])
        for b in range(4):
            for which, row in enumerate((ROW_Q, ROW_G)):
                value = ref[row + b * 128 : row + b * 128 + 128]
                operands_ref[n * 4 + b, which] = value
                operands_ref[n * 4 + b, 2 + which] = value.T
            table[0:1] = lse[b : b + 1]
            table[1:2] = delta[b : b + 1]
            columns_ref[n * 4 + b] = table[...].T
    block = jnp.concatenate(blocks, 0).astype(I32)
    row = lax.broadcasted_iota(I32, block.shape, 0)
    word = (((block >> 2) & 3) * 1024 + (block >> 4) * 128 + (block & 1) * 16) * 2
    word = word + (block >> 2) * 2 + (block & 1) + (row << 14) + (1 << 20)
    words_ref[...] = jnp.where(((block >> 1) & 1) == core, word, NONE)


def main_kernel(
    kv_ref, operands_ref, columns_ref, words_ref, part_ref, dq_own_ref, dq_other_ref,
    acc, dq_acc, part, words_s, slots, sem, part_sems,
):
    copy = pltpu.make_async_copy(words_ref, words_s, sem)
    copy.start()
    dq_acc[...] = jnp.zeros(dq_acc.shape, F32)
    acc[0:8] = jnp.zeros((8,) + acc.shape[1:], F32)
    copy.wait()
    acc[8:17] = jnp.zeros((9,) + acc.shape[1:], F32)
    slot = jnp.int32(0)
    for b in range(8):
        for r in range(8):
            word = words_s[b, r]
            slots[slot] = word
            slot = slot + (word >> 20)
        slots[slot] = NONE
        slot = (slot + 1) & -2
    for p in range(2 * PAIRS):
        slots[slot + p] = NO_PAIR

    def tiles(words, which):
        columns = []
        for word in words:
            block = kv_ref.at[pl.ds(pl.multiple_of((word & 8160) >> 1, 16), SPAN)]
            rows = [
                block[yl * 512 + zl * 256 + core * 64 + which * 32 : yl * 512 + zl * 256 + core * 64 + which * 32 + 16]
                for zl in range(2)
                for yl in range(2)
                for core in range(2)
            ]
            columns.append(jnp.concatenate(rows, 0))
        return jnp.concatenate(columns, 1)

    def step(group, carry):
        begun = []
        for u in range(PAIRS):
            at = (group * PAIRS + u) * 2
            words = slots[at], slots[at + 1]
            b = (words[0] >> 14) & 7
            k = tiles(words, 0)
            scores = jnp.dot(operands_ref[b, 0], k, preferred_element_type=F32)
            weight_grad = jnp.dot(operands_ref[b, 1], tiles(words, 1), preferred_element_type=F32)
            lse, delta = (
                jnp.broadcast_to(columns_ref[b, :, n : n + 1], (128, 128)) for n in range(2)
            )
            weights, score_grads = [], []
            for n in range(2):
                cols = slice(n * 128, n * 128 + 128)
                weight = jnp.exp2(scores[:, cols] * (SCALE * LOG2E) - lse)
                score_grad = (weight * (weight_grad[:, cols] - delta) * SCALE).astype(BF16)
                if n:
                    score_grad = jnp.where((words[1] & 31) < NONE, score_grad, jnp.zeros_like(score_grad))
                weights.append(weight.astype(BF16))
                score_grads.append(score_grad)
            begun.append((words, b, k, jnp.concatenate(weights, 1), jnp.concatenate(score_grads, 1)))
        for words, b, k, weights, score_grad in begun:
            dq = lax.dot_general(score_grad, k, (((1,), (1,)), ((), ())), preferred_element_type=F32)
            dk = jnp.dot(operands_ref[b, 2], score_grad, preferred_element_type=F32)
            dv = jnp.dot(operands_ref[b, 3], weights, preferred_element_type=F32)
            dq_acc[(words[0] >> 14) & 15] += dq
            first, second = words[0] & 31, words[1] & 31
            old = [acc[n, which] for n in (first, second) for which in range(2)]
            new = [dk[:, :128], dv[:, :128], dk[:, 128:], dv[:, 128:]]
            new = [x + y for x, y in zip(old, new)]
            acc[first, 0], acc[first, 1], acc[second, 0], acc[second, 1] = new
        return carry

    lax.fori_loop(0, ((slot >> 1) + PAIRS - 1) // PAIRS, step, 0)
    copies = []
    for x in range(4):
        for yl in range(2):
            for zl in range(2):
                for yh in range(2):
                    for core in range(2):
                        for which in range(2):
                            for j in range(2):
                                at = x * 1024 + yl * 512 + zl * 256 + yh * 128 + core * 64 + which * 32 + j * 16
                                feature = (zl * 2 + yl) * 32 + core * 16
                                tile = acc[(yh * 4 + x) * 2 + j, which, feature : feature + 16]
                                part[at : at + 16] = tile.astype(BF16)
        rows = slice(x * 1024, x * 1024 + 1024)
        copies.append(pltpu.make_async_copy(part.at[rows], part_ref.at[rows], part_sems.at[x]))
        copies[-1].start()
    for b in range(4):
        dq_own_ref[b * 128 : b * 128 + 128] = dq_acc[b]
        dq_other_ref[b * 128 : b * 128 + 128] = dq_acc[b + 4]
    for copy in copies:
        copy.wait()


def dq_kernel(own_ref, got_ref, out_ref):
    out_ref[...] = (own_ref[...] + got_ref[...]).astype(BF16)


def sum_kernel(got_ref, out_ref):
    for core in range(2):
        for which in range(2):
            for j in range(2):
                at = core * 64 + which * 32 + j * 16
                value = got_ref[0, at : at + 16].astype(F32)
                for chip in range(1, 32):
                    value = value + got_ref[chip, at : at + 16].astype(F32)
                column = core * 256 + j * 128
                out_ref[which, :, column : column + 128] = value


def shards(queries, outputs, out_grad, keys_values, row_lse, collide):
    swap = [(0, 1), (1, 0)]
    struct = jax.ShapeDtypeStruct
    spread = call(
        spread_kernel, struct((32, 128, 128), BF16), [VMEM],
        [pltpu.VMEM((8, 128, 128), BF16), pltpu.SemaphoreType.DMA((4,))],
        name="spread", outs_at=HBM,
    )(keys_values.transpose(0, 2, 1))

    def exchange(value):
        return lax.all_to_all(value.reshape(64, 64, 128), DEVICES, 0, 0)

    gathered = exchange(spread)
    packed = call(
        pack_kernel, struct((ROWS, DH), BF16), [HBM] * 5,
        [
            pltpu.VMEM((512, DH), BF16),
            pltpu.VMEM((4, 128), F32),
            pltpu.VMEM((4, 8), I32),
            pltpu.VMEM((32, 128), F32),
            pltpu.SemaphoreType.DMA((5,)),
        ],
        name="pack",
    )(queries, out_grad, outputs, row_lse.reshape(4, BLOCK), collide.reshape(4, 8))
    pay = lax.ppermute(packed, "core", swap)
    ready = call(
        ready_kernel,
        (struct((8, 4, 128, 128), BF16), struct((8, 128, 128), F32), struct((8, 128), I32)),
        [VMEM] * 2, [pltpu.VMEM((128, 128), F32)], name="ready",
    )(packed, pay)
    part, dq_own, dq_other = call(
        main_kernel,
        (struct((4096, DH), BF16), struct((512, DH), F32), struct((512, DH), F32)),
        [VMEM] * 4,
        [
            pltpu.VMEM((17, 2, 128, 128), F32),
            pltpu.VMEM((9, 128, 128), F32),
            pltpu.VMEM((4096, DH), BF16),
            pltpu.SMEM((8, 128), I32),
            pltpu.SMEM((64 + 16 + 2 * PAIRS,), I32),
            pltpu.SemaphoreType.DMA,
            pltpu.SemaphoreType.DMA((4,)),
        ],
        name="attend",
        limit=16,
        outs_at=(HBM, VMEM, VMEM),
    )(gathered.reshape(4096, 128), *ready)
    got = exchange(part)
    query_grad = call(dq_kernel, struct((512, DH), BF16), [VMEM] * 2, name="dq")(
        dq_own, lax.ppermute(dq_other, "core", swap)
    )
    kv_grad = call(sum_kernel, struct((2, 16, 512), F32), [VMEM], name="total")(got.reshape(32, 128, 128))
    return query_grad, kv_grad.transpose(0, 2, 1)


def solution(mesh):
    fine = Mesh(
        mesh.devices.reshape(2, 4, KVH, 2, 2, 2), ("yh", "x", "group", "zl", "yl", "core")
    )
    ctx, head = ("yh", "x"), ("group", "zl", "yl", "core")
    placed = (
        P(ctx, head), P(ctx, head), P(ctx, head), P(None, ctx, head), P(head, ctx), P(head, ctx, None),
    )
    return jax.shard_map(
        shards, mesh=fine, in_specs=placed, out_specs=(P(ctx, head), P(None, ctx, head)),
        check_vma=False,
    )
```

time: 64.1 us -> 60 us (0.936)
  starting transfers between devices: 28.6 us -> 21.2 us
  waiting for transfers between devices: 24.6 us -> 29 us
  Pallas kernels: 8.38 us -> 7.53 us
    ppermute x2 -> x0, starting transfers between devices: 14.5 us -> none  [the longest x1 8.75 us: shards(): got_kv = lax.ppermute(kv, 'core', swap)]
    all_to_all x2, starting transfers between devices: 8.01 us -> 16.3 us  [exchange(): return lax.all_to_all(value.reshape(64, 64, 128), DEVICES, 0, 0)]
    all_to_all x2, waiting for transfers between devices: 23 us -> 26.7 us  [exchange(): return lax.all_to_all(value.reshape(64, 64, 128), DEVICES, 0, 0)]
    ppermute x1, starting transfers between devices: 3.83 us -> 2.4 us  [shards(): lax.ppermute(dq_other, 'core', swap)]
    ppermute x1, waiting for transfers between devices: 0.01 us -> 1.14 us  [shards(): lax.ppermute(dq_other, 'core', swap)]
    pallas_call x1, Pallas kernels: 4.68 us -> 3.93 us  [shards(): call(main_kernel, (struct((4096, DH), BF16), struct((512, DH), F32), stru...]
    pallas_call x5 -> x3, Pallas kernels: 2.28 us -> 2.18 us  [the longest x1 1.04 us: shards(): call(spread_kernel, struct((32, 128, 128), BF16), [VMEM], [pltpu.VMEM((8,...]
  transfers between devices with their start and end apart: 6 -> 4, of which waited for: 5 -> 4; matrix products, arithmetic and copies ran while one was open for 0% -> 0% of each run, Pallas kernels for 3% -> 3%
where the time goes in v4:
time: 60 us; the launch traced here: 59.9 us
  waiting for transfers between devices  29 us (48%)
  starting transfers between devices  21.2 us (35%)
  Pallas kernels  7.53 us (13%)
  local copies, waits for them, and re-layouts  1.41 us (2%)
  between operations  0.77 us (1%)
    all_to_all x2, waiting for transfers between devices, exchange(): return lax.all_to_all(value.reshape(64, 64, 128), DEVICES, 0, 0)  26.7 us
    all_to_all x2, starting transfers between devices, exchange(): return lax.all_to_all(value.reshape(64, 64, 128), DEVICES, 0, 0)  16.3 us
    pallas_call x1, Pallas kernels, shards(): call(main_kernel, (struct((4096, DH), BF16), struct((512, DH), F32), stru...  3.93 us
    ppermute x1, starting transfers between devices, shards(): pay = lax.ppermute(packed, 'core', swap)  2.48 us
    ppermute x1, starting transfers between devices, shards(): lax.ppermute(dq_other, 'core', swap)  2.4 us
    unnamed x12, local copies, waits for them, and re-layouts  1.41 us
  transfers between devices with their start and end apart: 4, of which 4 were waited for; matrix products, arithmetic and copies ran while one was open for 0% of the time, Pallas kernels for 3%

profile of v4, /device:TPU:1, one launch (start us, length us, event | category | flops | bytes accessed | tf_op | source)
XLA Modules:
  0.0 59.9 jit_solution(4578381937254779286)
XLA Ops:
  0.6 0.0 copy-start.3
  0.6 0.7 %copy-done.3 = bf16[2,512,16]{1,2,0:T(8,128)(2,1)S(1)} copy-done((bf16[2,512,16]{1,2,0:T(8,128)(2,1)S(1)}, bf16[2,512,16]{1,2,0:T(8,128)(2,1)}, u32[]{:S(2)}) %copy-start.3) | copy-done | bytes 32792
  1.4 1.0 %spread.1 = bf16[32,128,128]{2,1,0:T(8,128)(2,1)} custom-call(bf16[2,16,512]{2,1,0:T(8,128)(2,1)S(1)} %bitcast.10), custom_call_target="tpu_custom_call" | custom-call | tf_op jit(solution)/shard_map/spread/pallas_call | solution.py:228
  2.4 0.0 copy-start
  2.4 0.0 copy-start.1
  2.5 0.0 copy-start.2
  2.5 0.0 copy-start.5
  2.5 11.1 %all-to-all-start = ((bf16[64,64,128]{2,1,0:T(8,128)(2,1)}), bf16[64,64,128]{2,1,0:T(8,128)(2,1)S(1)}, u32[]{:S(2)}, u32[]{:S(2)}) async-start(bf16[64,64,128]{2,1,0:T(8,128)(2,1)} %bitcast.1), calls=%async_computation | async-start | bytes 2097152 | tf_op jit(solution)/shard_map/all_to_all | solution.py:235
  13.6 0.0 copy-start.4
  13.6 0.0 copy-done
  13.6 0.0 copy-done.1
  13.6 0.0 copy-done.2
  13.6 0.0 copy-done.5
  13.6 0.6 %copy-done.4 = f32[1,512]{1,0:T(1,128)S(1)} copy-done((f32[1,512]{1,0:T(1,128)S(1)}, f32[1,512]{1,0:T(1,128)}, u32[]{:S(2)}) %copy-start.4) | copy-done | bytes 2072
  14.2 0.7 %pack.1.own_ref = bf16[1056,128]{1,0:T(8,128)(2,1)S(1)} custom-call(bf16[512,128]{1,0:T(8,128)(2,1)S(1)} %copy-done, bf16[512,128]{1,0:T(8,128)(2,1)S(1)} %copy-done.1, bf16[512,128]{1,0:T(8,128)(2,1)S(1)} %copy-done.2, f32[4,128]{1,0:T(4,128)S(1)} %bitcast.11, s32[4,8]{1,0:T(4,128)S(1)} %bitcast.12), custom_call_target="tpu_custom_call" | custom-call | tf_op jit(solution)/shard_map/pack/pallas_call | solution.py:238
  15.0 2.5 %collective-permute-start = (bf16[1056,128]{1,0:T(8,128)(2,1)S(1)}, bf16[1056,128]{1,0:T(8,128)(2,1)S(1)}, u32[]{:S(2)}, u32[]{:S(2)}) collective-permute-start(bf16[1056,128]{1,0:T(8,128)(2,1)S(1)} %pack.1.own_ref), channel_id=1, source_target_pairs={{0,1},{1,0},{2,3},{3,2},{4,5},{5,4},{6,7},{7,6},{8,9},{9,8},{10,11... | collective-permute-start | bytes 811016 | tf_op jit(solution)/shard_map/ppermute | solution.py:249
  17.5 1.2 %collective-permute-done.got_ref = bf16[1056,128]{1,0:T(8,128)(2,1)S(1)} collective-permute-done((bf16[1056,128]{1,0:T(8,128)(2,1)S(1)}, bf16[1056,128]{1,0:T(8,128)(2,1)S(1)}, u32[]{:S(2)}, u32[]{:S(2)}) %collective-permute-start) | collective-permute-done | bytes 270368 | tf_op jit(solution)/shard_map/ppermute | solution.py:249
  18.6 0.4 ready.1
  19.0 12.8 %all-to-all-done = bf16[64,64,128]{2,1,0:T(8,128)(2,1)S(1)} async-done(((bf16[64,64,128]{2,1,0:T(8,128)(2,1)}), bf16[64,64,128]{2,1,0:T(8,128)(2,1)S(1)}, u32[]{:S(2)}, u32[]{:S(2)}) %all-to-all-start) | async-done | bytes 1048608 | tf_op jit(solution)/shard_map/all_to_all | solution.py:235
  31.8 3.9 %attend.1 = (bf16[4096,128]{1,0:T(8,128)(2,1)}, f32[512,128]{1,0:T(8,128)S(1)}, f32[512,128]{1,0:T(8,128)S(1)}) custom-call(bf16[4096,128]{1,0:T(8,128)(2,1)S(1)} %bitcast.8, bf16[8,4,128,128]{3,2,1,0:T(8,128)(2,1)S(1)} %get-tuple-element.8.operands_ref, f32[8,128,128]{2,1,0:T(8,128)S(1)} %get-tuple-element.9.columns_ref, ...), custom_call_target="tpu_custom_call" | custom-call | tf_op jit(solution)/shard_map/attend/pallas_call | solution.py:255
  35.7 5.2 %all-to-all-start.1 = ((bf16[64,64,128]{2,1,0:T(8,128)(2,1)}), bf16[64,64,128]{2,1,0:T(8,128)(2,1)S(1)}, u32[]{:S(2)}, u32[]{:S(2)}) async-start(bf16[64,64,128]{2,1,0:T(8,128)(2,1)} %bitcast.5), calls=%async_computation.1 | async-start | bytes 2097152 | tf_op jit(solution)/shard_map/all_to_all | solution.py:235
  40.9 2.4 %collective-permute-start.1 = (f32[512,128]{1,0:T(8,128)S(1)}, f32[512,128]{1,0:T(8,128)S(1)}, u32[]{:S(2)}, u32[]{:S(2)}) collective-permute-start(f32[512,128]{1,0:T(8,128)S(1)} %get-tuple-element.12), channel_id=1, source_target_pairs={{0,1},{1,0},{2,3},{3,2},{4,5},{5,4},{6,7},{7,6},{8,9},{9,8},{10,11... | collective-permute-start | bytes 786440 | tf_op jit(solution)/shard_map/ppermute | solution.py:274
  43.4 1.1 %collective-permute-done.1.got_ref = f32[512,128]{1,0:T(8,128)S(1)} collective-permute-done((f32[512,128]{1,0:T(8,128)S(1)}, f32[512,128]{1,0:T(8,128)S(1)}, u32[]{:S(2)}, u32[]{:S(2)}) %collective-permute-start.1) | collective-permute-done | bytes 262176 | tf_op jit(solution)/shard_map/ppermute | solution.py:274
  44.5 0.7 %dq.1 = bf16[512,128]{1,0:T(8,128)(2,1)} custom-call(f32[512,128]{1,0:T(8,128)S(1)} %get-tuple-element.11.own_ref, f32[512,128]{1,0:T(8,128)S(1)} %collective-permute-done.1.got_ref), custom_call_target="tpu_custom_call" | custom-call | tf_op jit(solution)/shard_map/dq/pallas_call | solution.py:273
  45.2 13.9 %all-to-all-done.1 = bf16[64,64,128]{2,1,0:T(8,128)(2,1)S(1)} async-done(((bf16[64,64,128]{2,1,0:T(8,128)(2,1)}), bf16[64,64,128]{2,1,0:T(8,128)(2,1)S(1)}, u32[]{:S(2)}, u32[]{:S(2)}) %all-to-all-start.1) | async-done | bytes 1048608 | tf_op jit(solution)/shard_map/all_to_all | solution.py:235
  59.1 0.8 %total.1 = f32[2,16,512]{2,1,0:T(8,128)} custom-call(bf16[32,128,128]{2,1,0:T(8,128)(2,1)S(1)} %bitcast.9), custom_call_target="tpu_custom_call" | custom-call | tf_op jit(solution)/shard_map/total/pallas_call | solution.py:276
Async XLA Ops:
  0.6 0.8 %copy-start.3 = (bf16[2,512,16]{1,2,0:T(8,128)(2,1)S(1)}, bf16[2,512,16]{1,2,0:T(8,128)(2,1)}, u32[]{:S(2)}) copy-start(bf16[2,512,16]{1,2,0:T(8,128)(2,1)} %param.9) | copy-start | bytes 98308
  2.4 11.1 %copy-start = (bf16[512,128]{1,0:T(8,128)(2,1)S(1)}, bf16[512,128]{1,0:T(8,128)(2,1)}, u32[]{:S(2)}) copy-start(bf16[512,128]{1,0:T(8,128)(2,1)} %q_ref.1) | copy-start | bytes 393220
  2.4 11.1 %copy-start.1 = (bf16[512,128]{1,0:T(8,128)(2,1)S(1)}, bf16[512,128]{1,0:T(8,128)(2,1)}, u32[]{:S(2)}) copy-start(bf16[512,128]{1,0:T(8,128)(2,1)} %g_ref.1) | copy-start | bytes 393220
  2.5 11.1 %copy-start.2 = (bf16[512,128]{1,0:T(8,128)(2,1)S(1)}, bf16[512,128]{1,0:T(8,128)(2,1)}, u32[]{:S(2)}) copy-start(bf16[512,128]{1,0:T(8,128)(2,1)} %o_ref.1) | copy-start | bytes 393220
  2.5 11.1 %copy-start.5 = (s32[1,4,8]{2,1,0:T(4,128)S(1)}, s32[1,4,8]{2,1,0:T(4,128)}, u32[]{:S(2)}) copy-start(s32[1,4,8]{2,1,0:T(4,128)} %param.11) | copy-start | bytes 388
  2.5 29.3 %all-to-all-start = ((bf16[64,64,128]{2,1,0:T(8,128)(2,1)}), bf16[64,64,128]{2,1,0:T(8,128)(2,1)S(1)}, u32[]{:S(2)}, u32[]{:S(2)}) async-start(bf16[64,64,128]{2,1,0:T(8,128)(2,1)} %bitcast.1), calls=%async_computation | async-start | bytes 2097152 | tf_op jit(solution)/shard_map/all_to_all | solution.py:235
  13.6 0.7 %copy-start.4 = (f32[1,512]{1,0:T(1,128)S(1)}, f32[1,512]{1,0:T(1,128)}, u32[]{:S(2)}) copy-start(f32[1,512]{1,0:T(1,128)} %param.10) | copy-start | bytes 6148
  15.0 3.6 %collective-permute-start = (bf16[1056,128]{1,0:T(8,128)(2,1)S(1)}, bf16[1056,128]{1,0:T(8,128)(2,1)S(1)}, u32[]{:S(2)}, u32[]{:S(2)}) collective-permute-start(bf16[1056,128]{1,0:T(8,128)(2,1)S(1)} %pack.1.own_ref), channel_id=1, source_target_pairs={{0,1},{1,0},{2,3},{3,2},{4,5},{5,4},{6,7},{7,6},{8,9},{9,8},{10,11... | collective-permute-start | bytes 811016 | tf_op jit(solution)/shard_map/ppermute | solution.py:249
  35.7 23.4 %all-to-all-start.1 = ((bf16[64,64,128]{2,1,0:T(8,128)(2,1)}), bf16[64,64,128]{2,1,0:T(8,128)(2,1)S(1)}, u32[]{:S(2)}, u32[]{:S(2)}) async-start(bf16[64,64,128]{2,1,0:T(8,128)(2,1)} %bitcast.5), calls=%async_computation.1 | async-start | bytes 2097152 | tf_op jit(solution)/shard_map/all_to_all | solution.py:235
  40.9 3.5 %collective-permute-start.1 = (f32[512,128]{1,0:T(8,128)S(1)}, f32[512,128]{1,0:T(8,128)S(1)}, u32[]{:S(2)}, u32[]{:S(2)}) collective-permute-start(f32[512,128]{1,0:T(8,128)S(1)} %get-tuple-element.12), channel_id=1, source_target_pairs={{0,1},{1,0},{2,3},{3,2},{4,5},{5,4},{6,7},{7,6},{8,9},{9,8},{10,11... | collective-permute-start | bytes 786440 | tf_op jit(solution)/shard_map/ppermute | solution.py:274

commit v5 on v4

v5 whole, which is shorter than its diff:
```python
import jax
import jax.numpy as jnp
from jax import lax
from jax.experimental import pallas as pl
from jax.experimental.pallas import tpu as pltpu
from jax.sharding import Mesh, PartitionSpec as P

KVH = 8
DH = 128
BLOCK = 128
F32 = jnp.float32
BF16 = jnp.bfloat16
I32 = jnp.int32
SCALE = DH ** -0.5
PAIRS = 6
LOG2E = 1.4426950408889634
DEVICES = ("x", "yl", "zl", "yh", "core")
HBM = pl.BlockSpec(memory_space=pltpu.MemorySpace.HBM)
VMEM = pl.BlockSpec(memory_space=pltpu.VMEM)
ROW_Q, ROW_G, ROW_S, ROWS = 0, 512, 1024, 1056


def call(kernel, outs, in_specs, scratch=(), limit=4, outs_at=None):
    return pl.pallas_call(
        kernel,
        out_shape=outs,
        in_specs=in_specs,
        out_specs=outs_at or jax.tree.map(lambda _: VMEM, outs),
        scratch_shapes=list(scratch),
        compiler_params=pltpu.CompilerParams(vmem_limit_bytes=limit * 2**20),
    )


def pieces(value):
    high = value.astype(BF16).astype(F32)
    rest = value - high
    middle = rest.astype(BF16).astype(F32)
    return high, middle, rest - middle


def pack_kernel(q_ref, g_ref, o_ref, lse_ref, ids_ref, out_ref, o_v, lse_v, ids_v, small, sems):
    copies = [
        pltpu.make_async_copy(source, target, sems.at[n])
        for n, (source, target) in enumerate((
            (lse_ref, lse_v),
            (ids_ref, ids_v),
            (q_ref, out_ref.at[ROW_Q:ROW_G]),
            (g_ref, out_ref.at[ROW_G:ROW_S]),
            (o_ref, o_v),
        ))
    ]
    for copy in copies:
        copy.start()
    small[...] = jnp.zeros((32, 128), F32)
    for copy in copies:
        copy.wait()
    lane = lax.broadcasted_iota(I32, (128, 128), 1)
    columns = jnp.zeros((128, 128), F32)
    for b in range(4):
        rows = slice(b * 128, b * 128 + 128)
        g = out_ref[ROW_G + b * 128 : ROW_G + b * 128 + 128]
        delta = jnp.sum(g.astype(F32) * o_v[rows].astype(F32), axis=1, keepdims=True)
        columns = jnp.where(lane == b, delta, columns)
    for n, piece in enumerate(pieces(lse_v[...]) + pieces(columns.T[0:4])):
        small[n * 4 : n * 4 + 4] = piece
    small[24:28, 0:8] = ids_v[...].astype(F32)
    out_ref[ROW_S:ROWS] = small[...].astype(BF16)


def spread_kernel(kv_ref, out_ref, chunk, sems):
    for zl in range(2):
        for core in range(2):
            for which in range(2):
                column = (zl * 2 + core) * 128
                value = kv_ref[which, :, column : column + 128]
                for n in range(2):
                    for yh in range(2):
                        at = n * 256 + zl * 128 + yh * 64 + core * 32 + which * 16
                        chunk[at : at + 16] = value
    copies = [
        pltpu.make_async_copy(chunk, out_ref.at[n * 512 : n * 512 + 512], sems.at[n]) for n in range(4)
    ]
    for copy in copies:
        copy.start()
    for copy in copies:
        copy.wait()


SPAN = 448
NONE = 8
NO_PAIR = NONE + (16 << 14)


def ready_kernel(*refs):
    packed, (turned_ref, columns_ref, words_ref, table) = refs[:4], refs[4:]
    mine = lax.axis_index("zl") * 2 + lax.axis_index("core")
    table[...] = jnp.zeros((128, 128), F32)
    for n, ref in enumerate(packed):
        small = ref[ROW_S:ROWS].astype(F32)
        table[n * 4 : n * 4 + 4] = (small[0:4] + small[4:8] + small[8:12]) * LOG2E
        table[16 + n * 4 : 20 + n * 4] = small[12:16] + small[16:20] + small[20:24]
        table[32 + n * 4 : 36 + n * 4] = small[24:28]
        for b in range(4):
            for which, row in enumerate((ROW_Q, ROW_G)):
                turned_ref[n * 4 + b, which] = ref[row + b * 128 : row + b * 128 + 128].T
    block = table[32:48].astype(I32)
    row = lax.broadcasted_iota(I32, block.shape, 0)
    word = ((block >> 2) & 3) * 512 + (block >> 4) * 64 + (block >> 2) + (row << 14) + (1 << 20)
    words_ref[...] = jnp.where((block & 3) == mine, word, NONE)
    columns_ref[...] = table[...].T


def main_kernel(
    kv_ref, own_ref, near_ref, far_ref, last_ref, turned_ref, columns_ref, words_ref,
    part_ref, dq_near_ref, dq_far_ref,
    plain, level, acc, dq_acc, part, words_s, slots, sem, part_sems,
):
    copy = pltpu.make_async_copy(words_ref, words_s, sem)
    copy.start()
    for n, ref in enumerate((own_ref, near_ref, far_ref, last_ref)):
        for b in range(4):
            for which, row in enumerate((ROW_Q, ROW_G)):
                plain[n * 4 + b, which] = ref[row + b * 128 : row + b * 128 + 128]
    copy.wait()
    for b in range(16):
        for which in range(2):
            n = which * 16 + b
            level[b, which] = jnp.broadcast_to(columns_ref[:, n : n + 1], (128, 128))
    acc[...] = jnp.zeros(acc.shape, F32)
    dq_acc[...] = jnp.zeros(dq_acc.shape, F32)
    slot = jnp.int32(0)
    for b in range(16):
        for r in range(8):
            word = words_s[b, r]
            slots[slot] = word
            slot = slot + (word >> 20)
        slots[slot] = NONE
        slot = (slot + 1) & -2
    for p in range(2 * PAIRS):
        slots[slot + p] = NO_PAIR

    def tiles(words, which):
        columns = []
        for word in words:
            block = kv_ref.at[pl.ds(pl.multiple_of(word & 1984, 64), SPAN)]
            at = [yl * 256 + zl * 128 + core * 32 + which * 16 for zl in range(2) for yl in range(2) for core in range(2)]
            columns.append(jnp.concatenate([block[n : n + 16] for n in at], 0))
        return jnp.concatenate(columns, 1)

    def step(group, carry):
        begun = []
        for u in range(PAIRS):
            at = (group * PAIRS + u) * 2
            words = slots[at], slots[at + 1]
            b = (words[0] >> 14) & 15
            k = tiles(words, 0)
            scores = jnp.dot(plain[b, 0], k, preferred_element_type=F32)
            weight_grad = jnp.dot(plain[b, 1], tiles(words, 1), preferred_element_type=F32)
            lse, delta = level[b, 0], level[b, 1]
            weights, score_grads = [], []
            for n in range(2):
                cols = slice(n * 128, n * 128 + 128)
                weight = jnp.exp2(scores[:, cols] * (SCALE * LOG2E) - lse)
                score_grad = (weight * (weight_grad[:, cols] - delta) * SCALE).astype(BF16)
                if n:
                    score_grad = jnp.where((words[1] & 15) < NONE, score_grad, jnp.zeros_like(score_grad))
                weights.append(weight.astype(BF16))
                score_grads.append(score_grad)
            begun.append((words, b, k, jnp.concatenate(weights, 1), jnp.concatenate(score_grads, 1)))
        for words, b, k, weights, score_grad in begun:
            dq = lax.dot_general(score_grad, k, (((1,), (1,)), ((), ())), preferred_element_type=F32)
            dk = jnp.dot(turned_ref[b, 0], score_grad, preferred_element_type=F32)
            dv = jnp.dot(turned_ref[b, 1], weights, preferred_element_type=F32)
            dq_acc[(words[0] >> 14) & 31] += dq
            first, second = words[0] & 15, words[1] & 15
            old = [acc[n, which] for n in (first, second) for which in range(2)]
            new = [dk[:, :128], dv[:, :128], dk[:, 128:], dv[:, 128:]]
            new = [x + y for x, y in zip(old, new)]
            acc[first, 0], acc[first, 1], acc[second, 0], acc[second, 1] = new
        return carry

    lax.fori_loop(0, ((slot >> 1) + PAIRS - 1) // PAIRS, step, 0)
    copies = []
    for x in range(4):
        for yl in range(2):
            for zl in range(2):
                for yh in range(2):
                    for core in range(2):
                        for which in range(2):
                            at = x * 512 + yl * 256 + zl * 128 + yh * 64 + core * 32 + which * 16
                            feature = (zl * 2 + yl) * 32 + core * 16
                            tile = acc[yh * 4 + x, which, feature : feature + 16]
                            part[at : at + 16] = tile.astype(BF16)
        rows = slice(x * 512, x * 512 + 512)
        copies.append(pltpu.make_async_copy(part.at[rows], part_ref.at[rows], part_sems.at[x]))
        copies[-1].start()
    for b in range(8):
        dq_near_ref[b * 128 : b * 128 + 128] = dq_acc[b]
        dq_far_ref[b * 128 : b * 128 + 128] = dq_acc[b + 8].astype(BF16)
    for copy in copies:
        copy.wait()


def add_kernel(near_ref, got_ref, own_ref, other_ref):
    own_ref[...] = near_ref[0:512] + got_ref[0:512].astype(F32)
    other_ref[...] = near_ref[512:1024] + got_ref[512:1024].astype(F32)


def dq_kernel(own_ref, got_ref, out_ref):
    out_ref[...] = (own_ref[...] + got_ref[...]).astype(BF16)


def sum_kernel(got_ref, out_ref):
    for zl in range(2):
        for core in range(2):
            for which in range(2):
                value = jnp.zeros((16, 128), F32)
                for x in range(4):
                    for yl in range(2):
                        for yh in range(2):
                            at = x * 512 + yl * 256 + zl * 128 + yh * 64 + core * 32 + which * 16
                            value = value + got_ref[at : at + 16].astype(F32)
                column = (zl * 2 + core) * 128
                out_ref[which, :, column : column + 128] = value


def backward(queries, outputs, out_grad, keys_values, row_lse, collide):
    swap = [(0, 1), (1, 0)]
    struct = jax.ShapeDtypeStruct

    def exchange(value):
        return lax.all_to_all(value.reshape(64, 32, 128), DEVICES, 0, 0).reshape(2048, 128)

    packed = call(
        pack_kernel, struct((ROWS, DH), BF16), [HBM] * 5,
        [
            pltpu.VMEM((512, DH), BF16),
            pltpu.VMEM((4, 128), F32),
            pltpu.VMEM((4, 8), I32),
            pltpu.VMEM((32, 128), F32),
            pltpu.SemaphoreType.DMA((5,)),
        ],
        limit=60,
    )(queries, out_grad, outputs, row_lse.reshape(4, BLOCK), collide.reshape(4, 8))
    far = lax.ppermute(packed, "zl", swap)
    spread = call(
        spread_kernel, struct((2048, 128), BF16), [VMEM],
        [pltpu.VMEM((512, 128), BF16), pltpu.SemaphoreType.DMA((4,))],
        outs_at=HBM,
    )(keys_values.transpose(0, 2, 1))
    gathered = exchange(spread)
    queries_of = packed, lax.ppermute(packed, "core", swap), far, lax.ppermute(far, "core", swap)
    ready = call(
        ready_kernel,
        (struct((16, 2, 128, 128), BF16), struct((128, 128), F32), struct((16, 128), I32)),
        [VMEM] * 4, [pltpu.VMEM((128, 128), F32)],
    )(*queries_of)
    part, dq_near, dq_far = call(
        main_kernel,
        (struct((2048, DH), BF16), struct((1024, DH), F32), struct((1024, DH), BF16)),
        [VMEM] * 8,
        [
            pltpu.VMEM((16, 2, 128, 128), BF16),
            pltpu.VMEM((16, 2, 128, 128), F32),
            pltpu.VMEM((9, 2, 128, 128), F32),
            pltpu.VMEM((17, 128, 128), F32),
            pltpu.VMEM((2048, DH), BF16),
            pltpu.SMEM((16, 128), I32),
            pltpu.SMEM((128 + 32 + 2 * PAIRS,), I32),
            pltpu.SemaphoreType.DMA,
            pltpu.SemaphoreType.DMA((4,)),
        ],
        limit=16,
        outs_at=(HBM, VMEM, VMEM),
    )(gathered, *queries_of, *ready)
    got_dq = lax.ppermute(dq_far, "zl", swap)
    got = exchange(part)
    half = struct((512, DH), F32)
    dq_own, dq_other = call(add_kernel, (half, half), [VMEM] * 2)(dq_near, got_dq)
    query_grad = call(dq_kernel, struct((512, DH), BF16), [VMEM] * 2)(dq_own, lax.ppermute(dq_other, "core", swap))
    kv_grad = call(sum_kernel, struct((2, 16, 512), F32), [VMEM])(got)
    return query_grad, kv_grad.transpose(0, 2, 1)


def solution(mesh):
    fine = Mesh(
        mesh.devices.reshape(2, 4, KVH, 2, 2, 2), ("yh", "x", "group", "zl", "yl", "core")
    )
    ctx, head = ("yh", "x"), ("group", "zl", "yl", "core")
    placed = (
        P(ctx, head), P(ctx, head), P(ctx, head), P(None, ctx, head), P(head, ctx), P(head, ctx, None),
    )
    return jax.shard_map(
        backward, mesh=fine, in_specs=placed, out_specs=(P(ctx, head), P(None, ctx, head)),
        check_vma=False,
    )
```

time: 60 us -> 65.3 us (1.088)
  starting transfers between devices: 21.2 us -> 33.6 us
  waiting for transfers between devices: 29 us -> 17.5 us
  Pallas kernels: 7.53 us -> 9.8 us
  local copies, waits for them, and re-layouts: 1.41 us -> 3.07 us
    all_to_all x2, waiting for transfers between devices: 26.7 us -> 0.01 us  [exchange(): lax.all_to_all(value.reshape(64, 32, 128), DEVICES, 0, 0).reshape(2048, 128)]
    ppermute x2 -> x5, waiting for transfers between devices: 2.29 us -> 17.5 us  [the longest x1 9.83 us: backward(): got_dq = lax.ppermute(dq_far, 'zl', swap)]
    ppermute x2 -> x5, starting transfers between devices: 4.88 us -> 14.9 us  [the longest x1 3.29 us: backward(): far = lax.ppermute(packed, 'zl', swap)]
    all_to_all x2, starting transfers between devices: 16.3 us -> 18.7 us  [exchange(): lax.all_to_all(value.reshape(64, 32, 128), DEVICES, 0, 0).reshape(2048, 128)]
    pallas_call x6 -> x7, Pallas kernels: 7.53 us -> 9.8 us  [the longest x1 5.17 us: backward(): call(main_kernel, (struct((2048, DH), BF16), struct((1024, DH), F32), str...]
    unnamed x12 -> x8, local copies, waits for them, and re-layouts: 1.41 us -> 3.07 us
  transfers between devices with their start and end apart: 4 -> 7, of which waited for: 4 -> 4; matrix products, arithmetic and copies ran while one was open for 0% -> 0% of each run, Pallas kernels for 3% -> 5%
where the time goes in v5:
time: 65.3 us; the launch traced here: 64.7 us
  starting transfers between devices  33.6 us (51%)
  waiting for transfers between devices  17.5 us (27%)
  Pallas kernels  9.8 us (15%)
  local copies, waits for them, and re-layouts  3.07 us (5%)
  between operations  0.75 us (1%)
    all_to_all x2, starting transfers between devices, exchange(): lax.all_to_all(value.reshape(64, 32, 128), DEVICES, 0, 0).reshape(2048, 128)  18.7 us
    ppermute x1, waiting for transfers between devices, backward(): got_dq = lax.ppermute(dq_far, 'zl', swap)  9.83 us
    ppermute x1, waiting for transfers between devices, backward(): far = lax.ppermute(packed, 'zl', swap)  5.4 us
    pallas_call x1, Pallas kernels, backward(): call(main_kernel, (struct((2048, DH), BF16), struct((1024, DH), F32), str...  5.17 us
    ppermute x1, starting transfers between devices, backward(): far = lax.ppermute(packed, 'zl', swap)  3.29 us
    ppermute x1, starting transfers between devices, backward(): got_dq = lax.ppermute(dq_far, 'zl', swap)  3.26 us
    unnamed x8, local copies, waits for them, and re-layouts  3.07 us
    ppermute x1, starting transfers between devices, backward(): lax.ppermute(dq_other, 'core', swap)  2.88 us
  transfers between devices with their start and end apart: 7, of which 4 were waited for; matrix products, arithmetic and copies ran while one was open for 0% of the time, Pallas kernels for 5%

profile of v5, /device:TPU:1, one launch (start us, length us, event | category | flops | bytes accessed | tf_op | source)
XLA Modules:
  0.0 64.7 jit_solution(413957567208960412)
XLA Ops:
  0.6 0.0 copy-start.3
  0.6 0.7 %copy-done.3 = bf16[2,512,16]{1,2,0:T(8,128)(2,1)S(1)} copy-done((bf16[2,512,16]{1,2,0:T(8,128)(2,1)S(1)}, bf16[2,512,16]{1,2,0:T(8,128)(2,1)}, u32[]{:S(2)}) %copy-start.3) | copy-done | bytes 32792
  1.4 0.8 %shard_map.77 = bf16[2048,128]{1,0:T(8,128)(2,1)} custom-call(bf16[2,16,512]{2,1,0:T(8,128)(2,1)S(1)} %bitcast.11), custom_call_target="tpu_custom_call" | custom-call | tf_op jit(solution)/shard_map/pallas_call | solution.py:246
  2.2 10.9 %all-to-all-start = ((bf16[64,32,128]{2,1,0:T(8,128)(2,1)}), bf16[64,32,128]{2,1,0:T(8,128)(2,1)S(1)}, u32[]{:S(2)}, u32[]{:S(2)}) async-start(bf16[64,32,128]{2,1,0:T(8,128)(2,1)} %bitcast.1), calls=%async_computation | async-start | bytes 1048576 | tf_op jit(solution)/shard_map/all_to_all | solution.py:232
  13.2 2.0 %shard_map.78.refs_0_.own_ref = bf16[1056,128]{1,0:T(8,128)(2,1)} custom-call(bf16[512,128]{1,0:T(8,128)(2,1)} %q_ref.1, bf16[512,128]{1,0:T(8,128)(2,1)} %g_ref.1, bf16[512,128]{1,0:T(8,128)(2,1)} %o_ref.1, f32[4,128]{1,0:T(4,128)} %bitcast.13, s32[4,8]{1,0:T(4,128)} %bitcast.14), custom_call_target="tpu_custom_call" | custom-call | tf_op jit(solution)/shard_map/pallas_call | solution.py:234
  15.2 3.3 %collective-permute-start.1 = (bf16[1056,128]{1,0:T(8,128)(2,1)}, bf16[1056,128]{1,0:T(8,128)(2,1)S(1)}, u32[]{:S(2)}, u32[]{:S(2)}) collective-permute-start(bf16[1056,128]{1,0:T(8,128)(2,1)} %shard_map.78.refs_0_.own_ref), channel_id=1, source_target_pairs={{0,4},{4,0},{1,5},{5,1},{2,6},{6,2},{3,7},{7,3},{8,12},{12,8},{9,1... | collective-permute-start | bytes 811016 | tf_op jit(solution)/shard_map/ppermute | solution.py:245
  18.5 2.6 %collective-permute-start = (bf16[1056,128]{1,0:T(8,128)(2,1)}, bf16[1056,128]{1,0:T(8,128)(2,1)S(1)}, u32[]{:S(2)}, u32[]{:S(2)}) collective-permute-start(bf16[1056,128]{1,0:T(8,128)(2,1)} %shard_map.78.refs_0_.own_ref), channel_id=1, source_target_pairs={{0,1},{1,0},{2,3},{3,2},{4,5},{5,4},{6,7},{7,6},{8,9},{9,8},{10,11... | collective-permute-start | bytes 811016 | tf_op jit(solution)/shard_map/ppermute | solution.py:252
  21.1 5.4 %collective-permute-done.1.refs_2_.far_ref = bf16[1056,128]{1,0:T(8,128)(2,1)S(1)} collective-permute-done((bf16[1056,128]{1,0:T(8,128)(2,1)}, bf16[1056,128]{1,0:T(8,128)(2,1)S(1)}, u32[]{:S(2)}, u32[]{:S(2)}) %collective-permute-start.1) | collective-permute-done | bytes 270368 | tf_op jit(solution)/shard_map/ppermute | solution.py:245
  26.5 2.9 %collective-permute-start.2 = (bf16[1056,128]{1,0:T(8,128)(2,1)S(1)}, bf16[1056,128]{1,0:T(8,128)(2,1)S(1)}, u32[]{:S(2)}, u32[]{:S(2)}) collective-permute-start(bf16[1056,128]{1,0:T(8,128)(2,1)S(1)} %collective-permute-done.1.refs_2_.far_ref), channel_id=1, source_target_pairs={{0,1},{1,0},{2,3},{3,2},{4,5},{5,4},{6,7},{7,6},{8,9},{9,8},{10,11... | collective-permute-start | bytes 811016 | tf_op jit(solution)/shard_map/ppermute | solution.py:252
  29.3 0.0 collective-permute-done.refs_1_.near_ref
  29.3 1.1 %collective-permute-done.2.refs_3_.last_ref = bf16[1056,128]{1,0:T(8,128)(2,1)S(1)} collective-permute-done((bf16[1056,128]{1,0:T(8,128)(2,1)S(1)}, bf16[1056,128]{1,0:T(8,128)(2,1)S(1)}, u32[]{:S(2)}, u32[]{:S(2)}) %collective-permute-start.2) | collective-permute-done | bytes 270368 | tf_op jit(solution)/shard_map/ppermute | solution.py:252
  30.5 0.0 copy-start
  30.5 1.0 %copy-done = bf16[1056,128]{1,0:T(8,128)(2,1)S(1)} copy-done((bf16[1056,128]{1,0:T(8,128)(2,1)S(1)}, bf16[1056,128]{1,0:T(8,128)(2,1)}, u32[]{:S(2)}) %copy-start) | copy-done | bytes 270360
  31.4 0.0 copy-start.1
  31.4 0.4 shard_map.79
  31.8 0.0 all-to-all-done
  31.8 0.6 copy-done.1
  32.4 5.2 %shard_map.80 = (bf16[2048,128]{1,0:T(8,128)(2,1)S(1)}, f32[1024,128]{1,0:T(8,128)S(1)}, bf16[1024,128]{1,0:T(8,128)(2,1)S(1)}) custom-call(bf16[2048,128]{1,0:T(8,128)(2,1)S(1)} %bitcast.9, bf16[1056,128]{1,0:T(8,128)(2,1)S(1)} %copy-done.1, bf16[1056,128]{1,0:T(8,128)(2,1)S(1)} %collective-permute-done.refs_1_.near_ref, ...), custom_call_target="tpu_custom_call" | custom-call | tf_op jit(solution)/shard_map/pallas_call | solution.py:258
  37.6 0.0 copy-start.2
  37.6 0.8 %copy-done.2 = bf16[2048,128]{1,0:T(8,128)(2,1)} copy-done((bf16[2048,128]{1,0:T(8,128)(2,1)}, bf16[2048,128]{1,0:T(8,128)(2,1)S(1)}, u32[]{:S(2)}) %copy-start.2) | copy-done | bytes 524312
  38.4 7.8 %all-to-all-start.1 = ((bf16[64,32,128]{2,1,0:T(8,128)(2,1)}), bf16[64,32,128]{2,1,0:T(8,128)(2,1)S(1)}, u32[]{:S(2)}, u32[]{:S(2)}) async-start(bf16[64,32,128]{2,1,0:T(8,128)(2,1)} %bitcast.10), calls=%async_computation.1 | async-start | bytes 1048576 | tf_op jit(solution)/shard_map/all_to_all | solution.py:232
  46.1 3.3 %collective-permute-start.3 = (bf16[1024,128]{1,0:T(8,128)(2,1)S(1)}, bf16[1024,128]{1,0:T(8,128)(2,1)S(1)}, u32[]{:S(2)}, u32[]{:S(2)}) collective-permute-start(bf16[1024,128]{1,0:T(8,128)(2,1)S(1)} %get-tuple-element.14), channel_id=1, source_target_pairs={{0,4},{4,0},{1,5},{5,1},{2,6},{6,2},{3,7},{7,3},{8,12},{12,8},{9,1... | collective-permute-start | bytes 786440 | tf_op jit(solution)/shard_map/ppermute | solution.py:276
  49.4 9.8 %collective-permute-done.3.got_ref = bf16[1024,128]{1,0:T(8,128)(2,1)S(1)} collective-permute-done((bf16[1024,128]{1,0:T(8,128)(2,1)S(1)}, bf16[1024,128]{1,0:T(8,128)(2,1)S(1)}, u32[]{:S(2)}, u32[]{:S(2)}) %collective-permute-start.3) | collective-permute-done | bytes 262176 | tf_op jit(solution)/shard_map/ppermute | solution.py:276
  59.3 2.9 %collective-permute-start.4 = (f32[512,128]{1,0:T(8,128)S(1)}, f32[512,128]{1,0:T(8,128)S(1)}, u32[]{:S(2)}, u32[]{:S(2)}) collective-permute-start(f32[512,128]{1,0:T(8,128)S(1)} %get-tuple-element.16), channel_id=1, source_target_pairs={{0,1},{1,0},{2,3},{3,2},{4,5},{5,4},{6,7},{7,6},{8,9},{9,8},{10,11... | collective-permute-start | bytes 786440 | tf_op jit(solution)/shard_map/ppermute | solution.py:280
  62.2 1.1 %collective-permute-done.4.got_ref = f32[512,128]{1,0:T(8,128)S(1)} collective-permute-done((f32[512,128]{1,0:T(8,128)S(1)}, f32[512,128]{1,0:T(8,128)S(1)}, u32[]{:S(2)}, u32[]{:S(2)}) %collective-permute-start.4) | collective-permute-done | bytes 262176 | tf_op jit(solution)/shard_map/ppermute | solution.py:280
  63.3 0.7 %shard_map.82 = bf16[512,128]{1,0:T(8,128)(2,1)} custom-call(f32[512,128]{1,0:T(8,128)S(1)} %get-tuple-element.15.own_ref, f32[512,128]{1,0:T(8,128)S(1)} %collective-permute-done.4.got_ref), custom_call_target="tpu_custom_call" | custom-call | tf_op jit(solution)/shard_map/pallas_call | solution.py:280
  64.0 0.0 all-to-all-done.1
  64.0 0.7 %shard_map.83 = f32[2,16,512]{2,1,0:T(8,128)} custom-call(bf16[2048,128]{1,0:T(8,128)(2,1)S(1)} %bitcast.8), custom_call_target="tpu_custom_call" | custom-call | tf_op jit(solution)/shard_map/pallas_call | solution.py:281
  (1 shorter events, 0.0 us)
Async XLA Ops:
  0.6 0.8 %copy-start.3 = (bf16[2,512,16]{1,2,0:T(8,128)(2,1)S(1)}, bf16[2,512,16]{1,2,0:T(8,128)(2,1)}, u32[]{:S(2)}) copy-start(bf16[2,512,16]{1,2,0:T(8,128)(2,1)} %param.9) | copy-start | bytes 98308
  2.2 29.6 %all-to-all-start = ((bf16[64,32,128]{2,1,0:T(8,128)(2,1)}), bf16[64,32,128]{2,1,0:T(8,128)(2,1)S(1)}, u32[]{:S(2)}, u32[]{:S(2)}) async-start(bf16[64,32,128]{2,1,0:T(8,128)(2,1)} %bitcast.1), calls=%async_computation | async-start | bytes 1048576 | tf_op jit(solution)/shard_map/all_to_all | solution.py:232
  15.2 11.3 %collective-permute-start.1 = (bf16[1056,128]{1,0:T(8,128)(2,1)}, bf16[1056,128]{1,0:T(8,128)(2,1)S(1)}, u32[]{:S(2)}, u32[]{:S(2)}) collective-permute-start(bf16[1056,128]{1,0:T(8,128)(2,1)} %shard_map.78.refs_0_.own_ref), channel_id=1, source_target_pairs={{0,4},{4,0},{1,5},{5,1},{2,6},{6,2},{3,7},{7,3},{8,12},{12,8},{9,1... | collective-permute-start | bytes 811016 | tf_op jit(solution)/shard_map/ppermute | solution.py:245
  18.5 10.9 %collective-permute-start = (bf16[1056,128]{1,0:T(8,128)(2,1)}, bf16[1056,128]{1,0:T(8,128)(2,1)S(1)}, u32[]{:S(2)}, u32[]{:S(2)}) collective-permute-start(bf16[1056,128]{1,0:T(8,128)(2,1)} %shard_map.78.refs_0_.own_ref), channel_id=1, source_target_pairs={{0,1},{1,0},{2,3},{3,2},{4,5},{5,4},{6,7},{7,6},{8,9},{9,8},{10,11... | collective-permute-start | bytes 811016 | tf_op jit(solution)/shard_map/ppermute | solution.py:252
  26.5 4.0 %collective-permute-start.2 = (bf16[1056,128]{1,0:T(8,128)(2,1)S(1)}, bf16[1056,128]{1,0:T(8,128)(2,1)S(1)}, u32[]{:S(2)}, u32[]{:S(2)}) collective-permute-start(bf16[1056,128]{1,0:T(8,128)(2,1)S(1)} %collective-permute-done.1.refs_2_.far_ref), channel_id=1, source_target_pairs={{0,1},{1,0},{2,3},{3,2},{4,5},{5,4},{6,7},{7,6},{8,9},{9,8},{10,11... | collective-permute-start | bytes 811016 | tf_op jit(solution)/shard_map/ppermute | solution.py:252
  30.5 1.0 %copy-start = (bf16[1056,128]{1,0:T(8,128)(2,1)S(1)}, bf16[1056,128]{1,0:T(8,128)(2,1)}, u32[]{:S(2)}) copy-start(bf16[1056,128]{1,0:T(8,128)(2,1)} %shard_map.78.refs_0_.own_ref) | copy-start | bytes 811012
  31.4 1.0 %copy-start.1 = (bf16[1056,128]{1,0:T(8,128)(2,1)S(1)}, bf16[1056,128]{1,0:T(8,128)(2,1)}, u32[]{:S(2)}) copy-start(bf16[1056,128]{1,0:T(8,128)(2,1)} %shard_map.78.refs_0_.own_ref) | copy-start | bytes 811012
  37.6 0.8 %copy-start.2 = (bf16[2048,128]{1,0:T(8,128)(2,1)}, bf16[2048,128]{1,0:T(8,128)(2,1)S(1)}, u32[]{:S(2)}) copy-start(bf16[2048,128]{1,0:T(8,128)(2,1)S(1)} %get-tuple-element.17) | copy-start | bytes 1572868
  38.4 25.6 %all-to-all-start.1 = ((bf16[64,32,128]{2,1,0:T(8,128)(2,1)}), bf16[64,32,128]{2,1,0:T(8,128)(2,1)S(1)}, u32[]{:S(2)}, u32[]{:S(2)}) async-start(bf16[64,32,128]{2,1,0:T(8,128)(2,1)} %bitcast.10), calls=%async_computation.1 | async-start | bytes 1048576 | tf_op jit(solution)/shard_map/all_to_all | solution.py:232
  46.1 13.1 %collective-permute-start.3 = (bf16[1024,128]{1,0:T(8,128)(2,1)S(1)}, bf16[1024,128]{1,0:T(8,128)(2,1)S(1)}, u32[]{:S(2)}, u32[]{:S(2)}) collective-permute-start(bf16[1024,128]{1,0:T(8,128)(2,1)S(1)} %get-tuple-element.14), channel_id=1, source_target_pairs={{0,4},{4,0},{1,5},{5,1},{2,6},{6,2},{3,7},{7,3},{8,12},{12,8},{9,1... | collective-permute-start | bytes 786440 | tf_op jit(solution)/shard_map/ppermute | solution.py:276
  59.3 4.0 %collective-permute-start.4 = (f32[512,128]{1,0:T(8,128)S(1)}, f32[512,128]{1,0:T(8,128)S(1)}, u32[]{:S(2)}, u32[]{:S(2)}) collective-permute-start(f32[512,128]{1,0:T(8,128)S(1)} %get-tuple-element.16), channel_id=1, source_target_pairs={{0,1},{1,0},{2,3},{3,2},{4,5},{5,4},{6,7},{7,6},{8,9},{9,8},{10,11... | collective-permute-start | bytes 786440 | tf_op jit(solution)/shard_map/ppermute | solution.py:280

commit v6 on v5

--- a/solution.py
+++ b/solution.py
@@ -38,21 +38,40 @@
     return high, middle, rest - middle
 
 
-def pack_kernel(q_ref, g_ref, o_ref, lse_ref, ids_ref, out_ref, o_v, lse_v, ids_v, small, sems):
+def pack_kernel(
+    q_ref, g_ref, o_ref, lse_ref, ids_ref, kv_ref, out_ref, spread_ref,
+    o_v, lse_v, ids_v, kv_v, small, chunk, sems,
+):
     copies = [
         pltpu.make_async_copy(source, target, sems.at[n])
         for n, (source, target) in enumerate((
+            (kv_ref, kv_v),
             (lse_ref, lse_v),
             (ids_ref, ids_v),
-            (q_ref, out_ref.at[ROW_Q:ROW_G]),
             (g_ref, out_ref.at[ROW_G:ROW_S]),
             (o_ref, o_v),
+            (q_ref, out_ref.at[ROW_Q:ROW_G]),
         ))
     ]
     for copy in copies:
         copy.start()
     small[...] = jnp.zeros((32, 128), F32)
-    for copy in copies:
+    copies[0].wait()
+    for zl in range(2):
+        for core in range(2):
+            for which in range(2):
+                column = (zl * 2 + core) * 128
+                value = kv_v[which, :, column : column + 128]
+                for n in range(2):
+                    for yh in range(2):
+                        at = n * 256 + zl * 128 + yh * 64 + core * 32 + which * 16
+                        chunk[at : at + 16] = value
+    spreads = [
+        pltpu.make_async_copy(chunk, spread_ref.at[n * 512 : n * 512 + 512], sems.at[6 + n]) for n in range(4)
+    ]
+    for copy in spreads:
+        copy.start()
+    for copy in copies[1:]:
         copy.wait()
     lane = lax.broadcasted_iota(I32, (128, 128), 1)
     columns = jnp.zeros((128, 128), F32)
@@ -65,24 +84,7 @@
         small[n * 4 : n * 4 + 4] = piece
     small[24:28, 0:8] = ids_v[...].astype(F32)
     out_ref[ROW_S:ROWS] = small[...].astype(BF16)
-
-
-def spread_kernel(kv_ref, out_ref, chunk, sems):
-    for zl in range(2):
-        for core in range(2):
-            for which in range(2):
-                column = (zl * 2 + core) * 128
-                value = kv_ref[which, :, column : column + 128]
-                for n in range(2):
-                    for yh in range(2):
-                        at = n * 256 + zl * 128 + yh * 64 + core * 32 + which * 16
-                        chunk[at : at + 16] = value
-    copies = [
-        pltpu.make_async_copy(chunk, out_ref.at[n * 512 : n * 512 + 512], sems.at[n]) for n in range(4)
-    ]
-    for copy in copies:
-        copy.start()
-    for copy in copies:
+    for copy in spreads:
         copy.wait()
 
 
@@ -112,8 +114,8 @@
 
 def main_kernel(
     kv_ref, own_ref, near_ref, far_ref, last_ref, turned_ref, columns_ref, words_ref,
-    part_ref, dq_near_ref, dq_far_ref,
-    plain, level, acc, dq_acc, part, words_s, slots, sem, part_sems,
+    acc, dq_near_ref, dq_far_ref,
+    plain, dq_acc, words_s, slots, sem,
 ):
     copy = pltpu.make_async_copy(words_ref, words_s, sem)
     copy.start()
@@ -122,10 +124,6 @@
             for which, row in enumerate((ROW_Q, ROW_G)):
                 plain[n * 4 + b, which] = ref[row + b * 128 : row + b * 128 + 128]
     copy.wait()
-    for b in range(16):
-        for which in range(2):
-            n = which * 16 + b
-            level[b, which] = jnp.broadcast_to(columns_ref[:, n : n + 1], (128, 128))
     acc[...] = jnp.zeros(acc.shape, F32)
     dq_acc[...] = jnp.zeros(dq_acc.shape, F32)
     slot = jnp.int32(0)
@@ -156,7 +154,9 @@
             k = tiles(words, 0)
             scores = jnp.dot(plain[b, 0], k, preferred_element_type=F32)
             weight_grad = jnp.dot(plain[b, 1], tiles(words, 1), preferred_element_type=F32)
-            lse, delta = level[b, 0], level[b, 1]
+            lse, delta = (
+                jnp.take_along_axis(columns_ref[...], jnp.full((128, 128), n, I32), axis=1) for n in (b, 16 + b)
+            )
             weights, score_grads = [], []
             for n in range(2):
                 cols = slice(n * 128, n * 128 + 128)
@@ -180,6 +180,12 @@
         return carry
 
     lax.fori_loop(0, ((slot >> 1) + PAIRS - 1) // PAIRS, step, 0)
+    for b in range(8):
+        dq_near_ref[b * 128 : b * 128 + 128] = dq_acc[b]
+        dq_far_ref[b * 128 : b * 128 + 128] = dq_acc[b + 8].astype(BF16)
+
+
+def partial_kernel(acc, part_ref, part, sems):
     copies = []
     for x in range(4):
         for yl in range(2):
@@ -192,11 +198,8 @@
                             tile = acc[yh * 4 + x, which, feature : feature + 16]
                             part[at : at + 16] = tile.astype(BF16)
         rows = slice(x * 512, x * 512 + 512)
-        copies.append(pltpu.make_async_copy(part.at[rows], part_ref.at[rows], part_sems.at[x]))
+        copies.append(pltpu.make_async_copy(part.at[rows], part_ref.at[rows], sems.at[x]))
         copies[-1].start()
-    for b in range(8):
-        dq_near_ref[b * 128 : b * 128 + 128] = dq_acc[b]
-        dq_far_ref[b * 128 : b * 128 + 128] = dq_acc[b + 8].astype(BF16)
     for copy in copies:
         copy.wait()
 
@@ -231,23 +234,24 @@
     def exchange(value):
         return lax.all_to_all(value.reshape(64, 32, 128), DEVICES, 0, 0).reshape(2048, 128)
 
-    packed = call(
-        pack_kernel, struct((ROWS, DH), BF16), [HBM] * 5,
+    packed, spread = call(
+        pack_kernel, (struct((ROWS, DH), BF16), struct((2048, DH), BF16)), [HBM] * 6,
         [
             pltpu.VMEM((512, DH), BF16),
             pltpu.VMEM((4, 128), F32),
             pltpu.VMEM((4, 8), I32),
+            pltpu.VMEM((2, 16, 512), BF16),
             pltpu.VMEM((32, 128), F32),
-            pltpu.SemaphoreType.DMA((5,)),
+            pltpu.VMEM((512, DH), BF16),
+            pltpu.SemaphoreType.DMA((10,)),
         ],
         limit=60,
-    )(queries, out_grad, outputs, row_lse.reshape(4, BLOCK), collide.reshape(4, 8))
+        outs_at=(VMEM, HBM),
+    )(
+        queries, out_grad, outputs, row_lse.reshape(4, BLOCK), collide.reshape(4, 8),
+        keys_values.transpose(0, 2, 1),
+    )
     far = lax.ppermute(packed, "zl", swap)
-    spread = call(
-        spread_kernel, struct((2048, 128), BF16), [VMEM],
-        [pltpu.VMEM((512, 128), BF16), pltpu.SemaphoreType.DMA((4,))],
-        outs_at=HBM,
-    )(keys_values.transpose(0, 2, 1))
     gathered = exchange(spread)
     queries_of = packed, lax.ppermute(packed, "core", swap), far, lax.ppermute(far, "core", swap)
     ready = call(
@@ -255,25 +259,24 @@
         (struct((16, 2, 128, 128), BF16), struct((128, 128), F32), struct((16, 128), I32)),
         [VMEM] * 4, [pltpu.VMEM((128, 128), F32)],
     )(*queries_of)
-    part, dq_near, dq_far = call(
+    sums, dq_near, dq_far = call(
         main_kernel,
-        (struct((2048, DH), BF16), struct((1024, DH), F32), struct((1024, DH), BF16)),
+        (struct((9, 2, 128, 128), F32), struct((1024, DH), F32), struct((1024, DH), BF16)),
         [VMEM] * 8,
         [
             pltpu.VMEM((16, 2, 128, 128), BF16),
-            pltpu.VMEM((16, 2, 128, 128), F32),
-            pltpu.VMEM((9, 2, 128, 128), F32),
             pltpu.VMEM((17, 128, 128), F32),
-            pltpu.VMEM((2048, DH), BF16),
             pltpu.SMEM((16, 128), I32),
             pltpu.SMEM((128 + 32 + 2 * PAIRS,), I32),
             pltpu.SemaphoreType.DMA,
-            pltpu.SemaphoreType.DMA((4,)),
         ],
         limit=16,
-        outs_at=(HBM, VMEM, VMEM),
     )(gathered, *queries_of, *ready)
     got_dq = lax.ppermute(dq_far, "zl", swap)
+    part = call(
+        partial_kernel, struct((2048, DH), BF16), [VMEM],
+        [pltpu.VMEM((2048, DH), BF16), pltpu.SemaphoreType.DMA((4,))], outs_at=HBM,
+    )(sums)
     got = exchange(part)
     half = struct((512, DH), F32)
     dq_own, dq_other = call(add_kernel, (half, half), [VMEM] * 2)(dq_near, got_dq)

time: 65.3 us -> 63.3 us (0.969)
  local copies, waits for them, and re-layouts: 3.07 us -> 0.01 us
  waiting for transfers between devices: 17.5 us -> 19.5 us
  Pallas kernels: 9.8 us -> 8.89 us
    unnamed x8 -> x2, local copies, waits for them, and re-layouts: 3.07 us -> 0.01 us
    ppermute x1, waiting for transfers between devices: 5.4 us -> 7.43 us  [backward(): far = lax.ppermute(packed, 'zl', swap)]
    pallas_call x3, Pallas kernels: 8.02 us -> 7.11 us  [the longest x1 3.9 us: backward(): call(main_kernel, (struct((9, 2, 128, 128), F32), struct((1024, DH), F32)...]
  transfers between devices with their start and end apart: 7 -> 7, of which waited for: 4 -> 4; matrix products, arithmetic and copies ran while one was open for 0% -> 0% of each run, Pallas kernels for 5% -> 2%
where the time goes in v6:
time: 63.3 us; the launch traced here: 62.9 us
  starting transfers between devices  33.7 us (53%)
  waiting for transfers between devices  19.5 us (31%)
  Pallas kernels  8.89 us (14%)
  between operations  0.74 us (1%)
    all_to_all x2, starting transfers between devices, exchange(): lax.all_to_all(value.reshape(64, 32, 128), DEVICES, 0, 0).reshape(2048, 128)  18.8 us
    ppermute x1, waiting for transfers between devices, backward(): got_dq = lax.ppermute(dq_far, 'zl', swap)  9.83 us
    ppermute x1, waiting for transfers between devices, backward(): far = lax.ppermute(packed, 'zl', swap)  7.43 us
    pallas_call x1, Pallas kernels, backward(): call(main_kernel, (struct((9, 2, 128, 128), F32), struct((1024, DH), F32)...  3.9 us
    ppermute x1, starting transfers between devices, backward(): far = lax.ppermute(packed, 'zl', swap)  3.29 us
    ppermute x1, starting transfers between devices, backward(): got_dq = lax.ppermute(dq_far, 'zl', swap)  3.26 us
    ppermute x1, starting transfers between devices, backward(): lax.ppermute(dq_other, 'core', swap)  2.88 us
    ppermute x1, starting transfers between devices, backward(): lax.ppermute(far, 'core', swap)  2.86 us
  transfers between devices with their start and end apart: 7, of which 4 were waited for; matrix products, arithmetic and copies ran while one was open for 0% of the time, Pallas kernels for 2%

profile of v6, /device:TPU:1, one launch (start us, length us, event | category | flops | bytes accessed | tf_op | source)
XLA Modules:
  0.0 62.9 jit_solution(9466148925251515499)
XLA Ops:
  0.6 2.4 %shard_map.77 = (bf16[1056,128]{1,0:T(8,128)(2,1)}, bf16[2048,128]{1,0:T(8,128)(2,1)}) custom-call(bf16[512,128]{1,0:T(8,128)(2,1)} %q_ref.1, bf16[512,128]{1,0:T(8,128)(2,1)} %g_ref.1, bf16[512,128]{1,0:T(8,128)(2,1)} %o_ref.1, f32[4,128]{1,0:T(4,128)} %bitcast.13, s32[4,8]{1,0:T(4,128)} %bitcast.14, bf16[2,16,512]{2,1,0:T(8,128)(2,1)} %bitcast.12), custom_call_target="tpu_custom_call" | custom-call | tf_op jit(solution)/shard_map/pallas_call | solution.py:237
  3.0 0.0 copy-start
  3.0 11.0 %all-to-all-start = ((bf16[64,32,128]{2,1,0:T(8,128)(2,1)}), bf16[64,32,128]{2,1,0:T(8,128)(2,1)S(1)}, u32[]{:S(2)}, u32[]{:S(2)}) async-start(bf16[64,32,128]{2,1,0:T(8,128)(2,1)} %bitcast.10), calls=%async_computation | async-start | bytes 1048576 | tf_op jit(solution)/shard_map/all_to_all | solution.py:235
  14.1 3.3 %collective-permute-start.1 = (bf16[1056,128]{1,0:T(8,128)(2,1)}, bf16[1056,128]{1,0:T(8,128)(2,1)S(1)}, u32[]{:S(2)}, u32[]{:S(2)}) collective-permute-start(bf16[1056,128]{1,0:T(8,128)(2,1)} %get-tuple-element.13.refs_0_.own_ref), channel_id=1, source_target_pairs={{0,4},{4,0},{1,5},{5,1},{2,6},{6,2},{3,7},{7,3},{8,12},{12,8},{9,1... | collective-permute-start | bytes 811016 | tf_op jit(solution)/shard_map/ppermute | solution.py:254
  17.4 2.6 %collective-permute-start = (bf16[1056,128]{1,0:T(8,128)(2,1)}, bf16[1056,128]{1,0:T(8,128)(2,1)S(1)}, u32[]{:S(2)}, u32[]{:S(2)}) collective-permute-start(bf16[1056,128]{1,0:T(8,128)(2,1)} %get-tuple-element.13.refs_0_.own_ref), channel_id=1, source_target_pairs={{0,1},{1,0},{2,3},{3,2},{4,5},{5,4},{6,7},{7,6},{8,9},{9,8},{10,11... | collective-permute-start | bytes 811016 | tf_op jit(solution)/shard_map/ppermute | solution.py:256
  19.9 7.4 %collective-permute-done.1.refs_2_.far_ref = bf16[1056,128]{1,0:T(8,128)(2,1)S(1)} collective-permute-done((bf16[1056,128]{1,0:T(8,128)(2,1)}, bf16[1056,128]{1,0:T(8,128)(2,1)S(1)}, u32[]{:S(2)}, u32[]{:S(2)}) %collective-permute-start.1) | collective-permute-done | bytes 270368 | tf_op jit(solution)/shard_map/ppermute | solution.py:254
  27.4 2.9 %collective-permute-start.2 = (bf16[1056,128]{1,0:T(8,128)(2,1)S(1)}, bf16[1056,128]{1,0:T(8,128)(2,1)S(1)}, u32[]{:S(2)}, u32[]{:S(2)}) collective-permute-start(bf16[1056,128]{1,0:T(8,128)(2,1)S(1)} %collective-permute-done.1.refs_2_.far_ref), channel_id=1, source_target_pairs={{0,1},{1,0},{2,3},{3,2},{4,5},{5,4},{6,7},{7,6},{8,9},{9,8},{10,11... | collective-permute-start | bytes 811016 | tf_op jit(solution)/shard_map/ppermute | solution.py:256
  30.2 0.0 collective-permute-done.refs_1_.near_ref
  30.3 1.1 %collective-permute-done.2.refs_3_.last_ref = bf16[1056,128]{1,0:T(8,128)(2,1)S(1)} collective-permute-done((bf16[1056,128]{1,0:T(8,128)(2,1)S(1)}, bf16[1056,128]{1,0:T(8,128)(2,1)S(1)}, u32[]{:S(2)}, u32[]{:S(2)}) %collective-permute-start.2) | collective-permute-done | bytes 270368 | tf_op jit(solution)/shard_map/ppermute | solution.py:256
  31.4 0.0 copy-done
  31.4 0.4 shard_map.78
  31.7 0.0 all-to-all-done
  31.8 3.9 %shard_map.79 = (f32[9,2,128,128]{3,2,1,0:T(8,128)S(1)}, f32[1024,128]{1,0:T(8,128)S(1)}, bf16[1024,128]{1,0:T(8,128)(2,1)S(1)}) custom-call(bf16[2048,128]{1,0:T(8,128)(2,1)S(1)} %bitcast.9, bf16[1056,128]{1,0:T(8,128)(2,1)S(1)} %copy-done, bf16[1056,128]{1,0:T(8,128)(2,1)S(1)} %collective-permute-done.refs_1_.near_ref, ...), custom_call_target="tpu_custom_call" | custom-call | tf_op jit(solution)/shard_map/pallas_call | solution.py:262
  35.7 0.8 %shard_map.82 = bf16[2048,128]{1,0:T(8,128)(2,1)} custom-call(f32[9,2,128,128]{3,2,1,0:T(8,128)S(1)} %get-tuple-element.21.acc), custom_call_target="tpu_custom_call" | custom-call | tf_op jit(solution)/shard_map/pallas_call | solution.py:276
  36.5 7.8 %all-to-all-start.1 = ((bf16[64,32,128]{2,1,0:T(8,128)(2,1)}), bf16[64,32,128]{2,1,0:T(8,128)(2,1)S(1)}, u32[]{:S(2)}, u32[]{:S(2)}) async-start(bf16[64,32,128]{2,1,0:T(8,128)(2,1)} %bitcast.5), calls=%async_computation.1 | async-start | bytes 1048576 | tf_op jit(solution)/shard_map/all_to_all | solution.py:235
  44.3 3.3 %collective-permute-start.3 = (bf16[1024,128]{1,0:T(8,128)(2,1)S(1)}, bf16[1024,128]{1,0:T(8,128)(2,1)S(1)}, u32[]{:S(2)}, u32[]{:S(2)}) collective-permute-start(bf16[1024,128]{1,0:T(8,128)(2,1)S(1)} %get-tuple-element.18), channel_id=1, source_target_pairs={{0,4},{4,0},{1,5},{5,1},{2,6},{6,2},{3,7},{7,3},{8,12},{12,8},{9,1... | collective-permute-start | bytes 786440 | tf_op jit(solution)/shard_map/ppermute | solution.py:275
  47.6 9.8 %collective-permute-done.3.got_ref = bf16[1024,128]{1,0:T(8,128)(2,1)S(1)} collective-permute-done((bf16[1024,128]{1,0:T(8,128)(2,1)S(1)}, bf16[1024,128]{1,0:T(8,128)(2,1)S(1)}, u32[]{:S(2)}, u32[]{:S(2)}) %collective-permute-start.3) | collective-permute-done | bytes 262176 | tf_op jit(solution)/shard_map/ppermute | solution.py:275
  57.5 2.9 %collective-permute-start.4 = (f32[512,128]{1,0:T(8,128)S(1)}, f32[512,128]{1,0:T(8,128)S(1)}, u32[]{:S(2)}, u32[]{:S(2)}) collective-permute-start(f32[512,128]{1,0:T(8,128)S(1)} %get-tuple-element.20), channel_id=1, source_target_pairs={{0,1},{1,0},{2,3},{3,2},{4,5},{5,4},{6,7},{7,6},{8,9},{9,8},{10,11... | collective-permute-start | bytes 786440 | tf_op jit(solution)/shard_map/ppermute | solution.py:283
  60.4 1.1 %collective-permute-done.4.got_ref = f32[512,128]{1,0:T(8,128)S(1)} collective-permute-done((f32[512,128]{1,0:T(8,128)S(1)}, f32[512,128]{1,0:T(8,128)S(1)}, u32[]{:S(2)}, u32[]{:S(2)}) %collective-permute-start.4) | collective-permute-done | bytes 262176 | tf_op jit(solution)/shard_map/ppermute | solution.py:283
  61.5 0.7 %shard_map.81 = bf16[512,128]{1,0:T(8,128)(2,1)} custom-call(f32[512,128]{1,0:T(8,128)S(1)} %get-tuple-element.19.own_ref, f32[512,128]{1,0:T(8,128)S(1)} %collective-permute-done.4.got_ref), custom_call_target="tpu_custom_call" | custom-call | tf_op jit(solution)/shard_map/pallas_call | solution.py:283
  62.2 0.0 all-to-all-done.1
  62.2 0.7 %shard_map.83 = f32[2,16,512]{2,1,0:T(8,128)} custom-call(bf16[2048,128]{1,0:T(8,128)(2,1)S(1)} %bitcast.8), custom_call_target="tpu_custom_call" | custom-call | tf_op jit(solution)/shard_map/pallas_call | solution.py:284
  (1 shorter events, 0.0 us)
Async XLA Ops:
  3.0 28.4 %copy-start = (bf16[1056,128]{1,0:T(8,128)(2,1)S(1)}, bf16[1056,128]{1,0:T(8,128)(2,1)}, u32[]{:S(2)}) copy-start(bf16[1056,128]{1,0:T(8,128)(2,1)} %get-tuple-element.13.refs_0_.own_ref) | copy-start | bytes 811012
  3.0 28.7 %all-to-all-start = ((bf16[64,32,128]{2,1,0:T(8,128)(2,1)}), bf16[64,32,128]{2,1,0:T(8,128)(2,1)S(1)}, u32[]{:S(2)}, u32[]{:S(2)}) async-start(bf16[64,32,128]{2,1,0:T(8,128)(2,1)} %bitcast.10), calls=%async_computation | async-start | bytes 1048576 | tf_op jit(solution)/shard_map/all_to_all | solution.py:235
  14.1 13.3 %collective-permute-start.1 = (bf16[1056,128]{1,0:T(8,128)(2,1)}, bf16[1056,128]{1,0:T(8,128)(2,1)S(1)}, u32[]{:S(2)}, u32[]{:S(2)}) collective-permute-start(bf16[1056,128]{1,0:T(8,128)(2,1)} %get-tuple-element.13.refs_0_.own_ref), channel_id=1, source_target_pairs={{0,4},{4,0},{1,5},{5,1},{2,6},{6,2},{3,7},{7,3},{8,12},{12,8},{9,1... | collective-permute-start | bytes 811016 | tf_op jit(solution)/shard_map/ppermute | solution.py:254
  17.4 12.9 %collective-permute-start = (bf16[1056,128]{1,0:T(8,128)(2,1)}, bf16[1056,128]{1,0:T(8,128)(2,1)S(1)}, u32[]{:S(2)}, u32[]{:S(2)}) collective-permute-start(bf16[1056,128]{1,0:T(8,128)(2,1)} %get-tuple-element.13.refs_0_.own_ref), channel_id=1, source_target_pairs={{0,1},{1,0},{2,3},{3,2},{4,5},{5,4},{6,7},{7,6},{8,9},{9,8},{10,11... | collective-permute-start | bytes 811016 | tf_op jit(solution)/shard_map/ppermute | solution.py:256
  27.4 4.0 %collective-permute-start.2 = (bf16[1056,128]{1,0:T(8,128)(2,1)S(1)}, bf16[1056,128]{1,0:T(8,128)(2,1)S(1)}, u32[]{:S(2)}, u32[]{:S(2)}) collective-permute-start(bf16[1056,128]{1,0:T(8,128)(2,1)S(1)} %collective-permute-done.1.refs_2_.far_ref), channel_id=1, source_target_pairs={{0,1},{1,0},{2,3},{3,2},{4,5},{5,4},{6,7},{7,6},{8,9},{9,8},{10,11... | collective-permute-start | bytes 811016 | tf_op jit(solution)/shard_map/ppermute | solution.py:256
  36.5 25.7 %all-to-all-start.1 = ((bf16[64,32,128]{2,1,0:T(8,128)(2,1)}), bf16[64,32,128]{2,1,0:T(8,128)(2,1)S(1)}, u32[]{:S(2)}, u32[]{:S(2)}) async-start(bf16[64,32,128]{2,1,0:T(8,128)(2,1)} %bitcast.5), calls=%async_computation.1 | async-start | bytes 1048576 | tf_op jit(solution)/shard_map/all_to_all | solution.py:235
  44.3 13.1 %collective-permute-start.3 = (bf16[1024,128]{1,0:T(8,128)(2,1)S(1)}, bf16[1024,128]{1,0:T(8,128)(2,1)S(1)}, u32[]{:S(2)}, u32[]{:S(2)}) collective-permute-start(bf16[1024,128]{1,0:T(8,128)(2,1)S(1)} %get-tuple-element.18), channel_id=1, source_target_pairs={{0,4},{4,0},{1,5},{5,1},{2,6},{6,2},{3,7},{7,3},{8,12},{12,8},{9,1... | collective-permute-start | bytes 786440 | tf_op jit(solution)/shard_map/ppermute | solution.py:275
  57.5 4.0 %collective-permute-start.4 = (f32[512,128]{1,0:T(8,128)S(1)}, f32[512,128]{1,0:T(8,128)S(1)}, u32[]{:S(2)}, u32[]{:S(2)}) collective-permute-start(f32[512,128]{1,0:T(8,128)S(1)} %get-tuple-element.20), channel_id=1, source_target_pairs={{0,1},{1,0},{2,3},{3,2},{4,5},{5,4},{6,7},{7,6},{8,9},{9,8},{10,11... | collective-permute-start | bytes 786440 | tf_op jit(solution)/shard_map/ppermute | solution.py:283

commit v7 on v6

--- a/solution.py
+++ b/solution.py
@@ -12,7 +12,7 @@
 BF16 = jnp.bfloat16
 I32 = jnp.int32
 SCALE = DH ** -0.5
-PAIRS = 6
+PAIRS = 9
 LOG2E = 1.4426950408889634
 DEVICES = ("x", "yl", "zl", "yh", "core")
 HBM = pl.BlockSpec(memory_space=pltpu.MemorySpace.HBM)
@@ -40,7 +40,7 @@
 
 def pack_kernel(
     q_ref, g_ref, o_ref, lse_ref, ids_ref, kv_ref, out_ref, spread_ref,
-    o_v, lse_v, ids_v, kv_v, small, chunk, sems,
+    out_v, o_v, lse_v, ids_v, kv_v, small, chunk, sems,
 ):
     copies = [
         pltpu.make_async_copy(source, target, sems.at[n])
@@ -48,9 +48,9 @@
             (kv_ref, kv_v),
             (lse_ref, lse_v),
             (ids_ref, ids_v),
-            (g_ref, out_ref.at[ROW_G:ROW_S]),
+            (g_ref, out_v.at[ROW_G:ROW_S]),
             (o_ref, o_v),
-            (q_ref, out_ref.at[ROW_Q:ROW_G]),
+            (q_ref, out_v.at[ROW_Q:ROW_G]),
         ))
     ]
     for copy in copies:
@@ -73,17 +73,23 @@
         copy.start()
     for copy in copies[1:]:
         copy.wait()
+    spreads += [
+        pltpu.make_async_copy(out_v.at[rows], out_ref.at[rows], sems.at[10 + n])
+        for n, rows in enumerate((slice(ROW_Q, ROW_S), slice(ROW_S, ROWS)))
+    ]
+    spreads[4].start()
     lane = lax.broadcasted_iota(I32, (128, 128), 1)
     columns = jnp.zeros((128, 128), F32)
     for b in range(4):
         rows = slice(b * 128, b * 128 + 128)
-        g = out_ref[ROW_G + b * 128 : ROW_G + b * 128 + 128]
+        g = out_v[ROW_G + b * 128 : ROW_G + b * 128 + 128]
         delta = jnp.sum(g.astype(F32) * o_v[rows].astype(F32), axis=1, keepdims=True)
         columns = jnp.where(lane == b, delta, columns)
     for n, piece in enumerate(pieces(lse_v[...]) + pieces(columns.T[0:4])):
         small[n * 4 : n * 4 + 4] = piece
     small[24:28, 0:8] = ids_v[...].astype(F32)
-    out_ref[ROW_S:ROWS] = small[...].astype(BF16)
+    out_v[ROW_S:ROWS] = small[...].astype(BF16)
+    spreads[5].start()
     for copy in spreads:
         copy.wait()
 
@@ -237,16 +243,17 @@
     packed, spread = call(
         pack_kernel, (struct((ROWS, DH), BF16), struct((2048, DH), BF16)), [HBM] * 6,
         [
+            pltpu.VMEM((ROWS, DH), BF16),
             pltpu.VMEM((512, DH), BF16),
             pltpu.VMEM((4, 128), F32),
             pltpu.VMEM((4, 8), I32),
             pltpu.VMEM((2, 16, 512), BF16),
             pltpu.VMEM((32, 128), F32),
             pltpu.VMEM((512, DH), BF16),
-            pltpu.SemaphoreType.DMA((10,)),
+            pltpu.SemaphoreType.DMA((12,)),
         ],
         limit=60,
-        outs_at=(VMEM, HBM),
+        outs_at=(HBM, HBM),
     )(
         queries, out_grad, outputs, row_lse.reshape(4, BLOCK), collide.reshape(4, 8),
         keys_values.transpose(0, 2, 1),

time: 63.3 us -> 63.2 us (level)
  no operation moved by 1% of the time
where the time goes in v7:
time: 63.2 us; the launch traced here: 62.7 us
  starting transfers between devices  33.7 us (53%)
  waiting for transfers between devices  19.5 us (31%)
  Pallas kernels  8.73 us (14%)
  between operations  0.74 us (1%)
    all_to_all x2, starting transfers between devices, exchange(): lax.all_to_all(value.reshape(64, 32, 128), DEVICES, 0, 0).reshape(2048, 128)  18.8 us
    ppermute x1, waiting for transfers between devices, backward(): got_dq = lax.ppermute(dq_far, 'zl', swap)  9.83 us
    ppermute x1, waiting for transfers between devices, backward(): far = lax.ppermute(packed, 'zl', swap)  7.43 us
    pallas_call x1, Pallas kernels, backward(): call(main_kernel, (struct((9, 2, 128, 128), F32), struct((1024, DH), F32)...  4.12 us
    ppermute x1, starting transfers between devices, backward(): far = lax.ppermute(packed, 'zl', swap)  3.29 us
    ppermute x1, starting transfers between devices, backward(): got_dq = lax.ppermute(dq_far, 'zl', swap)  3.26 us
    ppermute x1, starting transfers between devices, backward(): lax.ppermute(dq_other, 'core', swap)  2.88 us
    ppermute x1, starting transfers between devices, backward(): lax.ppermute(far, 'core', swap)  2.86 us
  transfers between devices with their start and end apart: 7, of which 4 were waited for; matrix products, arithmetic and copies ran while one was open for 0% of the time, Pallas kernels for 2%

profile of v7, /device:TPU:1, one launch (start us, length us, event | category | flops | bytes accessed | tf_op | source)
XLA Modules:
  0.0 62.7 jit_solution(11912059927250676335)
XLA Ops:
  0.6 2.0 %shard_map.77 = (bf16[1056,128]{1,0:T(8,128)(2,1)}, bf16[2048,128]{1,0:T(8,128)(2,1)}) custom-call(bf16[512,128]{1,0:T(8,128)(2,1)} %q_ref.1, bf16[512,128]{1,0:T(8,128)(2,1)} %g_ref.1, bf16[512,128]{1,0:T(8,128)(2,1)} %o_ref.1, f32[4,128]{1,0:T(4,128)} %bitcast.13, s32[4,8]{1,0:T(4,128)} %bitcast.14, bf16[2,16,512]{2,1,0:T(8,128)(2,1)} %bitcast.12), custom_call_target="tpu_custom_call" | custom-call | tf_op jit(solution)/shard_map/pallas_call | solution.py:243
  2.6 0.0 copy-start
  2.6 11.0 %all-to-all-start = ((bf16[64,32,128]{2,1,0:T(8,128)(2,1)}), bf16[64,32,128]{2,1,0:T(8,128)(2,1)S(1)}, u32[]{:S(2)}, u32[]{:S(2)}) async-start(bf16[64,32,128]{2,1,0:T(8,128)(2,1)} %bitcast.10), calls=%async_computation | async-start | bytes 1048576 | tf_op jit(solution)/shard_map/all_to_all | solution.py:241
  13.7 3.3 %collective-permute-start.1 = (bf16[1056,128]{1,0:T(8,128)(2,1)}, bf16[1056,128]{1,0:T(8,128)(2,1)S(1)}, u32[]{:S(2)}, u32[]{:S(2)}) collective-permute-start(bf16[1056,128]{1,0:T(8,128)(2,1)} %get-tuple-element.13.refs_0_.own_ref), channel_id=1, source_target_pairs={{0,4},{4,0},{1,5},{5,1},{2,6},{6,2},{3,7},{7,3},{8,12},{12,8},{9,1... | collective-permute-start | bytes 811016 | tf_op jit(solution)/shard_map/ppermute | solution.py:261
  17.0 2.6 %collective-permute-start = (bf16[1056,128]{1,0:T(8,128)(2,1)}, bf16[1056,128]{1,0:T(8,128)(2,1)S(1)}, u32[]{:S(2)}, u32[]{:S(2)}) collective-permute-start(bf16[1056,128]{1,0:T(8,128)(2,1)} %get-tuple-element.13.refs_0_.own_ref), channel_id=1, source_target_pairs={{0,1},{1,0},{2,3},{3,2},{4,5},{5,4},{6,7},{7,6},{8,9},{9,8},{10,11... | collective-permute-start | bytes 811016 | tf_op jit(solution)/shard_map/ppermute | solution.py:263
  19.6 7.4 %collective-permute-done.1.refs_2_.far_ref = bf16[1056,128]{1,0:T(8,128)(2,1)S(1)} collective-permute-done((bf16[1056,128]{1,0:T(8,128)(2,1)}, bf16[1056,128]{1,0:T(8,128)(2,1)S(1)}, u32[]{:S(2)}, u32[]{:S(2)}) %collective-permute-start.1) | collective-permute-done | bytes 270368 | tf_op jit(solution)/shard_map/ppermute | solution.py:261
  27.0 2.9 %collective-permute-start.2 = (bf16[1056,128]{1,0:T(8,128)(2,1)S(1)}, bf16[1056,128]{1,0:T(8,128)(2,1)S(1)}, u32[]{:S(2)}, u32[]{:S(2)}) collective-permute-start(bf16[1056,128]{1,0:T(8,128)(2,1)S(1)} %collective-permute-done.1.refs_2_.far_ref), channel_id=1, source_target_pairs={{0,1},{1,0},{2,3},{3,2},{4,5},{5,4},{6,7},{7,6},{8,9},{9,8},{10,11... | collective-permute-start | bytes 811016 | tf_op jit(solution)/shard_map/ppermute | solution.py:263
  29.9 0.0 collective-permute-done.refs_1_.near_ref
  29.9 1.1 %collective-permute-done.2.refs_3_.last_ref = bf16[1056,128]{1,0:T(8,128)(2,1)S(1)} collective-permute-done((bf16[1056,128]{1,0:T(8,128)(2,1)S(1)}, bf16[1056,128]{1,0:T(8,128)(2,1)S(1)}, u32[]{:S(2)}, u32[]{:S(2)}) %collective-permute-start.2) | collective-permute-done | bytes 270368 | tf_op jit(solution)/shard_map/ppermute | solution.py:263
  31.0 0.0 copy-done
  31.0 0.4 shard_map.78
  31.4 0.0 all-to-all-done
  31.4 4.1 %shard_map.79 = (f32[9,2,128,128]{3,2,1,0:T(8,128)S(1)}, f32[1024,128]{1,0:T(8,128)S(1)}, bf16[1024,128]{1,0:T(8,128)(2,1)S(1)}) custom-call(bf16[2048,128]{1,0:T(8,128)(2,1)S(1)} %bitcast.9, bf16[1056,128]{1,0:T(8,128)(2,1)S(1)} %copy-done, bf16[1056,128]{1,0:T(8,128)(2,1)S(1)} %collective-permute-done.refs_1_.near_ref, ...), custom_call_target="tpu_custom_call" | custom-call | tf_op jit(solution)/shard_map/pallas_call | solution.py:269
  35.5 0.8 %shard_map.82 = bf16[2048,128]{1,0:T(8,128)(2,1)} custom-call(f32[9,2,128,128]{3,2,1,0:T(8,128)S(1)} %get-tuple-element.21.acc), custom_call_target="tpu_custom_call" | custom-call | tf_op jit(solution)/shard_map/pallas_call | solution.py:283
  36.4 7.8 %all-to-all-start.1 = ((bf16[64,32,128]{2,1,0:T(8,128)(2,1)}), bf16[64,32,128]{2,1,0:T(8,128)(2,1)S(1)}, u32[]{:S(2)}, u32[]{:S(2)}) async-start(bf16[64,32,128]{2,1,0:T(8,128)(2,1)} %bitcast.5), calls=%async_computation.1 | async-start | bytes 1048576 | tf_op jit(solution)/shard_map/all_to_all | solution.py:241
  44.2 3.3 %collective-permute-start.3 = (bf16[1024,128]{1,0:T(8,128)(2,1)S(1)}, bf16[1024,128]{1,0:T(8,128)(2,1)S(1)}, u32[]{:S(2)}, u32[]{:S(2)}) collective-permute-start(bf16[1024,128]{1,0:T(8,128)(2,1)S(1)} %get-tuple-element.18), channel_id=1, source_target_pairs={{0,4},{4,0},{1,5},{5,1},{2,6},{6,2},{3,7},{7,3},{8,12},{12,8},{9,1... | collective-permute-start | bytes 786440 | tf_op jit(solution)/shard_map/ppermute | solution.py:282
  47.4 9.8 %collective-permute-done.3.got_ref = bf16[1024,128]{1,0:T(8,128)(2,1)S(1)} collective-permute-done((bf16[1024,128]{1,0:T(8,128)(2,1)S(1)}, bf16[1024,128]{1,0:T(8,128)(2,1)S(1)}, u32[]{:S(2)}, u32[]{:S(2)}) %collective-permute-start.3) | collective-permute-done | bytes 262176 | tf_op jit(solution)/shard_map/ppermute | solution.py:282
  57.3 2.9 %collective-permute-start.4 = (f32[512,128]{1,0:T(8,128)S(1)}, f32[512,128]{1,0:T(8,128)S(1)}, u32[]{:S(2)}, u32[]{:S(2)}) collective-permute-start(f32[512,128]{1,0:T(8,128)S(1)} %get-tuple-element.20), channel_id=1, source_target_pairs={{0,1},{1,0},{2,3},{3,2},{4,5},{5,4},{6,7},{7,6},{8,9},{9,8},{10,11... | collective-permute-start | bytes 786440 | tf_op jit(solution)/shard_map/ppermute | solution.py:290
  60.2 1.1 %collective-permute-done.4.got_ref = f32[512,128]{1,0:T(8,128)S(1)} collective-permute-done((f32[512,128]{1,0:T(8,128)S(1)}, f32[512,128]{1,0:T(8,128)S(1)}, u32[]{:S(2)}, u32[]{:S(2)}) %collective-permute-start.4) | collective-permute-done | bytes 262176 | tf_op jit(solution)/shard_map/ppermute | solution.py:290
  61.3 0.7 %shard_map.81 = bf16[512,128]{1,0:T(8,128)(2,1)} custom-call(f32[512,128]{1,0:T(8,128)S(1)} %get-tuple-element.19.own_ref, f32[512,128]{1,0:T(8,128)S(1)} %collective-permute-done.4.got_ref), custom_call_target="tpu_custom_call" | custom-call | tf_op jit(solution)/shard_map/pallas_call | solution.py:290
  62.0 0.0 all-to-all-done.1
  62.0 0.7 %shard_map.83 = f32[2,16,512]{2,1,0:T(8,128)} custom-call(bf16[2048,128]{1,0:T(8,128)(2,1)S(1)} %bitcast.8), custom_call_target="tpu_custom_call" | custom-call | tf_op jit(solution)/shard_map/pallas_call | solution.py:291
  (1 shorter events, 0.0 us)
Async XLA Ops:
  2.6 28.4 %copy-start = (bf16[1056,128]{1,0:T(8,128)(2,1)S(1)}, bf16[1056,128]{1,0:T(8,128)(2,1)}, u32[]{:S(2)}) copy-start(bf16[1056,128]{1,0:T(8,128)(2,1)} %get-tuple-element.13.refs_0_.own_ref) | copy-start | bytes 811012
  2.6 28.7 %all-to-all-start = ((bf16[64,32,128]{2,1,0:T(8,128)(2,1)}), bf16[64,32,128]{2,1,0:T(8,128)(2,1)S(1)}, u32[]{:S(2)}, u32[]{:S(2)}) async-start(bf16[64,32,128]{2,1,0:T(8,128)(2,1)} %bitcast.10), calls=%async_computation | async-start | bytes 1048576 | tf_op jit(solution)/shard_map/all_to_all | solution.py:241
  13.7 13.3 %collective-permute-start.1 = (bf16[1056,128]{1,0:T(8,128)(2,1)}, bf16[1056,128]{1,0:T(8,128)(2,1)S(1)}, u32[]{:S(2)}, u32[]{:S(2)}) collective-permute-start(bf16[1056,128]{1,0:T(8,128)(2,1)} %get-tuple-element.13.refs_0_.own_ref), channel_id=1, source_target_pairs={{0,4},{4,0},{1,5},{5,1},{2,6},{6,2},{3,7},{7,3},{8,12},{12,8},{9,1... | collective-permute-start | bytes 811016 | tf_op jit(solution)/shard_map/ppermute | solution.py:261
  17.0 12.9 %collective-permute-start = (bf16[1056,128]{1,0:T(8,128)(2,1)}, bf16[1056,128]{1,0:T(8,128)(2,1)S(1)}, u32[]{:S(2)}, u32[]{:S(2)}) collective-permute-start(bf16[1056,128]{1,0:T(8,128)(2,1)} %get-tuple-element.13.refs_0_.own_ref), channel_id=1, source_target_pairs={{0,1},{1,0},{2,3},{3,2},{4,5},{5,4},{6,7},{7,6},{8,9},{9,8},{10,11... | collective-permute-start | bytes 811016 | tf_op jit(solution)/shard_map/ppermute | solution.py:263
  27.0 4.0 %collective-permute-start.2 = (bf16[1056,128]{1,0:T(8,128)(2,1)S(1)}, bf16[1056,128]{1,0:T(8,128)(2,1)S(1)}, u32[]{:S(2)}, u32[]{:S(2)}) collective-permute-start(bf16[1056,128]{1,0:T(8,128)(2,1)S(1)} %collective-permute-done.1.refs_2_.far_ref), channel_id=1, source_target_pairs={{0,1},{1,0},{2,3},{3,2},{4,5},{5,4},{6,7},{7,6},{8,9},{9,8},{10,11... | collective-permute-start | bytes 811016 | tf_op jit(solution)/shard_map/ppermute | solution.py:263
  36.4 25.7 %all-to-all-start.1 = ((bf16[64,32,128]{2,1,0:T(8,128)(2,1)}), bf16[64,32,128]{2,1,0:T(8,128)(2,1)S(1)}, u32[]{:S(2)}, u32[]{:S(2)}) async-start(bf16[64,32,128]{2,1,0:T(8,128)(2,1)} %bitcast.5), calls=%async_computation.1 | async-start | bytes 1048576 | tf_op jit(solution)/shard_map/all_to_all | solution.py:241
  44.2 13.1 %collective-permute-start.3 = (bf16[1024,128]{1,0:T(8,128)(2,1)S(1)}, bf16[1024,128]{1,0:T(8,128)(2,1)S(1)}, u32[]{:S(2)}, u32[]{:S(2)}) collective-permute-start(bf16[1024,128]{1,0:T(8,128)(2,1)S(1)} %get-tuple-element.18), channel_id=1, source_target_pairs={{0,4},{4,0},{1,5},{5,1},{2,6},{6,2},{3,7},{7,3},{8,12},{12,8},{9,1... | collective-permute-start | bytes 786440 | tf_op jit(solution)/shard_map/ppermute | solution.py:282
  57.3 4.0 %collective-permute-start.4 = (f32[512,128]{1,0:T(8,128)S(1)}, f32[512,128]{1,0:T(8,128)S(1)}, u32[]{:S(2)}, u32[]{:S(2)}) collective-permute-start(f32[512,128]{1,0:T(8,128)S(1)} %get-tuple-element.20), channel_id=1, source_target_pairs={{0,1},{1,0},{2,3},{3,2},{4,5},{5,4},{6,7},{7,6},{8,9},{9,8},{10,11... | collective-permute-start | bytes 786440 | tf_op jit(solution)/shard_map/ppermute | solution.py:290
